TPU v7x, 32 devices: a whole 2x2x4 slice. The times are simulated.
32 devices in a mesh: clips: 2 (over y), space: 8 (over z, x), tm: 2 (over core).
Axes of the slice: x: 2, y: 2, z: 4, core: 2. Of those that a mesh axis runs over, the one named last changes fastest.
Arguments:
- tokens_in: bfloat16 [16, 8, 60, 1536], P(('clips', 'tm'), 'space'), parts along dimension 0, may hold values from -24 to 24
- mod_shift: float32 [3072], P('clips'), parts along dimension 0, may hold values from -3 to 3
- mod_scale: float32 [3072], P('clips'), parts along dimension 0, may hold values from -2 to 2
- mod_gate: float32 [3072], P('clips'), parts along dimension 0, may hold values from 0.5 to 1.5
- w_qkv: bfloat16 [1536, 2304], replicated, may hold values from -1 to 1, as said below
- q_gain: float32 [768], replicated, may hold values from 0.5 to 7, as said below
- k_gain: float32 [768], replicated, may hold values from 0.5 to 7, as said below
- w_out: bfloat16 [768, 1536], replicated, may hold values from -0.21875 to 0.21875
- windows: int32 [6, 2], replicated, may hold values from 1 to 3, as said below
- frame_lists: int32 [16, 6], P('clips'), parts along dimension 0, may hold values from 0 to 7, as said below
- frame_valid: int32 [16], P('clips'), parts along dimension 0, may hold values from 0 to 1, as said below
Outputs:
- mixed: bfloat16 [16, 8, 60, 1536], P(('clips', 'tm'), 'space'), parts along dimension 0
There are 2 independent parts, one for each index of `clips`. A program takes and returns all parts, laid end to end along the dimension named above; an argument that names none is the same for every part. Nothing has to cross between parts.
Inputs may be any that keep to these rules, and one draw needn't show every extreme that they name: `w_qkv`: query, key and value columns in that order. `q_gain`: positive gains. `k_gain`: positive gains. `windows`: each entry 1 or 3; some head has 3 and 3, another head 1 and 1. `frame_lists`: row f names 6 different frames; entry 0 is f and entry 1 is (f + 4) mod 8. `frame_valid`: 1 for every frame f with f // 4 even; the other frames may be 0 or 1.
All inputs are finite; a program needn't handle non-finite values.
Results may differ from a plain program's by a relative error of at most 0.008.
Values may be sent and summed in bfloat16 or wider, within the bound.
No kernel may reach another device: no remote copies, remote signals or barrier semaphores. Data moves between devices by JAX's collectives and lax.ppermute only.
A program may use at most 128 MiB of HBM per device.

v0:
```python
import jax
import jax.numpy as jnp
from jax import lax
from jax.sharding import PartitionSpec as P

HEAD_DIM = 128
HEADS = 6


def shifted(value, axis, by):
    peers = lax.axis_size(axis)
    pairs = [(i, i + by) for i in range(peers) if 0 <= i + by < peers]
    return lax.ppermute(value, axis, pairs)


def layer_mod(tokens, shift_vec, scale_vec):
    floated = tokens.astype(jnp.float32)
    average = jnp.mean(floated, axis=-1, keepdims=True)
    centered = floated - average
    variance = jnp.mean(centered * centered, axis=-1, keepdims=True)
    normed = centered * lax.rsqrt(variance + 1e-06)
    return (normed * (1.0 + scale_vec) + shift_vec).astype(jnp.bfloat16)


def rms_gain(columns, gains):
    scaled = columns * lax.rsqrt(jnp.mean(columns * columns, axis=-1, keepdims=True) + 1e-06)
    return (scaled * gains).astype(jnp.bfloat16)


def frame_table(frame_lists, frame_valid):
    frame_total = frame_lists.shape[0]
    listed = jnp.any(
        frame_lists[:, :, None] == jnp.arange(frame_total, dtype=jnp.int32)[None, None, :], axis=1
    )
    return listed & (frame_valid == 1)[None, :]


def head_table(windows, exists):
    offsets = jnp.arange(9, dtype=jnp.int32)
    row_step = jnp.abs(offsets // 3 - 1)
    col_step = jnp.abs(offsets % 3 - 1)
    reaches = (windows - 1) // 2
    return (
        exists[None, :]
        & (row_step[None, :] <= reaches[:, 0:1])
        & (col_step[None, :] <= reaches[:, 1:2])
    )


def per_device(
    tokens_in,
    mod_shift,
    mod_scale,
    mod_gate,
    w_qkv,
    q_gain,
    k_gain,
    w_out,
    windows,
    frame_lists,
    frame_valid,
):
    frames, _, tile_tokens, feature_dim = tokens_in.shape
    inner_dim = w_out.shape[0]
    rows_here = frames * tile_tokens
    modulated = layer_mod(tokens_in, mod_shift, mod_scale).reshape(rows_here, feature_dim)
    projected = jnp.dot(modulated, w_qkv, preferred_element_type=jnp.float32)
    queries = rms_gain(projected[:, :inner_dim], q_gain)
    keys_here = rms_gain(projected[:, inner_dim : 2 * inner_dim], k_gain)
    values_here = projected[:, 2 * inner_dim :].astype(jnp.bfloat16)
    paired = jnp.stack([keys_here, values_here]).reshape(2, frames, tile_tokens, inner_dim)
    space_size = lax.axis_size("space")
    tile_cols = min(8, space_size // 2)
    tile_rows = space_size // tile_cols
    position = lax.axis_index("space")
    tile_row = position // tile_cols
    tile_col = position % tile_cols
    offsets = jnp.arange(9, dtype=jnp.int32)
    row_step = offsets // 3 - 1
    col_step = offsets % 3 - 1
    exists = (
        (tile_row + row_step >= 0)
        & (tile_row + row_step < tile_rows)
        & (tile_col + col_step >= 0)
        & (tile_col + col_step < tile_cols)
    )
    head_allow = head_table(windows, exists)
    pieces = []
    for tile_spot in range(9):
        offset = (tile_spot // 3 - 1) * tile_cols + tile_spot % 3 - 1
        if offset == 0:
            pieces.append(paired)
        else:
            pieces.append(shifted(paired, "space", -offset))
    gathered = jnp.stack(pieces, axis=2)
    frame_ok = frame_table(frame_lists, frame_valid)
    frame_block = lax.axis_index("tm")
    score_scale = HEAD_DIM ** (-0.5)
    initial = (
        jnp.full((HEADS, rows_here), -1e30, jnp.float32),
        jnp.zeros((HEADS, rows_here), jnp.float32),
        jnp.zeros((rows_here, inner_dim), jnp.float32),
    )
    portion = lax.all_gather(gathered, "tm", axis=1, tiled=True)
    frame_total = portion.shape[1]
    key_rows = frame_total * 9 * tile_tokens
    near_keys = portion[0].reshape(key_rows, inner_dim)
    near_values = portion[1].reshape(key_rows, inner_dim)
    frame_seen = lax.dynamic_slice(
        frame_ok, (frame_block * frames, jnp.int32(0)), (frames, frame_total)
    )

    def per_head(head_index, running_state):
        max_all, total_all, sum_all = running_state
        lower = head_index * HEAD_DIM
        query_head = lax.dynamic_slice_in_dim(queries, lower, HEAD_DIM, 1)
        key_head = lax.dynamic_slice_in_dim(near_keys, lower, HEAD_DIM, 1)
        value_head = lax.dynamic_slice_in_dim(near_values, lower, HEAD_DIM, 1)
        scores = (
            lax.dot_general(
                query_head, key_head, (((1,), (1,)), ((), ())), preferred_element_type=jnp.float32
            )
            * score_scale
        )
        tile_allow = lax.dynamic_index_in_dim(head_allow, head_index, 0, keepdims=False)
        allowed = jnp.broadcast_to(
            frame_seen[:, None, :, None, None] & tile_allow[None, None, None, :, None],
            (frames, tile_tokens, frame_total, 9, tile_tokens),
        ).reshape(rows_here, key_rows)
        max_old = lax.dynamic_index_in_dim(max_all, head_index, 0, keepdims=False)
        max_new = jnp.maximum(max_old, jnp.max(jnp.where(allowed, scores, -1e30), axis=1))
        weights = jnp.where(allowed, jnp.exp(scores - max_new[:, None]), 0.0)
        rescale = jnp.exp(max_old - max_new)
        total_old = lax.dynamic_index_in_dim(total_all, head_index, 0, keepdims=False)
        total_new = total_old * rescale + jnp.sum(weights, axis=1)
        sum_head = lax.dynamic_slice_in_dim(sum_all, lower, HEAD_DIM, 1)
        sum_head = sum_head * rescale[:, None] + jnp.dot(
            weights.astype(jnp.bfloat16), value_head, preferred_element_type=jnp.float32
        )
        max_all = lax.dynamic_update_index_in_dim(max_all, max_new, head_index, 0)
        total_all = lax.dynamic_update_index_in_dim(total_all, total_new, head_index, 0)
        sum_all = lax.dynamic_update_slice_in_dim(sum_all, sum_head, lower, 1)
        return (max_all, total_all, sum_all)

    row_max, totals, summed = lax.fori_loop(0, HEADS, per_head, initial)
    attended = (
        (summed.reshape(rows_here, HEADS, HEAD_DIM) / totals.T[:, :, None])
        .reshape(rows_here, inner_dim)
        .astype(jnp.bfloat16)
    )
    branch = jnp.dot(attended, w_out, preferred_element_type=jnp.float32)
    mixed = tokens_in.reshape(rows_here, feature_dim).astype(jnp.float32) + mod_gate * branch
    return mixed.astype(jnp.bfloat16).reshape(frames, 1, tile_tokens, feature_dim)


def solution(mesh):
    in_specs = (
        P(("clips", "tm"), "space", None, None),
        P("clips"),
        P("clips"),
        P("clips"),
        P(),
        P(),
        P(),
        P(),
        P(),
        P("clips", None),
        P("clips"),
    )
    out_specs = P(("clips", "tm"), "space", None, None)
    return jax.shard_map(
        per_device, mesh=mesh, in_specs=in_specs, out_specs=out_specs, check_vma=False
    )
```

profile of v0, /device:TPU:0, one launch (start us, length us, event | category | flops | bytes accessed | tf_op | source)
XLA Modules:
  0.0 360.6 jit_solution(10619549504101083522)
XLA Ops:
  6.5 1.6 convert_reduce_fusion
  8.2 1.7 multiply_reduce_fusion
  10.6 1.8 add_convert_fusion
  13.6 5.1 %fusion.30 = f32[240,2304]{1,0:T(8,128)S(1)} fusion(bf16[240,1536]{1,0:T(8,128)(2,1)} %reshape.157, bf16[1536,2304]{1,0:T(8,128)(2,1)} %param.17), kind=kOutput, calls=%fused_computation.75 | convolution fusion | flops 1698693120 | bytes 10027008 | tf_op jit(solution)/shard_map/dot_general | solution.py:67
  21.8 1.4 copy.63
  23.3 7.8 %collective-permute-start = (bf16[2,4,60,768]{3,1,2,0:T(4,128)(2,1)}, bf16[2,4,60,768]{3,1,2,0:T(4,128)(2,1)}, u32[]{:S(2)}, u32[]{:S(2)}) collective-permute-start(bf16[2,4,60,768]{3,1,2,0:T(4,128)(2,1)} %copy.63), channel_id=1, source_target_pairs={{0,10},{2,12},{4,14},{1,11},{3,13},{5,15},{16,26},{18,28},{20,30},... | collective-permute-start | bytes 2211848 | tf_op jit(solution)/shard_map/ppermute | solution.py:13
  31.0 2.2 collective-permute-start.1
  33.2 3.5 collective-permute-start.2
  36.7 3.0 collective-permute-start.3
  39.7 1.3 collective-permute-start.4
  41.9 11.8 %collective-permute-done = bf16[2,4,60,768]{3,1,2,0:T(4,128)(2,1)} collective-permute-done((bf16[2,4,60,768]{3,1,2,0:T(4,128)(2,1)}, bf16[2,4,60,768]{3,1,2,0:T(4,128)(2,1)}, u32[]{:S(2)}, u32[]{:S(2)}) %collective-permute-start) | collective-permute-done | bytes 737312 | tf_op jit(solution)/shard_map/ppermute | solution.py:13
  53.7 1.3 collective-permute-start.5
  55.0 2.1 bitcast_dynamic-update-slice_fusion.7
  57.1 12.4 %collective-permute-done.1 = bf16[2,4,60,768]{3,1,2,0:T(4,128)(2,1)} collective-permute-done((bf16[2,4,60,768]{3,1,2,0:T(4,128)(2,1)}, bf16[2,4,60,768]{3,1,2,0:T(4,128)(2,1)}, u32[]{:S(2)}, u32[]{:S(2)}) %collective-permute-start.1) | collective-permute-done | bytes 737312 | tf_op jit(solution)/shard_map/ppermute | solution.py:13
  70.8 2.1 bitcast_dynamic-update-slice_fusion.6
  72.9 21.8 %collective-permute-done.2 = bf16[2,4,60,768]{3,1,2,0:T(4,128)(2,1)} collective-permute-done((bf16[2,4,60,768]{3,1,2,0:T(4,128)(2,1)}, bf16[2,4,60,768]{3,1,2,0:T(4,128)(2,1)}, u32[]{:S(2)}, u32[]{:S(2)}) %collective-permute-start.2) | collective-permute-done | bytes 737312 | tf_op jit(solution)/shard_map/ppermute | solution.py:13
  94.7 1.5 collective-permute-start.7
  96.2 2.1 bitcast_dynamic-update-slice_fusion.5
  98.3 2.1 bitcast_dynamic-update-slice_fusion.4
  101.3 2.1 bitcast_dynamic-update-slice_fusion.3
  104.4 31.9 %collective-permute-done.6 = bf16[2,4,60,768]{3,1,2,0:T(4,128)(2,1)S(1)} collective-permute-done((bf16[2,4,60,768]{3,1,2,0:T(4,128)(2,1)}, bf16[2,4,60,768]{3,1,2,0:T(4,128)(2,1)S(1)}, u32[]{:S(2)}, u32[]{:S(2)}) %collective-permute-start.6) | collective-permute-done | bytes 737312 | tf_op jit(solution)/shard_map/ppermute | solution.py:13
  137.3 34.0 %collective-permute-done.7 = bf16[2,4,60,768]{3,1,2,0:T(4,128)(2,1)S(1)} collective-permute-done((bf16[2,4,60,768]{3,1,2,0:T(4,128)(2,1)}, bf16[2,4,60,768]{3,1,2,0:T(4,128)(2,1)S(1)}, u32[]{:S(2)}, u32[]{:S(2)}) %collective-permute-start.7) | collective-permute-done | bytes 737312 | tf_op jit(solution)/shard_map/ppermute | solution.py:13
  172.3 1.4 copy.60
  174.0 2.7 reshape.159
  176.9 19.2 %all-gather.2.cloned.1.call-done = bf16[2,8,9,60,768]{4,3,1,2,0:T(8,128)(2,1)} async-done(((bf16[2,4,9,60,768]{4,3,1,2,0:T(8,128)(2,1)}), bf16[2,8,9,60,768]{4,3,1,2,0:T(8,128)(2,1)}) %all-gather.2.cloned.1.call-update) | async-done | bytes 13271056 | tf_op jit(solution)/shard_map/all_gather | solution.py:104
  196.1 8.3 %fusion.29 = (bf16[1,8,9,60,768]{4,3,1,2,0:T(8,128)(2,1)}, bf16[1,8,9,60,768]{4,3,1,2,0:T(8,128)(2,1)S(1)}) fusion(bf16[2,8,9,60,768]{4,3,1,2,0:T(8,128)(2,1)} %all-gather.2.cloned.1.call-done), kind=kLoop, calls=%fused_computation.74 | loop fusion | bytes 26542080 | tf_op jit(solution)/shard_map/slice | solution.py:108
  204.3 3.4 copy.79
  207.7 9.9 %reshape_squeeze.6 = bf16[4320,768]{1,0:T(8,128)(2,1)} reshape(bf16[1,8,9,60,768]{4,3,2,1,0:T(8,128)(2,1)} %copy.79) | data formatting | bytes 13271040 | tf_op jit(solution)/shard_map/reshape;squeeze | solution.py:107
  217.6 6.8 %copy.80 = bf16[1,8,9,60,768]{4,3,2,1,0:T(8,128)(2,1)} copy(bf16[1,8,9,60,768]{4,3,1,2,0:T(8,128)(2,1)} %get-tuple-element.197) | data formatting | bytes 13271040 | tf_op jit(solution)/shard_map/slice | solution.py:108
  224.4 9.8 %reshape_squeeze.7 = bf16[4320,768]{1,0:T(8,128)(2,1)} reshape(bf16[1,8,9,60,768]{4,3,2,1,0:T(8,128)(2,1)} %copy.80) | data formatting | bytes 13271040 | tf_op jit(solution)/shard_map/reshape;squeeze | solution.py:108
  235.2 111.4 %while.17 = (s32[]{:T(128)}, f32[6,240]{1,0:T(8,128)S(1)}, f32[6,240]{1,0:T(8,128)S(1)}, f32[240,768]{1,0:T(8,128)}, pred[4,8]{0,1:T(8,128)(4,1)S(1)}, /*index=5...) while((s32[]{:T(128)}, f32[6,240]{1,0:T(8,128)S(1)}, ...), condition=%wide.region_8.9_spmd, body=%wide.region_5.8_spmd.sunk | while | flops 540235456 | bytes 27432980 | solution.py:145
  235.3 2.6 broadcast_in_dim.94
  237.8 6.2 %reshape.161 = pred[240,4320]{0,1:T(8,128)(4,1)S(1)} reshape(pred[4,60,8,9,60]{1,0,4,3,2:T(4,128)(4,1)} %broadcast_in_dim.94) | data formatting | bytes 2073600 | tf_op jit(solution)/shard_map/while/body/eval_jaxpr/reshape | solution.py:129
  244.0 2.7 copy.93
  246.7 2.7 select_reduce_fusion.2
  249.5 3.0 fusion.46
  253.8 2.6 broadcast_in_dim.94
  256.4 6.2 %reshape.161 = pred[240,4320]{0,1:T(8,128)(4,1)S(1)} reshape(pred[4,60,8,9,60]{1,0,4,3,2:T(4,128)(4,1)} %broadcast_in_dim.94) | data formatting | bytes 2073600 | tf_op jit(solution)/shard_map/while/body/eval_jaxpr/reshape | solution.py:129
  262.6 2.7 copy.93
  265.3 2.7 select_reduce_fusion.2
  268.0 3.0 fusion.46
  272.4 2.6 broadcast_in_dim.94
  275.0 6.2 %reshape.161 = pred[240,4320]{0,1:T(8,128)(4,1)S(1)} reshape(pred[4,60,8,9,60]{1,0,4,3,2:T(4,128)(4,1)} %broadcast_in_dim.94) | data formatting | bytes 2073600 | tf_op jit(solution)/shard_map/while/body/eval_jaxpr/reshape | solution.py:129
  281.2 2.7 copy.93
  283.9 2.7 select_reduce_fusion.2
  286.6 3.0 fusion.46
  291.0 2.6 broadcast_in_dim.94
  293.6 6.2 %reshape.161 = pred[240,4320]{0,1:T(8,128)(4,1)S(1)} reshape(pred[4,60,8,9,60]{1,0,4,3,2:T(4,128)(4,1)} %broadcast_in_dim.94) | data formatting | bytes 2073600 | tf_op jit(solution)/shard_map/while/body/eval_jaxpr/reshape | solution.py:129
  299.7 2.7 copy.93
  302.4 2.7 select_reduce_fusion.2
  305.2 3.0 fusion.46
  309.5 2.6 broadcast_in_dim.94
  312.1 6.2 %reshape.161 = pred[240,4320]{0,1:T(8,128)(4,1)S(1)} reshape(pred[4,60,8,9,60]{1,0,4,3,2:T(4,128)(4,1)} %broadcast_in_dim.94) | data formatting | bytes 2073600 | tf_op jit(solution)/shard_map/while/body/eval_jaxpr/reshape | solution.py:129
  318.3 2.7 copy.93
  321.0 2.7 select_reduce_fusion.2
  323.7 3.0 fusion.46
  328.1 2.6 broadcast_in_dim.94
  330.7 6.2 %reshape.161 = pred[240,4320]{0,1:T(8,128)(4,1)S(1)} reshape(pred[4,60,8,9,60]{1,0,4,3,2:T(4,128)(4,1)} %broadcast_in_dim.94) | data formatting | bytes 2073600 | tf_op jit(solution)/shard_map/while/body/eval_jaxpr/reshape | solution.py:129
  336.9 2.7 copy.93
  339.6 2.7 select_reduce_fusion.2
  342.3 3.0 fusion.46
  346.6 1.4 copy.82
  348.0 2.1 fusion.22
  351.2 2.6 copy.83
  (118 shorter events, 21.5 us)
Async XLA Ops:
  6.5 341.5 %copy-start = (bf16[768,1536]{1,0:T(8,128)(2,1)S(1)}, bf16[768,1536]{1,0:T(8,128)(2,1)}, u32[]{:S(2)}) copy-start(bf16[768,1536]{1,0:T(8,128)(2,1)} %param.20) | copy-start | bytes 7077892
  6.5 189.5 %all-gather.2.cloned.1.call-start = ((), (), s32[]{:S(2)}) async-start(), calls=%async_computation | async-start | bytes 21233664 | tf_op jit(solution)/shard_map/all_gather | solution.py:104
  13.5 5.4 %copy-start.5 = (f32[768]{0:T(1024)S(1)}, f32[768]{0:T(1024)}, u32[]{:S(2)}) copy-start(f32[768]{0:T(1024)} %param.19) | copy-start | bytes 9220
  13.6 5.4 %copy-start.6 = (f32[768]{0:T(1024)S(1)}, f32[768]{0:T(1024)}, u32[]{:S(2)}) copy-start(f32[768]{0:T(1024)} %param.18) | copy-start | bytes 9220
  23.3 30.5 %collective-permute-start = (bf16[2,4,60,768]{3,1,2,0:T(4,128)(2,1)}, bf16[2,4,60,768]{3,1,2,0:T(4,128)(2,1)}, u32[]{:S(2)}, u32[]{:S(2)}) collective-permute-start(bf16[2,4,60,768]{3,1,2,0:T(4,128)(2,1)} %copy.63), channel_id=1, source_target_pairs={{0,10},{2,12},{4,14},{1,11},{3,13},{5,15},{16,26},{18,28},{20,30},... | collective-permute-start | bytes 2211848 | tf_op jit(solution)/shard_map/ppermute | solution.py:13
  31.0 38.5 %collective-permute-start.1 = (bf16[2,4,60,768]{3,1,2,0:T(4,128)(2,1)}, bf16[2,4,60,768]{3,1,2,0:T(4,128)(2,1)}, u32[]{:S(2)}, u32[]{:S(2)}) collective-permute-start(bf16[2,4,60,768]{3,1,2,0:T(4,128)(2,1)} %copy.63), channel_id=1, source_target_pairs={{0,8},{2,10},{4,12},{6,14},{1,9},{3,11},{5,13},{7,15},{16,24},{18,... | collective-permute-start | bytes 2211848 | tf_op jit(solution)/shard_map/ppermute | solution.py:13
  33.2 61.5 %collective-permute-start.2 = (bf16[2,4,60,768]{3,1,2,0:T(4,128)(2,1)}, bf16[2,4,60,768]{3,1,2,0:T(4,128)(2,1)}, u32[]{:S(2)}, u32[]{:S(2)}) collective-permute-start(bf16[2,4,60,768]{3,1,2,0:T(4,128)(2,1)} %copy.63), channel_id=1, source_target_pairs={{0,6},{2,8},{4,10},{6,12},{8,14},{1,7},{3,9},{5,11},{7,13},{9,15},... | collective-permute-start | bytes 2211848 | tf_op jit(solution)/shard_map/ppermute | solution.py:13
  36.7 61.6 %collective-permute-start.3 = (bf16[2,4,60,768]{3,1,2,0:T(4,128)(2,1)}, bf16[2,4,60,768]{3,1,2,0:T(4,128)(2,1)}, u32[]{:S(2)}, u32[]{:S(2)}) collective-permute-start(bf16[2,4,60,768]{3,1,2,0:T(4,128)(2,1)} %copy.63), channel_id=1, source_target_pairs={{0,2},{2,4},{4,6},{6,8},{8,10},{10,12},{12,14},{1,3},{3,5},{5,7},{... | collective-permute-start | bytes 2211848 | tf_op jit(solution)/shard_map/ppermute | solution.py:13
  39.7 61.6 %collective-permute-start.4 = (bf16[2,4,60,768]{3,1,2,0:T(4,128)(2,1)}, bf16[2,4,60,768]{3,1,2,0:T(4,128)(2,1)}, u32[]{:S(2)}, u32[]{:S(2)}) collective-permute-start(bf16[2,4,60,768]{3,1,2,0:T(4,128)(2,1)} %copy.63), channel_id=1, source_target_pairs={{2,0},{4,2},{6,4},{8,6},{10,8},{12,10},{14,12},{3,1},{5,3},{7,5},{... | collective-permute-start | bytes 2211848 | tf_op jit(solution)/shard_map/ppermute | solution.py:13
  41.9 58.5 %copy-start.3 = (bf16[1,4,1,60,768]{4,3,1,2,0:T(8,128)(2,1)S(1)}, bf16[1,4,1,60,768]{4,3,1,2,0:T(8,128)(2,1)}, u32[]{:S(2)}) copy-start(bf16[1,4,1,60,768]{4,3,1,2,0:T(8,128)(2,1)} %stack.50) | copy-start | bytes 1105924
  53.7 49.7 %collective-permute-start.5 = (bf16[2,4,60,768]{3,1,2,0:T(4,128)(2,1)}, bf16[2,4,60,768]{3,1,2,0:T(4,128)(2,1)S(1)}, u32[]{:S(2)}, u32[]{:S(2)}) collective-permute-start(bf16[2,4,60,768]{3,1,2,0:T(4,128)(2,1)} %copy.63), channel_id=1, source_target_pairs={{6,0},{8,2},{10,4},{12,6},{14,8},{7,1},{9,3},{11,5},{13,7},{15,9},... | collective-permute-start | bytes 2211848 | tf_op jit(solution)/shard_map/ppermute | solution.py:13
  69.5 66.8 %collective-permute-start.6 = (bf16[2,4,60,768]{3,1,2,0:T(4,128)(2,1)}, bf16[2,4,60,768]{3,1,2,0:T(4,128)(2,1)S(1)}, u32[]{:S(2)}, u32[]{:S(2)}) collective-permute-start(bf16[2,4,60,768]{3,1,2,0:T(4,128)(2,1)} %copy.63), channel_id=1, source_target_pairs={{8,0},{10,2},{12,4},{14,6},{9,1},{11,3},{13,5},{15,7},{24,16},{26,... | collective-permute-start | bytes 2211848 | tf_op jit(solution)/shard_map/ppermute | solution.py:13
  94.7 76.6 %collective-permute-start.7 = (bf16[2,4,60,768]{3,1,2,0:T(4,128)(2,1)}, bf16[2,4,60,768]{3,1,2,0:T(4,128)(2,1)S(1)}, u32[]{:S(2)}, u32[]{:S(2)}) collective-permute-start(bf16[2,4,60,768]{3,1,2,0:T(4,128)(2,1)} %copy.63), channel_id=1, source_target_pairs={{10,0},{12,2},{14,4},{11,1},{13,3},{15,5},{26,16},{28,18},{30,20},... | collective-permute-start | bytes 2211848 | tf_op jit(solution)/shard_map/ppermute | solution.py:13
  137.3 35.0 %copy-start.2 = (bf16[4,1,60,1536]{3,0,2,1:T(4,128)(2,1)S(1)}, bf16[4,1,60,1536]{3,0,2,1:T(4,128)(2,1)}, u32[]{:S(2)}) copy-start(bf16[4,1,60,1536]{3,0,2,1:T(4,128)(2,1)} %param.13) | copy-start | bytes 2211844
  172.3 1.5 copy-start.7
  172.3 1.6 copy-start.9
  172.3 4.5 %copy-start.8 = (s32[6,2]{0,1:T(2,128)S(1)}, s32[6,2]{0,1:T(2,128)}, u32[]{:S(2)}) copy-start(s32[6,2]{0,1:T(2,128)} %param.21) | copy-start | bytes 148
  235.2 112.9 %copy-start.4 = (f32[1536]{0:T(1024)S(1)}, f32[1536]{0:T(1024)}, u32[]{:S(2)}) copy-start(f32[1536]{0:T(1024)} %param.16) | copy-start | bytes 18436
  246.7 2.7 copy-start.1
  265.3 2.7 copy-start.1
  283.9 2.7 copy-start.1
  302.4 2.7 copy-start.1
  321.0 2.7 copy-start.1
  339.6 2.7 copy-start.1
Sparse Core Ops, SparseCore 0:
  172.4 23.6 all-gather.1
where the time goes:
time: 363 us; the launch traced here: 361 us
  local copies, waits for them, and re-layouts  136 us (37%)
  waiting for transfers between devices  131 us (36%)
  matrix products  41.5 us (11%)
  starting transfers between devices  21.8 us (6%)
  other arithmetic  16.6 us (5%)
  between operations  13.6 us (4%)
    ppermute x8, waiting for transfers between devices, shifted(): return lax.ppermute(value, axis, pairs)  112 us
    reshape x12, local copies, waits for them, and re-layouts, per_head(): allowed = jnp.broadcast_to(frame_seen[:, None, :, None, None] & tile_allo...  53.2 us
    ppermute x8, starting transfers between devices, shifted(): return lax.ppermute(value, axis, pairs)  21.8 us
    all_gather x1, waiting for transfers between devices, per_device(): portion = lax.all_gather(gathered, 'tm', axis=1, tiled=True)  19.2 us
    dot_general x6, matrix products, per_head(): jnp.dot(weights.astype(jnp.bfloat16), value_head, preferred_element_type=...  18.1 us
    dot_general x6, matrix products, per_head(): lax.dot_general(query_head, key_head, (((1,), (1,)), ((), ())), preferred...  16.2 us
    broadcast_in_dim x6, local copies, waits for them, and re-layouts, per_head(): jnp.broadcast_to(frame_seen[:, None, :, None, None] & tile_allow[None, No...  15.5 us
    slice x2, local copies, waits for them, and re-layouts, per_device(): near_values = portion[1].reshape(key_rows, inner_dim)  15.1 us
  transfers between devices with their start and end apart: 9, of which 6 were waited for; matrix products, arithmetic and copies ran while one was open for 5% of the time, Pallas kernels for 0%

commit v1 on v0

v1 whole, which is shorter than its diff:
```python
import functools

import jax
import jax.numpy as jnp
from jax import lax
from jax.experimental import pallas as pl
from jax.experimental.pallas import tpu as pltpu
from jax.sharding import PartitionSpec as P

HEAD_DIM = 128
NEG = -1e30
LOG2E = 1.4426950408889634
N_H, N_V, SLOT_H, SLOT_V, ORDER_H, ORDER_V = 0, 1, 8, 16, 24, 32
META = 40

VMEM = pl.BlockSpec(memory_space=pltpu.VMEM)
SMEM = pl.BlockSpec(memory_space=pltpu.SMEM)
ANY = pl.BlockSpec(memory_space=pl.ANY)


def rank_heads(windows, meta, heads):
    for column, count_at, slot_at, order_at in ((1, N_H, SLOT_H, ORDER_H), (0, N_V, SLOT_V, ORDER_V)):
        reach = [jnp.where(windows[h, column] >= 3, 1, 0) for h in range(heads)]
        total = sum(reach[1:], reach[0])
        meta[count_at] = total
        ahead, behind = jnp.int32(0), total
        for h in range(heads):
            slot = jnp.where(reach[h] == 1, ahead, behind)
            meta[slot_at + h] = slot
            meta[order_at + slot] = h
            ahead = ahead + reach[h]
            behind = behind + 1 - reach[h]


def project_kernel(
    heads, windows, tokens, shift, scale, w_qkv, q_gain, k_gain,
    meta, q_here, q_send, kv_here, kv_send, mod32, w_buf, sems,
):
    frames, _, tile_tokens, _ = tokens.shape
    inner = heads * HEAD_DIM
    half = inner // 2
    order = (2, 3, 4, 5, 0, 1)
    copies = {
        j: pltpu.make_async_copy(w_qkv.at[:, pl.ds(j * half, half)], w_buf.at[j], sems.at[j])
        for j in order
    }
    for j in order:
        copies[j].start()
    rank_heads(windows, meta, heads)
    gain_row = 1.0 + scale[...][None, :]
    shift_row = shift[...][None, :]
    for f in range(frames):
        floated = tokens[f, 0].astype(jnp.float32)
        average = jnp.mean(floated, axis=-1, keepdims=True)
        centered = floated - average
        variance = jnp.mean(centered * centered, axis=-1, keepdims=True)
        normed = centered * lax.rsqrt(variance + 1e-06)
        mod32[f * tile_tokens : (f + 1) * tile_tokens, :] = normed * gain_row + shift_row
    modulated = mod32[...].astype(jnp.bfloat16)

    def block(j):
        copies[j].wait()
        return jnp.dot(modulated, w_buf[j], preferred_element_type=jnp.float32)

    def normed_heads(first, second, gains):
        squares = jnp.sum(first * first, axis=-1, keepdims=True)
        squares = squares + jnp.sum(second * second, axis=-1, keepdims=True)
        factor = lax.rsqrt(squares * (1.0 / inner) + 1e-06)
        gains_row = gains[...][None, :]
        for h in range(heads):
            part, at = (first, h * HEAD_DIM) if h * HEAD_DIM < half else (second, h * HEAD_DIM - half)
            columns = part[:, at : at + HEAD_DIM] * factor
            yield h, (columns * gains_row[:, h * HEAD_DIM : (h + 1) * HEAD_DIM]).astype(jnp.bfloat16)

    for h, part in normed_heads(block(2), block(3), k_gain):
        kv_here[h, 0] = part
    first, second = block(4), block(5)
    for h in range(heads):
        part, at = (first, h * HEAD_DIM) if h * HEAD_DIM < half else (second, h * HEAD_DIM - half)
        kv_here[h, 1] = part[:, at : at + HEAD_DIM].astype(jnp.bfloat16)
    for i in range(kv_send.shape[0]):
        kv_send[i] = kv_here[meta[ORDER_H + i]]
    for h, part in normed_heads(block(0), block(1), q_gain):
        q_here[h] = part
    for i in range(q_send.shape[0]):
        q_send[i] = q_here[meta[ORDER_V + i]]


def attend_kernel(
    heads, lanes, meta, place, lists, valid, q_here, q_visit, kv_own, kv_own2, kv_left, kv_left2, kv_right, kv_right2,
    o_own, lse_own, o_visit, lse_visit, bias, q_all, stats,
):
    directions, slots, rows, _ = q_visit.shape
    frame_total, listed = lists.shape
    frames = frame_total // 2
    tile_tokens = rows // frames
    tile_keys = frame_total * tile_tokens
    here = place[0]
    has_left, has_right = place[1], place[2]

    key_at = lax.broadcasted_iota(jnp.int32, (1, 3 * tile_keys), 1)
    query_at = lax.broadcasted_iota(jnp.int32, (rows, 1), 0)
    group = jnp.zeros((1, 3 * tile_keys), jnp.int32)
    for j in range(1, 3 * frame_total):
        group = group + jnp.where(key_at >= j * tile_tokens, 1, 0)
    tile = jnp.where(group >= frame_total, 1, 0) + jnp.where(group >= 2 * frame_total, 1, 0)
    frame_slot = group - tile * frame_total
    absent = jnp.where((tile == 1) & (has_left == 0) | (tile == 2) & (has_right == 0), NEG, 0.0)
    full = jnp.zeros((rows, 3 * tile_keys), jnp.float32)
    for f in range(frames):
        row = jnp.full((1, 3 * tile_keys), NEG, jnp.float32)
        for s in range(frame_total):
            frame = (here * frames + s) % frame_total
            query_frame = here * frames + f
            seen = jnp.where(lists[query_frame, 0] == frame, 1, 0)
            for k in range(1, listed):
                seen = seen | jnp.where(lists[query_frame, k] == frame, 1, 0)
            seen = seen & jnp.where(valid[frame] == 1, 1, 0)
            row = jnp.where((frame_slot == s) & (seen == 1), 0.0, row)
        row = jnp.minimum(row, absent)
        inside = (query_at >= f * tile_tokens) & (query_at < (f + 1) * tile_tokens)
        full = jnp.where(inside, row, full)
    bias[...] = full
    stats[...] = jnp.zeros_like(stats)
    q_all[0:heads] = q_here[...]
    for d in range(directions):
        q_all[heads + d * slots : heads + (d + 1) * slots] = q_visit[d]

    lane = lax.broadcasted_iota(jnp.int32, (rows, lanes), 1)
    factor = HEAD_DIM**-0.5 * LOG2E

    def softmax_item(item, head, refs_slots, lane_at):
        keys = jnp.concatenate([ref[slot, 0] for ref, slot in refs_slots], axis=0)
        values = jnp.concatenate([ref[slot, 1] for ref, slot in refs_slots], axis=0)
        scores = lax.dot_general(
            q_all[item], keys, (((1,), (1,)), ((), ())), preferred_element_type=jnp.float32
        )
        scores = scores + bias[:, : keys.shape[0]]
        peak = jnp.max(scores, axis=1, keepdims=True)
        weights = jnp.exp2((scores - peak) * factor)
        total = jnp.sum(weights, axis=1, keepdims=True)
        summed = jnp.dot(weights.astype(jnp.bfloat16), values, preferred_element_type=jnp.float32)
        stats[0:rows] = jnp.where(lane == lane_at, peak * factor + jnp.log2(total), stats[0:rows])
        return summed / total

    def any_item(item, head, lane_at, store):
        slot = meta[SLOT_H + head]
        wide = slot < meta[N_H]

        @pl.when(wide)
        def _():
            store(softmax_item(
                item, head,
                [(kv_own, head), (kv_own2, head), (kv_left, slot), (kv_left2, slot), (kv_right, slot), (kv_right2, slot)],
                lane_at,
            ))

        @pl.when(jnp.logical_not(wide))
        def _():
            store(softmax_item(item, head, [(kv_own, head), (kv_own2, head)], lane_at))

    @pl.loop(0, heads)
    def _(h):
        def store(out):
            o_own[h] = out

        any_item(h, h, h, store)

    for d in range(directions):
        @pl.loop(0, meta[N_V])
        def _(i, d=d):
            def store(out):
                o_visit[d, i] = out.astype(o_visit.dtype)

            any_item(heads + d * slots + i, meta[ORDER_V + i], 16 + d * 8 + i, store)

    lse_own[...] = stats[...]
    turned = jnp.transpose(stats[...])
    for d in range(directions):
        lse_visit[d] = turned[16 + d * 8 : 24 + d * 8]


def output_kernel(
    heads, meta, place, tokens, gate, w_out, o_own, lse_own, o_back, lse_back,
    out, attended, wide, back,
):
    directions, slots, rows, _ = o_back.shape
    frames, _, tile_tokens, _ = tokens.shape
    back[...] = jnp.zeros_like(back)
    for d in range(directions):
        back[d * 8 : (d + 1) * 8] = lse_back[d]
    turned = jnp.transpose(back[...])[:rows]
    lane = lax.broadcasted_iota(jnp.int32, turned.shape, 1)
    for h in range(heads):
        slot = meta[SLOT_V + h]
        reaches = slot < meta[N_V]
        at = jnp.minimum(slot, slots - 1)
        parts = [(lse_own[0:rows, h : h + 1], o_own[h])]
        for d in range(directions):
            there = jnp.sum(jnp.where(lane == d * 8 + at, turned, 0.0), axis=1, keepdims=True)
            use = jnp.logical_and(reaches, place[3 + d] == 1)
            there = jnp.where(use, there, NEG)
            parts.append((there, jnp.where(use, o_back[d, at].astype(jnp.float32), 0.0)))
        peak = parts[0][0]
        for lse, _ in parts[1:]:
            peak = jnp.maximum(peak, lse)
        weights = [jnp.exp2(lse - peak) for lse, _ in parts]
        total = sum(weights[1:], weights[0])
        mixed = sum((w * o for w, (_, o) in zip(weights[1:], parts[1:])), weights[0] * parts[0][1])
        attended[:, h * HEAD_DIM : (h + 1) * HEAD_DIM] = (mixed / total).astype(jnp.bfloat16)
    branch = jnp.dot(attended[...], w_out[...], preferred_element_type=jnp.float32)
    wide[...] = branch * gate[...][None, :]
    for f in range(frames):
        mixed = tokens[f, 0].astype(jnp.float32) + wide[f * tile_tokens : (f + 1) * tile_tokens, :]
        out[f, 0] = mixed.astype(jnp.bfloat16)


def per_device(
    tokens_in, mod_shift, mod_scale, mod_gate, w_qkv, q_gain, k_gain, w_out, windows, frame_lists, frame_valid
):
    frames, _, tile_tokens, feature_dim = tokens_in.shape
    inner = w_out.shape[0]
    heads = windows.shape[0]
    rows = frames * tile_tokens
    slots = heads - 1
    space_size = lax.axis_size("space")
    assert lax.axis_size("tm") == 2
    tile_cols = min(8, space_size // 2)
    tile_rows = space_size // tile_cols
    bf16, f32 = jnp.bfloat16, jnp.float32

    spots = range(space_size)
    to_right = [(i, i + 1) for i in spots if i % tile_cols != tile_cols - 1]
    to_left = [(j, i) for i, j in to_right]
    down = [(i, i + tile_cols) for i in spots if i + tile_cols < space_size]
    up = [(j, i) for i, j in down]
    vertical = [down + up] if tile_rows == 2 else [down, up]
    directions = len(vertical)
    swap = [(0, 1), (1, 0)]

    position = lax.axis_index("space")
    tile_row = position // tile_cols
    tile_col = position % tile_cols
    has_partner = (
        [position >= 0] if tile_rows == 2 else [tile_row < tile_rows - 1, tile_row > 0]
    )
    place = jnp.stack(
        [lax.axis_index("tm"), tile_col > 0, tile_col < tile_cols - 1, *has_partner]
    ).astype(jnp.int32)

    meta, q_here, q_send, kv_here, kv_send = pl.pallas_call(
        functools.partial(project_kernel, heads),
        in_specs=[SMEM, VMEM, VMEM, VMEM, ANY, VMEM, VMEM],
        out_specs=[SMEM, VMEM, VMEM, VMEM, VMEM],
        out_shape=[
            jax.ShapeDtypeStruct((META,), jnp.int32),
            jax.ShapeDtypeStruct((heads, rows, HEAD_DIM), bf16),
            jax.ShapeDtypeStruct((slots, rows, HEAD_DIM), bf16),
            jax.ShapeDtypeStruct((heads, 2, rows, HEAD_DIM), bf16),
            jax.ShapeDtypeStruct((slots, 2, rows, HEAD_DIM), bf16),
        ],
        scratch_shapes=[
            pltpu.VMEM((rows, feature_dim), f32),
            pltpu.VMEM((6, feature_dim, inner // 2), bf16),
            pltpu.SemaphoreType.DMA((6,)),
        ],
        name="project",
    )(windows, tokens_in, mod_shift, mod_scale, w_qkv, q_gain, k_gain)

    kv_left = lax.ppermute(kv_send, "space", to_right)
    kv_right = lax.ppermute(kv_send, "space", to_left)
    q_visit = jnp.stack([lax.ppermute(q_send, "space", pairs) for pairs in vertical])
    kv_other = lax.ppermute(kv_here, "tm", swap)
    kv_left2 = lax.ppermute(kv_left, "tm", swap)
    kv_right2 = lax.ppermute(kv_right, "tm", swap)

    lanes = 128
    stat_rows = 256
    o_own, lse_own, o_visit, lse_visit = pl.pallas_call(
        functools.partial(attend_kernel, heads, lanes),
        in_specs=[SMEM] * 4 + [VMEM] * 8,
        out_specs=[VMEM] * 4,
        out_shape=[
            jax.ShapeDtypeStruct((heads, rows, HEAD_DIM), f32),
            jax.ShapeDtypeStruct((stat_rows, lanes), f32),
            jax.ShapeDtypeStruct((directions, slots, rows, HEAD_DIM), bf16),
            jax.ShapeDtypeStruct((directions, 8, stat_rows), f32),
        ],
        scratch_shapes=[
            pltpu.VMEM((rows, 3 * 2 * rows), f32),
            pltpu.VMEM((heads + directions * slots, rows, HEAD_DIM), bf16),
            pltpu.VMEM((stat_rows, lanes), f32),
        ],
        name="attend",
    )(meta, place, frame_lists, frame_valid, q_here, q_visit,
      kv_here, kv_other, kv_left, kv_left2, kv_right, kv_right2)

    back = [[(j, i) for i, j in pairs] for pairs in vertical]
    o_back = jnp.stack([lax.ppermute(o_visit[d], "space", back[d]) for d in range(directions)])
    lse_back = jnp.stack([lax.ppermute(lse_visit[d], "space", back[d]) for d in range(directions)])

    return pl.pallas_call(
        functools.partial(output_kernel, heads),
        in_specs=[SMEM, SMEM] + [VMEM] * 7,
        out_specs=VMEM,
        out_shape=jax.ShapeDtypeStruct(tokens_in.shape, bf16),
        scratch_shapes=[
            pltpu.VMEM((rows, inner), bf16),
            pltpu.VMEM((rows, feature_dim), f32),
            pltpu.VMEM((lanes, stat_rows), f32),
        ],
        name="output",
    )(meta, place, tokens_in, mod_gate, w_out, o_own, lse_own, o_back, lse_back)


def solution(mesh):
    in_specs = (
        P(("clips", "tm"), "space", None, None),
        P("clips"),
        P("clips"),
        P("clips"),
        P(),
        P(),
        P(),
        P(),
        P(),
        P("clips", None),
        P("clips"),
    )
    out_specs = P(("clips", "tm"), "space", None, None)
    return jax.shard_map(
        per_device, mesh=mesh, in_specs=in_specs, out_specs=out_specs, check_vma=False
    )
```

time: 363 us -> 96.6 us (0.27)
  local copies, waits for them, and re-layouts: 136 us -> 8.11 us
  waiting for transfers between devices: 131 us -> 53.5 us
  matrix products: 41.5 us -> 0 us
  Pallas kernels: 0 us -> 22 us
  other arithmetic: 16.6 us -> 0.65 us
  between operations: 13.6 us -> 0.09 us
  starting transfers between devices: 21.8 us -> 12.4 us
    ppermute x8, waiting for transfers between devices: 112 us -> 53.5 us  [the longest x1 14.1 us: per_device(): lax.ppermute(q_send, 'space', pairs)]
    reshape x15 -> x0, local copies, waits for them, and re-layouts: 57.8 us -> none  [the longest x12 53.2 us: per_head(): allowed = jnp.broadcast_to(frame_seen[:, None, :, None, None] & tile_allo...]
    dot_general x14 -> x0, matrix products: 41.5 us -> none  [the longest x6 18.1 us: per_head(): jnp.dot(weights.astype(jnp.bfloat16), value_head, preferred_element_type=...]
    another operation x8 -> x0, local copies, waits for them, and re-layouts: 23.9 us -> none  [the longest x1 9.88 us: per_device(): near_keys = portion[0].reshape(key_rows, inner_dim)]
    pallas_call x0 -> x3, Pallas kernels: none -> 22 us  [the longest x1 9.63 us: per_device(): pl.pallas_call(functools.partial(attend_kernel, heads, lanes), in_specs=[...]
    all_gather x1 -> x0, waiting for transfers between devices: 19.2 us -> none  [per_device(): portion = lax.all_gather(gathered, 'tm', axis=1, tiled=True)]
    slice x4 -> x0, local copies, waits for them, and re-layouts: 18.5 us -> none  [the longest x2 15.1 us: per_device(): near_values = portion[1].reshape(key_rows, inner_dim)]
    broadcast_in_dim x9 -> x0, local copies, waits for them, and re-layouts: 16.4 us -> none  [the longest x6 15.5 us: per_head(): jnp.broadcast_to(frame_seen[:, None, :, None, None] & tile_allow[None, No...]
  transfers between devices with their start and end apart: 9 -> 8, of which waited for: 6 -> 4; matrix products, arithmetic and copies ran while one was open for 5% -> 1% of each run, Pallas kernels for 0% -> 0%
where the time goes in v1:
time: 96.6 us; the launch traced here: 96.8 us
  waiting for transfers between devices  53.5 us (55%)
  Pallas kernels  22 us (23%)
  starting transfers between devices  12.4 us (13%)
  local copies, waits for them, and re-layouts  8.11 us (8%)
    ppermute x1, waiting for transfers between devices, per_device(): lax.ppermute(q_send, 'space', pairs)  14.1 us
    ppermute x1, waiting for transfers between devices, per_device(): lax.ppermute(lse_visit[d], 'space', back[d])  13.9 us
    ppermute x1, waiting for transfers between devices, per_device(): kv_left = lax.ppermute(kv_send, 'space', to_right)  13.4 us
    ppermute x1, waiting for transfers between devices, per_device(): kv_right = lax.ppermute(kv_send, 'space', to_left)  12 us
    pallas_call x1, Pallas kernels, per_device(): pl.pallas_call(functools.partial(attend_kernel, heads, lanes), in_specs=[...  9.63 us
    pallas_call x1, Pallas kernels, per_device(): pl.pallas_call(functools.partial(project_kernel, heads), in_specs=[SMEM,...  7.17 us
    unnamed x18, local copies, waits for them, and re-layouts  5.55 us
    ppermute x1, starting transfers between devices, per_device(): kv_left = lax.ppermute(kv_send, 'space', to_right)  5.53 us
  transfers between devices with their start and end apart: 8, of which 4 were waited for; matrix products, arithmetic and copies ran while one was open for 1% of the time, Pallas kernels for 0%

profile of v1, /device:TPU:0, one launch (start us, length us, event | category | flops | bytes accessed | tf_op | source)
XLA Modules:
  0.0 96.8 jit_solution(11459477312245658061)
XLA Ops:
  0.0 1.3 %copy.12.windows = s32[6,2]{1,0:T(8,128)} copy(s32[6,2]{0,1:T(2,128)} %param.19) | data formatting | bytes 96 | tf_op args[8]
  1.4 2.1 %copy.13.tokens = bf16[4,1,60,1536]{3,2,1,0:T(8,128)(2,1)} copy(bf16[4,1,60,1536]{3,0,2,1:T(4,128)(2,1)} %param.11) | data formatting | bytes 1474560 | tf_op args[0]
  3.5 7.2 %project.1 = (s32[40]{0:T(128)}, bf16[6,240,128]{2,1,0:T(8,128)(2,1)}, bf16[5,240,128]{2,1,0:T(8,128)(2,1)}, bf16[6,2,240,128]{3,2,1,0:T(8,128)(2,1)}, bf16[5,2,240,128]{3,2,1,0:T(8,128)(2,1)}) custom-call(s32[6,2]{1,0:T(8,128)} %copy.12.windows, bf16[4,1,60,1536]{3,2,1,0:T(8,128)(2,1)} %copy.13.tokens, f32[1536]{0:T(1024)} %shift.1, f32[1536]{0:T(1024)} %scale.1, ...), custom_call_target="tpu_custom_call" | custom-call | tf_op jit(solution)/shard_map/project/pallas_call | solution.py:251
  10.7 1.3 %collective-permute-start.4 = (bf16[5,2,240,128]{3,2,1,0:T(8,128)(2,1)}, bf16[5,2,240,128]{3,2,1,0:T(8,128)(2,1)S(1)}, u32[]{:S(2)}, u32[]{:S(2)}) collective-permute-start(bf16[5,2,240,128]{3,2,1,0:T(8,128)(2,1)} %get-tuple-element.18), channel_id=1, source_target_pairs={{2,0},{4,2},{6,4},{10,8},{12,10},{14,12},{3,1},{5,3},{7,5},{11,9},... | collective-permute-start | bytes 1843208 | tf_op jit(solution)/shard_map/ppermute | solution.py:271
  12.0 5.5 %collective-permute-start.2 = (bf16[5,2,240,128]{3,2,1,0:T(8,128)(2,1)}, bf16[5,2,240,128]{3,2,1,0:T(8,128)(2,1)S(1)}, u32[]{:S(2)}, u32[]{:S(2)}) collective-permute-start(bf16[5,2,240,128]{3,2,1,0:T(8,128)(2,1)} %get-tuple-element.18), channel_id=1, source_target_pairs={{0,2},{2,4},{4,6},{8,10},{10,12},{12,14},{1,3},{3,5},{5,7},{9,11},... | collective-permute-start | bytes 1843208 | tf_op jit(solution)/shard_map/ppermute | solution.py:270
  17.5 0.1 collective-permute-start.1
  17.6 12.0 %collective-permute-done.4.kv_right = bf16[5,2,240,128]{3,2,1,0:T(8,128)(2,1)S(1)} collective-permute-done((bf16[5,2,240,128]{3,2,1,0:T(8,128)(2,1)}, bf16[5,2,240,128]{3,2,1,0:T(8,128)(2,1)S(1)}, u32[]{:S(2)}, u32[]{:S(2)}) %collective-permute-start.4) | collective-permute-done | bytes 614432 | tf_op jit(solution)/shard_map/ppermute | solution.py:271
  29.6 0.0 copy-start.1
  29.6 0.0 collective-permute-start.5
  29.6 13.4 %collective-permute-done.2.kv_left = bf16[5,2,240,128]{3,2,1,0:T(8,128)(2,1)S(1)} collective-permute-done((bf16[5,2,240,128]{3,2,1,0:T(8,128)(2,1)}, bf16[5,2,240,128]{3,2,1,0:T(8,128)(2,1)S(1)}, u32[]{:S(2)}, u32[]{:S(2)}) %collective-permute-start.2) | collective-permute-done | bytes 614432 | tf_op jit(solution)/shard_map/ppermute | solution.py:270
  43.0 0.0 copy-start.2
  43.0 0.0 collective-permute-start.3
  43.0 2.6 %collective-permute-start = (bf16[5,240,128]{2,1,0:T(8,128)(2,1)}, bf16[5,240,128]{2,1,0:T(8,128)(2,1)S(1)}, u32[]{:S(2)}, u32[]{:S(2)}) collective-permute-start(bf16[5,240,128]{2,1,0:T(8,128)(2,1)} %get-tuple-element.16), channel_id=1, source_target_pairs={{0,8},{2,10},{4,12},{6,14},{8,0},{10,2},{12,4},{14,6},{1,9},{3,11}... | collective-permute-start | bytes 921608 | tf_op jit(solution)/shard_map/ppermute | solution.py:272
  45.6 0.7 pad_add_fusion.place
  46.3 14.1 %collective-permute-done = bf16[5,240,128]{2,1,0:T(8,128)(2,1)S(1)} collective-permute-done((bf16[5,240,128]{2,1,0:T(8,128)(2,1)}, bf16[5,240,128]{2,1,0:T(8,128)(2,1)S(1)}, u32[]{:S(2)}, u32[]{:S(2)}) %collective-permute-start) | collective-permute-done | bytes 307232 | tf_op jit(solution)/shard_map/ppermute | solution.py:272
  60.4 0.0 copy-start.6
  60.4 0.0 collective-permute-done.1.kv_own2
  60.4 0.0 copy-start
  60.4 0.0 collective-permute-done.5.kv_right2
  60.4 0.0 copy-start.3
  60.4 0.0 collective-permute-done.3.kv_left2
  60.4 0.0 copy-start.4
  60.4 0.0 copy-done.1
  60.5 0.0 copy-done.2
  60.5 0.7 copy-done.6
  61.1 0.2 copy-done
  61.4 0.2 copy-done.3
  61.5 0.2 copy-done.4
  61.8 9.6 %attend.1 = (f32[6,240,128]{2,1,0:T(8,128)}, f32[256,128]{1,0:T(8,128)}, bf16[1,5,240,128]{3,2,1,0:T(8,128)(2,1)}, f32[1,8,256]{2,1,0:T(8,128)}) custom-call(s32[40]{0:T(128)} %get-tuple-element.14.meta, s32[4]{0:T(128)} %pad_add_fusion.place, s32[8,6]{1,0:T(8,128)} %lists.1, s32[8]{0:T(128)} %valid.1, bf16[6,240,128]{2,1,0:T(8,128)(2,1)} %get-tuple-element.15.q_here, ...), custom_call_target="tpu_custom_call" | custom-call | tf_op jit(solution)/shard_map/attend/pallas_call | solution.py:279
  71.4 0.0 collective-permute-start.6
  71.4 2.9 %collective-permute-start.7 = (f32[8,256]{1,0:T(8,128)}, f32[8,256]{1,0:T(8,128)S(1)}, u32[]{:S(2)}, u32[]{:S(2)}) collective-permute-start(f32[8,256]{1,0:T(8,128)} %bitcast.13), channel_id=1, source_target_pairs={{8,0},{10,2},{12,4},{14,6},{0,8},{2,10},{4,12},{6,14},{9,1},{11,3}... | collective-permute-start | bytes 24584 | tf_op jit(solution)/shard_map/ppermute | solution.py:300
  74.4 13.9 %collective-permute-done.7 = f32[8,256]{1,0:T(8,128)S(1)} collective-permute-done((f32[8,256]{1,0:T(8,128)}, f32[8,256]{1,0:T(8,128)S(1)}, u32[]{:S(2)}, u32[]{:S(2)}) %collective-permute-start.7) | collective-permute-done | bytes 8224 | tf_op jit(solution)/shard_map/ppermute | solution.py:300
  88.3 0.0 copy-start.7
  88.3 0.0 collective-permute-done.6
  88.3 0.0 copy-start.5
  88.3 0.6 copy-done.7
  88.9 0.1 copy-done.5
  89.0 5.2 %output.1 = bf16[4,1,60,1536]{3,2,1,0:T(8,128)(2,1)} custom-call(s32[40]{0:T(128)} %get-tuple-element.14.meta, s32[4]{0:T(128)} %pad_add_fusion.place, bf16[4,1,60,1536]{3,2,1,0:T(8,128)(2,1)} %copy.13.tokens, f32[1536]{0:T(1024)} %gate.1, bf16[768,1536]{1,0:T(8,128)(2,1)} %w_out.1, f32[6,240,128]{2,1,0:T(8,128)} %get-tuple-element.19.o_own, ...), custom_call_target="tpu_custom_call" | custom-call | tf_op jit(solution)/shard_map/output/pallas_call | solution.py:302
  94.2 2.6 %copy.15 = bf16[4,1,60,1536]{3,0,2,1:T(4,128)(2,1)} copy(bf16[4,1,60,1536]{3,2,1,0:T(8,128)(2,1)} %output.1) | data formatting | bytes 1474560 | tf_op jit(solution)/shard_map/output/pallas_call | solution.py:302
Async XLA Ops:
  10.7 18.9 %collective-permute-start.4 = (bf16[5,2,240,128]{3,2,1,0:T(8,128)(2,1)}, bf16[5,2,240,128]{3,2,1,0:T(8,128)(2,1)S(1)}, u32[]{:S(2)}, u32[]{:S(2)}) collective-permute-start(bf16[5,2,240,128]{3,2,1,0:T(8,128)(2,1)} %get-tuple-element.18), channel_id=1, source_target_pairs={{2,0},{4,2},{6,4},{10,8},{12,10},{14,12},{3,1},{5,3},{7,5},{11,9},... | collective-permute-start | bytes 1843208 | tf_op jit(solution)/shard_map/ppermute | solution.py:271
  12.0 31.1 %collective-permute-start.2 = (bf16[5,2,240,128]{3,2,1,0:T(8,128)(2,1)}, bf16[5,2,240,128]{3,2,1,0:T(8,128)(2,1)S(1)}, u32[]{:S(2)}, u32[]{:S(2)}) collective-permute-start(bf16[5,2,240,128]{3,2,1,0:T(8,128)(2,1)} %get-tuple-element.18), channel_id=1, source_target_pairs={{0,2},{2,4},{4,6},{8,10},{10,12},{12,14},{1,3},{3,5},{5,7},{9,11},... | collective-permute-start | bytes 1843208 | tf_op jit(solution)/shard_map/ppermute | solution.py:270
  17.5 42.9 %collective-permute-start.1 = (bf16[6,2,240,128]{3,2,1,0:T(8,128)(2,1)}, bf16[6,2,240,128]{3,2,1,0:T(8,128)(2,1)S(1)}, u32[]{:S(2)}, u32[]{:S(2)}) collective-permute-start(bf16[6,2,240,128]{3,2,1,0:T(8,128)(2,1)} %get-tuple-element.17.kv_own), channel_id=1, source_target_pairs={{0,1},{1,0},{2,3},{3,2},{4,5},{5,4},{6,7},{7,6},{8,9},{9,8},{10,11... | collective-permute-start | bytes 2211848 | tf_op jit(solution)/shard_map/ppermute | solution.py:273
  29.6 30.9 %copy-start.1 = (bf16[5,2,240,128]{3,2,1,0:T(8,128)(2,1)}, bf16[5,2,240,128]{3,2,1,0:T(8,128)(2,1)S(1)}, u32[]{:S(2)}) copy-start(bf16[5,2,240,128]{3,2,1,0:T(8,128)(2,1)S(1)} %collective-permute-done.4.kv_right) | copy-start | bytes 1843204
  29.6 30.8 %collective-permute-start.5 = (bf16[5,2,240,128]{3,2,1,0:T(8,128)(2,1)S(1)}, bf16[5,2,240,128]{3,2,1,0:T(8,128)(2,1)S(1)}, u32[]{:S(2)}, u32[]{:S(2)}) collective-permute-start(bf16[5,2,240,128]{3,2,1,0:T(8,128)(2,1)S(1)} %collective-permute-done.4.kv_right), channel_id=1, source_target_pairs={{0,1},{1,0},{2,3},{3,2},{4,5},{5,4},{6,7},{7,6},{8,9},{9,8},{10,11... | collective-permute-start | bytes 1843208 | tf_op jit(solution)/shard_map/ppermute | solution.py:275
  43.0 17.4 %copy-start.2 = (bf16[5,2,240,128]{3,2,1,0:T(8,128)(2,1)}, bf16[5,2,240,128]{3,2,1,0:T(8,128)(2,1)S(1)}, u32[]{:S(2)}) copy-start(bf16[5,2,240,128]{3,2,1,0:T(8,128)(2,1)S(1)} %collective-permute-done.2.kv_left) | copy-start | bytes 1843204
  43.0 17.4 %collective-permute-start.3 = (bf16[5,2,240,128]{3,2,1,0:T(8,128)(2,1)S(1)}, bf16[5,2,240,128]{3,2,1,0:T(8,128)(2,1)S(1)}, u32[]{:S(2)}, u32[]{:S(2)}) collective-permute-start(bf16[5,2,240,128]{3,2,1,0:T(8,128)(2,1)S(1)} %collective-permute-done.2.kv_left), channel_id=1, source_target_pairs={{0,1},{1,0},{2,3},{3,2},{4,5},{5,4},{6,7},{7,6},{8,9},{9,8},{10,11... | collective-permute-start | bytes 1843208 | tf_op jit(solution)/shard_map/ppermute | solution.py:274
  43.0 17.4 %collective-permute-start = (bf16[5,240,128]{2,1,0:T(8,128)(2,1)}, bf16[5,240,128]{2,1,0:T(8,128)(2,1)S(1)}, u32[]{:S(2)}, u32[]{:S(2)}) collective-permute-start(bf16[5,240,128]{2,1,0:T(8,128)(2,1)} %get-tuple-element.16), channel_id=1, source_target_pairs={{0,8},{2,10},{4,12},{6,14},{8,0},{10,2},{12,4},{14,6},{1,9},{3,11}... | collective-permute-start | bytes 921608 | tf_op jit(solution)/shard_map/ppermute | solution.py:272
  60.4 0.7 copy-start.6
  60.4 0.9 copy-start
  60.4 1.1 %copy-start.3 = (bf16[5,2,240,128]{3,2,1,0:T(8,128)(2,1)}, bf16[5,2,240,128]{3,2,1,0:T(8,128)(2,1)S(1)}, u32[]{:S(2)}) copy-start(bf16[5,2,240,128]{3,2,1,0:T(8,128)(2,1)S(1)} %collective-permute-done.5.kv_right2) | copy-start | bytes 1843204
  60.4 1.4 %copy-start.4 = (bf16[5,2,240,128]{3,2,1,0:T(8,128)(2,1)}, bf16[5,2,240,128]{3,2,1,0:T(8,128)(2,1)S(1)}, u32[]{:S(2)}) copy-start(bf16[5,2,240,128]{3,2,1,0:T(8,128)(2,1)S(1)} %collective-permute-done.3.kv_left2) | copy-start | bytes 1843204
  71.4 16.9 %collective-permute-start.6 = (bf16[5,240,128]{2,1,0:T(8,128)(2,1)}, bf16[5,240,128]{2,1,0:T(8,128)(2,1)S(1)}, u32[]{:S(2)}, u32[]{:S(2)}) collective-permute-start(bf16[5,240,128]{2,1,0:T(8,128)(2,1)} %bitcast.12), channel_id=1, source_target_pairs={{8,0},{10,2},{12,4},{14,6},{0,8},{2,10},{4,12},{6,14},{9,1},{11,3}... | collective-permute-start | bytes 921608 | tf_op jit(solution)/shard_map/ppermute | solution.py:299
  71.4 16.8 %collective-permute-start.7 = (f32[8,256]{1,0:T(8,128)}, f32[8,256]{1,0:T(8,128)S(1)}, u32[]{:S(2)}, u32[]{:S(2)}) collective-permute-start(f32[8,256]{1,0:T(8,128)} %bitcast.13), channel_id=1, source_target_pairs={{8,0},{10,2},{12,4},{14,6},{0,8},{2,10},{4,12},{6,14},{9,1},{11,3}... | collective-permute-start | bytes 24584 | tf_op jit(solution)/shard_map/ppermute | solution.py:300
  88.3 0.6 copy-start.7
  88.3 0.7 copy-start.5

commit v2 on v1

--- a/solution.py
+++ b/solution.py
@@ -7,6 +7,7 @@
 from jax.experimental.pallas import tpu as pltpu
 from jax.sharding import PartitionSpec as P
 
+
 HEAD_DIM = 128
 NEG = -1e30
 LOG2E = 1.4426950408889634
@@ -20,7 +21,7 @@
 
 def rank_heads(windows, meta, heads):
     for column, count_at, slot_at, order_at in ((1, N_H, SLOT_H, ORDER_H), (0, N_V, SLOT_V, ORDER_V)):
-        reach = [jnp.where(windows[h, column] >= 3, 1, 0) for h in range(heads)]
+        reach = [jnp.where(windows[column, h] >= 3, 1, 0) for h in range(heads)]
         total = sum(reach[1:], reach[0])
         meta[count_at] = total
         ahead, behind = jnp.int32(0), total
@@ -34,9 +35,9 @@
 
 def project_kernel(
     heads, windows, tokens, shift, scale, w_qkv, q_gain, k_gain,
-    meta, q_here, q_send, kv_here, kv_send, mod32, w_buf, sems,
+    meta, q_here, q_send, kv_here, kv_send, w_buf, sems,
 ):
-    frames, _, tile_tokens, _ = tokens.shape
+    tile_tokens, frames, _ = tokens.shape
     inner = heads * HEAD_DIM
     half = inner // 2
     order = (2, 3, 4, 5, 0, 1)
@@ -49,14 +50,12 @@
     rank_heads(windows, meta, heads)
     gain_row = 1.0 + scale[...][None, :]
     shift_row = shift[...][None, :]
-    for f in range(frames):
-        floated = tokens[f, 0].astype(jnp.float32)
-        average = jnp.mean(floated, axis=-1, keepdims=True)
-        centered = floated - average
-        variance = jnp.mean(centered * centered, axis=-1, keepdims=True)
-        normed = centered * lax.rsqrt(variance + 1e-06)
-        mod32[f * tile_tokens : (f + 1) * tile_tokens, :] = normed * gain_row + shift_row
-    modulated = mod32[...].astype(jnp.bfloat16)
+    floated = tokens[...].astype(jnp.float32).reshape(tile_tokens * frames, -1)
+    average = jnp.mean(floated, axis=-1, keepdims=True)
+    centered = floated - average
+    variance = jnp.mean(centered * centered, axis=-1, keepdims=True)
+    normed = centered * lax.rsqrt(variance + 1e-06)
+    modulated = (normed * gain_row + shift_row).astype(jnp.bfloat16)
 
     def block(j):
         copies[j].wait()
@@ -93,18 +92,15 @@
     directions, slots, rows, _ = q_visit.shape
     frame_total, listed = lists.shape
     frames = frame_total // 2
-    tile_tokens = rows // frames
-    tile_keys = frame_total * tile_tokens
+    tile_keys = 2 * rows
     here = place[0]
     has_left, has_right = place[1], place[2]
 
     key_at = lax.broadcasted_iota(jnp.int32, (1, 3 * tile_keys), 1)
     query_at = lax.broadcasted_iota(jnp.int32, (rows, 1), 0)
-    group = jnp.zeros((1, 3 * tile_keys), jnp.int32)
-    for j in range(1, 3 * frame_total):
-        group = group + jnp.where(key_at >= j * tile_tokens, 1, 0)
-    tile = jnp.where(group >= frame_total, 1, 0) + jnp.where(group >= 2 * frame_total, 1, 0)
-    frame_slot = group - tile * frame_total
+    part = sum(jnp.where(key_at >= j * rows, 1, 0) for j in range(1, 6))
+    tile = part // 2
+    frame_slot = (part - 2 * tile) * frames + lax.rem(key_at, frames)
     absent = jnp.where((tile == 1) & (has_left == 0) | (tile == 2) & (has_right == 0), NEG, 0.0)
     full = jnp.zeros((rows, 3 * tile_keys), jnp.float32)
     for f in range(frames):
@@ -118,8 +114,7 @@
             seen = seen & jnp.where(valid[frame] == 1, 1, 0)
             row = jnp.where((frame_slot == s) & (seen == 1), 0.0, row)
         row = jnp.minimum(row, absent)
-        inside = (query_at >= f * tile_tokens) & (query_at < (f + 1) * tile_tokens)
-        full = jnp.where(inside, row, full)
+        full = jnp.where(lax.rem(query_at, frames) == f, row, full)
     bias[...] = full
     stats[...] = jnp.zeros_like(stats)
     q_all[0:heads] = q_here[...]
@@ -129,7 +124,7 @@
     lane = lax.broadcasted_iota(jnp.int32, (rows, lanes), 1)
     factor = HEAD_DIM**-0.5 * LOG2E
 
-    def softmax_item(item, head, refs_slots, lane_at):
+    def softmax_item(item, refs_slots, lane_at):
         keys = jnp.concatenate([ref[slot, 0] for ref, slot in refs_slots], axis=0)
         values = jnp.concatenate([ref[slot, 1] for ref, slot in refs_slots], axis=0)
         scores = lax.dot_general(
@@ -150,14 +145,14 @@
         @pl.when(wide)
         def _():
             store(softmax_item(
-                item, head,
+                item,
                 [(kv_own, head), (kv_own2, head), (kv_left, slot), (kv_left2, slot), (kv_right, slot), (kv_right2, slot)],
                 lane_at,
             ))
 
         @pl.when(jnp.logical_not(wide))
         def _():
-            store(softmax_item(item, head, [(kv_own, head), (kv_own2, head)], lane_at))
+            store(softmax_item(item, [(kv_own, head), (kv_own2, head)], lane_at))
 
     @pl.loop(0, heads)
     def _(h):
@@ -182,10 +177,10 @@
 
 def output_kernel(
     heads, meta, place, tokens, gate, w_out, o_own, lse_own, o_back, lse_back,
-    out, attended, wide, back,
+    out, attended, back,
 ):
     directions, slots, rows, _ = o_back.shape
-    frames, _, tile_tokens, _ = tokens.shape
+    tile_tokens, frames, _ = tokens.shape
     back[...] = jnp.zeros_like(back)
     for d in range(directions):
         back[d * 8 : (d + 1) * 8] = lse_back[d]
@@ -209,10 +204,8 @@
         mixed = sum((w * o for w, (_, o) in zip(weights[1:], parts[1:])), weights[0] * parts[0][1])
         attended[:, h * HEAD_DIM : (h + 1) * HEAD_DIM] = (mixed / total).astype(jnp.bfloat16)
     branch = jnp.dot(attended[...], w_out[...], preferred_element_type=jnp.float32)
-    wide[...] = branch * gate[...][None, :]
-    for f in range(frames):
-        mixed = tokens[f, 0].astype(jnp.float32) + wide[f * tile_tokens : (f + 1) * tile_tokens, :]
-        out[f, 0] = mixed.astype(jnp.bfloat16)
+    branch = (branch * gate[...][None, :]).reshape(tile_tokens, frames, -1)
+    out[...] = (tokens[...].astype(jnp.float32) + branch).astype(jnp.bfloat16)
 
 
 def per_device(
@@ -228,6 +221,7 @@
     tile_cols = min(8, space_size // 2)
     tile_rows = space_size // tile_cols
     bf16, f32 = jnp.bfloat16, jnp.float32
+    tokens = jnp.transpose(tokens_in[:, 0], (1, 0, 2))
 
     spots = range(space_size)
     to_right = [(i, i + 1) for i in spots if i % tile_cols != tile_cols - 1]
@@ -260,57 +254,73 @@
             jax.ShapeDtypeStruct((slots, 2, rows, HEAD_DIM), bf16),
         ],
         scratch_shapes=[
-            pltpu.VMEM((rows, feature_dim), f32),
             pltpu.VMEM((6, feature_dim, inner // 2), bf16),
             pltpu.SemaphoreType.DMA((6,)),
         ],
         name="project",
-    )(windows, tokens_in, mod_shift, mod_scale, w_qkv, q_gain, k_gain)
-
-    kv_left = lax.ppermute(kv_send, "space", to_right)
-    kv_right = lax.ppermute(kv_send, "space", to_left)
-    q_visit = jnp.stack([lax.ppermute(q_send, "space", pairs) for pairs in vertical])
-    kv_other = lax.ppermute(kv_here, "tm", swap)
-    kv_left2 = lax.ppermute(kv_left, "tm", swap)
-    kv_right2 = lax.ppermute(kv_right, "tm", swap)
-
+    )(windows.T, tokens, mod_shift, mod_scale, w_qkv, q_gain, k_gain)
+
+    back = [[(j, i) for i, j in pairs] for pairs in vertical]
     lanes = 128
     stat_rows = 256
-    o_own, lse_own, o_visit, lse_visit = pl.pallas_call(
-        functools.partial(attend_kernel, heads, lanes),
-        in_specs=[SMEM] * 4 + [VMEM] * 8,
-        out_specs=[VMEM] * 4,
-        out_shape=[
-            jax.ShapeDtypeStruct((heads, rows, HEAD_DIM), f32),
-            jax.ShapeDtypeStruct((stat_rows, lanes), f32),
-            jax.ShapeDtypeStruct((directions, slots, rows, HEAD_DIM), bf16),
-            jax.ShapeDtypeStruct((directions, 8, stat_rows), f32),
-        ],
-        scratch_shapes=[
-            pltpu.VMEM((rows, 3 * 2 * rows), f32),
-            pltpu.VMEM((heads + directions * slots, rows, HEAD_DIM), bf16),
-            pltpu.VMEM((stat_rows, lanes), f32),
-        ],
-        name="attend",
-    )(meta, place, frame_lists, frame_valid, q_here, q_visit,
-      kv_here, kv_other, kv_left, kv_left2, kv_right, kv_right2)
-
-    back = [[(j, i) for i, j in pairs] for pairs in vertical]
-    o_back = jnp.stack([lax.ppermute(o_visit[d], "space", back[d]) for d in range(directions)])
-    lse_back = jnp.stack([lax.ppermute(lse_visit[d], "space", back[d]) for d in range(directions)])
-
-    return pl.pallas_call(
-        functools.partial(output_kernel, heads),
-        in_specs=[SMEM, SMEM] + [VMEM] * 7,
-        out_specs=VMEM,
-        out_shape=jax.ShapeDtypeStruct(tokens_in.shape, bf16),
-        scratch_shapes=[
-            pltpu.VMEM((rows, inner), bf16),
-            pltpu.VMEM((rows, feature_dim), f32),
-            pltpu.VMEM((lanes, stat_rows), f32),
-        ],
-        name="output",
-    )(meta, place, tokens_in, mod_gate, w_out, o_own, lse_own, o_back, lse_back)
+
+    def along_row(sent, *operands):
+        return row_step(sent, *operands)
+
+    def row_step(sent, kv_send, kv_here, q_send, q_here, meta):
+        kv_send = kv_send[:sent]
+        q_visit = jnp.stack([lax.ppermute(q_send, "space", pairs) for pairs in vertical])
+        kv_left = lax.ppermute(kv_send, "space", to_right)
+        kv_right = lax.ppermute(kv_send, "space", to_left)
+        kv_other = lax.ppermute(kv_here, "tm", swap)
+        kv_left2 = lax.ppermute(kv_left, "tm", swap)
+        kv_right2 = lax.ppermute(kv_right, "tm", swap)
+        return pl.pallas_call(
+            functools.partial(attend_kernel, heads, lanes),
+            in_specs=[SMEM] * 4 + [VMEM] * 8,
+            out_specs=[VMEM] * 4,
+            out_shape=[
+                jax.ShapeDtypeStruct((heads, rows, HEAD_DIM), f32),
+                jax.ShapeDtypeStruct((stat_rows, lanes), f32),
+                jax.ShapeDtypeStruct((directions, slots, rows, HEAD_DIM), bf16),
+                jax.ShapeDtypeStruct((directions, 8, stat_rows), f32),
+            ],
+            scratch_shapes=[
+                pltpu.VMEM((rows, 3 * 2 * rows), f32),
+                pltpu.VMEM((heads + directions * slots, rows, HEAD_DIM), bf16),
+                pltpu.VMEM((stat_rows, lanes), f32),
+            ],
+            name="attend",
+        )(meta, place, frame_lists, frame_valid, q_here, q_visit,
+          kv_here, kv_other, kv_left, kv_left2, kv_right, kv_right2)
+
+    o_own, lse_own, o_visit, lse_visit = lax.switch(
+        meta[N_H] - 1,
+        [functools.partial(along_row, n) for n in range(1, slots + 1)],
+        kv_send, kv_here, q_send, q_here, meta,
+    )
+
+    def between_rows(sent, o_own, lse_own, o_visit, lse_visit, meta):
+        o_back = jnp.stack([lax.ppermute(o_visit[d, :sent], "space", back[d]) for d in range(directions)])
+        lse_back = jnp.stack([lax.ppermute(lse_visit[d], "space", back[d]) for d in range(directions)])
+        return pl.pallas_call(
+            functools.partial(output_kernel, heads),
+            in_specs=[SMEM, SMEM] + [VMEM] * 7,
+            out_specs=VMEM,
+            out_shape=jax.ShapeDtypeStruct(tokens.shape, bf16),
+            scratch_shapes=[
+                pltpu.VMEM((rows, inner), bf16),
+                pltpu.VMEM((lanes, stat_rows), f32),
+            ],
+            name="output",
+        )(meta, place, tokens, mod_gate, w_out, o_own, lse_own, o_back, lse_back)
+
+    mixed = lax.switch(
+        meta[N_V] - 1,
+        [functools.partial(between_rows, n) for n in range(1, slots + 1)],
+        o_own, lse_own, o_visit, lse_visit, meta,
+    )
+    return jnp.transpose(mixed, (1, 0, 2))[:, None]
 
 
 def solution(mesh):

time: 96.6 us -> 74.9 us (0.78)
  waiting for transfers between devices: 53.5 us -> 34.2 us
  local copies, waits for them, and re-layouts: 8.11 us -> 5.62 us
  Pallas kernels: 22 us -> 20.2 us
  between operations: 0.09 us -> 1.28 us
    ppermute x8, waiting for transfers between devices: 53.5 us -> 34.2 us  [the longest x1 14.8 us: row_step(): lax.ppermute(q_send, 'space', pairs)]
    unnamed x18 -> x10, local copies, waits for them, and re-layouts: 5.55 us -> 0.03 us
    cond x0 -> x14, local copies, waits for them, and re-layouts: none -> 2.91 us
    pallas_call x1 -> x0, local copies, waits for them, and re-layouts: 2.57 us -> none  [per_device(): pl.pallas_call(functools.partial(output_kernel, heads), in_specs=[SMEM, S...]
    slice x0 -> x2, local copies, waits for them, and re-layouts: none -> 1.77 us  [the longest x1 1.16 us: row_step(): kv_send = kv_send[:sent]]
    pallas_call x2, Pallas kernels: 14.9 us -> 13.4 us  [the longest x1 9.27 us: row_step(): pl.pallas_call(functools.partial(attend_kernel, heads, lanes), in_specs=[...]
  transfers between devices with their start and end apart: 8 -> 8, of which waited for: 4 -> 4; matrix products, arithmetic and copies ran while one was open for 1% -> 0% of each run, Pallas kernels for 0% -> 0%
where the time goes in v2:
time: 74.9 us; the launch traced here: 74.7 us
  waiting for transfers between devices  34.2 us (46%)
  Pallas kernels  20.2 us (27%)
  starting transfers between devices  12.7 us (17%)
  local copies, waits for them, and re-layouts  5.62 us (8%)
  between operations  1.28 us (2%)
    ppermute x1, waiting for transfers between devices, row_step(): lax.ppermute(q_send, 'space', pairs)  14.8 us
    pallas_call x1, Pallas kernels, row_step(): pl.pallas_call(functools.partial(attend_kernel, heads, lanes), in_specs=[...  9.27 us
    ppermute x1, waiting for transfers between devices, row_step(): kv_left = lax.ppermute(kv_send, 'space', to_right)  7.31 us
    pallas_call x1, Pallas kernels, per_device(): pl.pallas_call(functools.partial(project_kernel, heads), in_specs=[SMEM,...  6.8 us
    ppermute x1, waiting for transfers between devices, row_step(): kv_right = lax.ppermute(kv_send, 'space', to_left)  6.3 us
    ppermute x1, waiting for transfers between devices, between_rows(): lax.ppermute(lse_visit[d], 'space', back[d])  5.84 us
    ppermute x1, starting transfers between devices, row_step(): kv_left = lax.ppermute(kv_send, 'space', to_right)  5.77 us
    pallas_call x1, Pallas kernels, between_rows(): pl.pallas_call(functools.partial(output_kernel, heads), in_specs=[SMEM, S...  4.14 us
  transfers between devices with their start and end apart: 8, of which 4 were waited for; matrix products, arithmetic and copies ran while one was open for 0% of the time, Pallas kernels for 0%

profile of v2, /device:TPU:0, one launch (start us, length us, event | category | flops | bytes accessed | tf_op | source)
XLA Modules:
  0.0 74.7 jit_solution(10984151151771236817)
XLA Ops:
  0.0 0.0 copy-start.32
  0.0 0.0 copy-start.30
  0.0 0.1 pad_add_fusion
  0.1 6.8 %project.1 = (s32[40]{0:T(128)S(1)}, bf16[6,240,128]{2,1,0:T(8,128)(2,1)S(1)}, bf16[5,240,128]{2,1,0:T(8,128)(2,1)}, bf16[6,2,240,128]{3,2,1,0:T(8,128)(2,1)}, bf16[5,2,240,128]{3,2,1,0:T(8,128)(2,1)}) custom-call(s32[2,6]{1,0:T(2,128)} %bitcast.62, bf16[60,4,1536]{2,1,0:T(4,128)(2,1)} %bitcast.42, f32[1536]{0:T(1024)} %shift.1, f32[1536]{0:T(1024)} %scale.1, ...), custom_call_target="tpu_custom_call" | custom-call | tf_op jit(solution)/shard_map/project/pallas_call | solution.py:245
  6.9 0.6 fusion
  8.7 0.0 copy-done.32
  8.7 0.0 copy-done.30
  8.7 0.0 copy-start
  8.7 0.0 copy-start.1
  8.7 0.0 copy-start.23
  8.8 51.3 %conditional.2 = ((f32[6,240,128]{2,1,0:T(8,128)}, f32[256,128]{1,0:T(8,128)}, bf16[1,5,240,128]{3,2,1,0:T(8,128)(2,1)}, f32[1,8,256]{2,1,0:T(8,128)S(1)})) conditional(s32[]{:T(128)} %bitcast.29, (bf16[5,240,128]{2,1,0:T(8,128)(2,1)}, bf16[6,2,240,128]{3,2,1,0:T(8,128)(2,1)}, bf16[5,2,240,128]{3,2,1,0:T(8,128)(2,1)}, ...), branch_computations={%region_0.1_spmd, %region_1.2_spmd, %region_2.3_spmd, %region_3.4_... | conditional | bytes 25067908 | solution.py:297
  8.8 1.2 %slice.22 = bf16[3,2,240,128]{3,2,1,0:T(8,128)(2,1)S(1)} slice(bf16[5,2,240,128]{3,2,1,0:T(8,128)(2,1)} %get-tuple-element.204), slice={[0:3], [0:2], [0:240], [0:128]} | slice | bytes 737280 | tf_op jit(solution)/shard_map/cond/branch_2_fun/slice | solution.py:271
  9.9 1.3 %collective-permute-start.16 = (bf16[3,2,240,128]{3,2,1,0:T(8,128)(2,1)S(1)}, bf16[3,2,240,128]{3,2,1,0:T(8,128)(2,1)S(1)}, u32[]{:S(2)}, u32[]{:S(2)}) collective-permute-start(bf16[3,2,240,128]{3,2,1,0:T(8,128)(2,1)S(1)} %slice.22), channel_id=1, source_target_pairs={{2,0},{4,2},{6,4},{10,8},{12,10},{14,12},{3,1},{5,3},{7,5},{11,9},... | collective-permute-start | bytes 1105928 | tf_op jit(solution)/shard_map/cond/branch_2_fun/ppermute | solution.py:274
  11.2 5.8 %collective-permute-start.14 = (bf16[3,2,240,128]{3,2,1,0:T(8,128)(2,1)S(1)}, bf16[3,2,240,128]{3,2,1,0:T(8,128)(2,1)S(1)}, u32[]{:S(2)}, u32[]{:S(2)}) collective-permute-start(bf16[3,2,240,128]{3,2,1,0:T(8,128)(2,1)S(1)} %slice.22), channel_id=1, source_target_pairs={{0,2},{2,4},{4,6},{8,10},{10,12},{12,14},{1,3},{3,5},{5,7},{9,11},... | collective-permute-start | bytes 1105928 | tf_op jit(solution)/shard_map/cond/branch_2_fun/ppermute | solution.py:273
  17.0 0.1 collective-permute-start.13
  17.1 6.3 %collective-permute-done.16.kv_right = bf16[3,2,240,128]{3,2,1,0:T(8,128)(2,1)S(1)} collective-permute-done((bf16[3,2,240,128]{3,2,1,0:T(8,128)(2,1)S(1)}, bf16[3,2,240,128]{3,2,1,0:T(8,128)(2,1)S(1)}, u32[]{:S(2)}, u32[]{:S(2)}) %collective-permute-start.16) | collective-permute-done | bytes 368672 | tf_op jit(solution)/shard_map/cond/branch_2_fun/ppermute | solution.py:274
  23.4 0.0 copy-start.10
  23.4 0.7 copy-done.10
  24.1 0.0 collective-permute-start.17
  24.1 7.3 %collective-permute-done.14.kv_left = bf16[3,2,240,128]{3,2,1,0:T(8,128)(2,1)S(1)} collective-permute-done((bf16[3,2,240,128]{3,2,1,0:T(8,128)(2,1)S(1)}, bf16[3,2,240,128]{3,2,1,0:T(8,128)(2,1)S(1)}, u32[]{:S(2)}, u32[]{:S(2)}) %collective-permute-start.14) | collective-permute-done | bytes 368672 | tf_op jit(solution)/shard_map/cond/branch_2_fun/ppermute | solution.py:273
  31.5 0.0 copy-start.11
  31.5 0.0 collective-permute-start.15
  31.5 2.6 %collective-permute-start.12 = (bf16[5,240,128]{2,1,0:T(8,128)(2,1)}, bf16[5,240,128]{2,1,0:T(8,128)(2,1)S(1)}, u32[]{:S(2)}, u32[]{:S(2)}) collective-permute-start(bf16[5,240,128]{2,1,0:T(8,128)(2,1)} %get-tuple-element.202), channel_id=1, source_target_pairs={{0,8},{2,10},{4,12},{6,14},{8,0},{10,2},{12,4},{14,6},{1,9},{3,11}... | collective-permute-start | bytes 921608 | tf_op jit(solution)/shard_map/cond/branch_2_fun/ppermute | solution.py:272
  34.0 14.8 %collective-permute-done.12 = bf16[5,240,128]{2,1,0:T(8,128)(2,1)S(1)} collective-permute-done((bf16[5,240,128]{2,1,0:T(8,128)(2,1)}, bf16[5,240,128]{2,1,0:T(8,128)(2,1)S(1)}, u32[]{:S(2)}, u32[]{:S(2)}) %collective-permute-start.12) | collective-permute-done | bytes 307232 | tf_op jit(solution)/shard_map/cond/branch_2_fun/ppermute | solution.py:272
  48.8 0.0 copy-start.15
  48.8 0.0 collective-permute-done.17.kv_right2
  48.8 0.0 copy-done.11
  48.8 0.0 copy-start.12
  48.9 0.0 collective-permute-done.15.kv_left2
  48.9 0.8 %copy-done.12 = bf16[3,2,240,128]{3,2,1,0:T(8,128)(2,1)} copy-done((bf16[3,2,240,128]{3,2,1,0:T(8,128)(2,1)}, bf16[3,2,240,128]{3,2,1,0:T(8,128)(2,1)S(1)}, u32[]{:S(2)}) %copy-start.12) | copy-done | bytes 368664 | tf_op jit(solution)/shard_map/cond
  49.6 0.0 copy-start.13
  49.6 0.0 collective-permute-done.13.kv_own2
  49.6 0.7 copy-done.13
  50.4 0.0 copy-done.15
  50.4 9.3 %attend.7 = (f32[6,240,128]{2,1,0:T(8,128)}, f32[256,128]{1,0:T(8,128)}, bf16[1,5,240,128]{3,2,1,0:T(8,128)(2,1)}, f32[1,8,256]{2,1,0:T(8,128)S(1)}) custom-call(s32[40]{0:T(128)S(1)} %get-tuple-element.197.meta, s32[4]{0:T(128)S(1)} %get-tuple-element.198.place, s32[8,6]{1,0:T(8,128)S(1)} %get-tuple-element.199.lists, s32[8]{0:T(128)S(1)} %get-tuple-element.200.valid, ...), custom_call_target="tpu_custom_call" | custom-call | tf_op jit(solution)/shard_map/cond/branch_2_fun/attend/pallas_call | solution.py:278
  60.1 0.0 copy-done
  60.1 0.0 copy-done.1
  60.1 0.0 copy-done.23
  60.1 14.6 %conditional.3 = (bf16[60,4,1536]{2,1,0:T(4,128)(2,1)}) conditional(s32[]{:T(128)} %bitcast.28, (bf16[1,5,240,128]{3,2,1,0:T(8,128)(2,1)}, f32[1,8,256]{2,1,0:T(8,128)S(1)}, s32[40]{0:T(128)S(1)}, s32[4]{0:T(128)S(1)}, bf16[60,4,1536]{2,1,0:T(4,128)(2,1)S(1)}, /*index=5*/f32[1536]{0:T(1024)S(1)}, ...), branch_computations={%region_5.6_spmd, %region_6.7_spmd, %region_7.8_spmd, %region_8.9_... | conditional | bytes 2523280 | solution.py:318
  60.2 0.9 %slice_bitcast_fusion.1 = bf16[2,240,128]{2,1,0:T(8,128)(2,1)S(1)} fusion(bf16[1,5,240,128]{3,2,1,0:T(8,128)(2,1)} %get-tuple-element.237), kind=kLoop, calls=%fused_computation.1 | loop fusion | bytes 245760 | tf_op jit(solution)/shard_map/cond/branch_1_fun/squeeze | solution.py:304
  61.1 0.1 collective-permute-start.34
  61.2 2.9 %collective-permute-start.35 = (f32[8,256]{1,0:T(8,128)S(1)}, f32[8,256]{1,0:T(8,128)S(1)}, u32[]{:S(2)}, u32[]{:S(2)}) collective-permute-start(f32[8,256]{1,0:T(8,128)S(1)} %bitcast.64), channel_id=1, source_target_pairs={{8,0},{10,2},{12,4},{14,6},{0,8},{2,10},{4,12},{6,14},{9,1},{11,3}... | collective-permute-start | bytes 24584 | tf_op jit(solution)/shard_map/cond/branch_1_fun/ppermute | solution.py:305
  64.1 5.8 %collective-permute-done.35 = f32[8,256]{1,0:T(8,128)S(1)} collective-permute-done((f32[8,256]{1,0:T(8,128)S(1)}, f32[8,256]{1,0:T(8,128)S(1)}, u32[]{:S(2)}, u32[]{:S(2)}) %collective-permute-start.35) | collective-permute-done | bytes 8224 | tf_op jit(solution)/shard_map/cond/branch_1_fun/ppermute | solution.py:305
  69.9 0.0 copy-start.34
  69.9 0.0 collective-permute-done.34
  69.9 0.0 copy-start.29
  69.9 0.6 copy-done.34
  70.5 0.1 copy-done.29
  70.6 4.1 %output.6 = bf16[60,4,1536]{2,1,0:T(4,128)(2,1)} custom-call(s32[40]{0:T(128)S(1)} %get-tuple-element.230.meta, s32[4]{0:T(128)S(1)} %get-tuple-element.231.place, bf16[60,4,1536]{2,1,0:T(4,128)(2,1)S(1)} %get-tuple-element.232.tokens, f32[1536]{0:T(1024)S(1)} %get-tuple-element.233.gate, bf16[768,1536]{1,0:T(8,128)(2,1)S(1)} %get-tuple-element.234.w_out, ...), custom_call_target="tpu_custom_call" | custom-call | tf_op jit(solution)/shard_map/cond/branch_1_fun/output/pallas_call | solution.py:306
Async XLA Ops:
  0.0 8.7 %copy-start.32 = (s32[8]{0:T(128)S(1)}, s32[8]{0:T(128)}, u32[]{:S(2)}) copy-start(s32[8]{0:T(128)} %param.31) | copy-start | bytes 100
  0.0 8.7 %copy-start.30 = (s32[8,6]{1,0:T(8,128)S(1)}, s32[8,6]{1,0:T(8,128)}, u32[]{:S(2)}) copy-start(s32[8,6]{1,0:T(8,128)} %param.30) | copy-start | bytes 580
  8.7 51.4 %copy-start = (bf16[768,1536]{1,0:T(8,128)(2,1)S(1)}, bf16[768,1536]{1,0:T(8,128)(2,1)}, u32[]{:S(2)}) copy-start(bf16[768,1536]{1,0:T(8,128)(2,1)} %param.28) | copy-start | bytes 7077892
  8.7 51.4 %copy-start.1 = (bf16[4,1,60,1536]{3,0,2,1:T(4,128)(2,1)S(1)}, bf16[4,1,60,1536]{3,0,2,1:T(4,128)(2,1)}, u32[]{:S(2)}) copy-start(bf16[4,1,60,1536]{3,0,2,1:T(4,128)(2,1)} %param.21) | copy-start | bytes 2211844
  8.7 51.4 %copy-start.23 = (f32[1536]{0:T(1024)S(1)}, f32[1536]{0:T(1024)}, u32[]{:S(2)}) copy-start(f32[1536]{0:T(1024)} %param.24) | copy-start | bytes 18436
  9.9 13.5 %collective-permute-start.16 = (bf16[3,2,240,128]{3,2,1,0:T(8,128)(2,1)S(1)}, bf16[3,2,240,128]{3,2,1,0:T(8,128)(2,1)S(1)}, u32[]{:S(2)}, u32[]{:S(2)}) collective-permute-start(bf16[3,2,240,128]{3,2,1,0:T(8,128)(2,1)S(1)} %slice.22), channel_id=1, source_target_pairs={{2,0},{4,2},{6,4},{10,8},{12,10},{14,12},{3,1},{5,3},{7,5},{11,9},... | collective-permute-start | bytes 1105928 | tf_op jit(solution)/shard_map/cond/branch_2_fun/ppermute | solution.py:274
  11.2 20.2 %collective-permute-start.14 = (bf16[3,2,240,128]{3,2,1,0:T(8,128)(2,1)S(1)}, bf16[3,2,240,128]{3,2,1,0:T(8,128)(2,1)S(1)}, u32[]{:S(2)}, u32[]{:S(2)}) collective-permute-start(bf16[3,2,240,128]{3,2,1,0:T(8,128)(2,1)S(1)} %slice.22), channel_id=1, source_target_pairs={{0,2},{2,4},{4,6},{8,10},{10,12},{12,14},{1,3},{3,5},{5,7},{9,11},... | collective-permute-start | bytes 1105928 | tf_op jit(solution)/shard_map/cond/branch_2_fun/ppermute | solution.py:273
  17.0 32.6 %collective-permute-start.13 = (bf16[6,2,240,128]{3,2,1,0:T(8,128)(2,1)}, bf16[6,2,240,128]{3,2,1,0:T(8,128)(2,1)}, u32[]{:S(2)}, u32[]{:S(2)}) collective-permute-start(bf16[6,2,240,128]{3,2,1,0:T(8,128)(2,1)} %get-tuple-element.203.kv_own), channel_id=1, source_target_pairs={{0,1},{1,0},{2,3},{3,2},{4,5},{5,4},{6,7},{7,6},{8,9},{9,8},{10,11... | collective-permute-start | bytes 2211848 | tf_op jit(solution)/shard_map/cond/branch_2_fun/ppermute | solution.py:275
  23.4 0.7 copy-start.10
  24.1 24.7 %collective-permute-start.17 = (bf16[3,2,240,128]{3,2,1,0:T(8,128)(2,1)S(1)}, bf16[3,2,240,128]{3,2,1,0:T(8,128)(2,1)S(1)}, u32[]{:S(2)}, u32[]{:S(2)}) collective-permute-start(bf16[3,2,240,128]{3,2,1,0:T(8,128)(2,1)S(1)} %collective-permute-done.16.kv_right), channel_id=1, source_target_pairs={{0,1},{1,0},{2,3},{3,2},{4,5},{5,4},{6,7},{7,6},{8,9},{9,8},{10,11... | collective-permute-start | bytes 1105928 | tf_op jit(solution)/shard_map/cond/branch_2_fun/ppermute | solution.py:277
  31.5 17.4 %copy-start.11 = (bf16[3,2,240,128]{3,2,1,0:T(8,128)(2,1)}, bf16[3,2,240,128]{3,2,1,0:T(8,128)(2,1)S(1)}, u32[]{:S(2)}) copy-start(bf16[3,2,240,128]{3,2,1,0:T(8,128)(2,1)S(1)} %collective-permute-done.14.kv_left) | copy-start | bytes 1105924 | tf_op jit(solution)/shard_map/cond
  31.5 17.4 %collective-permute-start.15 = (bf16[3,2,240,128]{3,2,1,0:T(8,128)(2,1)S(1)}, bf16[3,2,240,128]{3,2,1,0:T(8,128)(2,1)S(1)}, u32[]{:S(2)}, u32[]{:S(2)}) collective-permute-start(bf16[3,2,240,128]{3,2,1,0:T(8,128)(2,1)S(1)} %collective-permute-done.14.kv_left), channel_id=1, source_target_pairs={{0,1},{1,0},{2,3},{3,2},{4,5},{5,4},{6,7},{7,6},{8,9},{9,8},{10,11... | collective-permute-start | bytes 1105928 | tf_op jit(solution)/shard_map/cond/branch_2_fun/ppermute | solution.py:276
  31.5 17.4 %collective-permute-start.12 = (bf16[5,240,128]{2,1,0:T(8,128)(2,1)}, bf16[5,240,128]{2,1,0:T(8,128)(2,1)S(1)}, u32[]{:S(2)}, u32[]{:S(2)}) collective-permute-start(bf16[5,240,128]{2,1,0:T(8,128)(2,1)} %get-tuple-element.202), channel_id=1, source_target_pairs={{0,8},{2,10},{4,12},{6,14},{8,0},{10,2},{12,4},{14,6},{1,9},{3,11}... | collective-permute-start | bytes 921608 | tf_op jit(solution)/shard_map/cond/branch_2_fun/ppermute | solution.py:272
  48.8 1.5 %copy-start.15 = (bf16[5,240,128]{2,1,0:T(8,128)(2,1)}, bf16[5,240,128]{2,1,0:T(8,128)(2,1)S(1)}, u32[]{:S(2)}) copy-start(bf16[5,240,128]{2,1,0:T(8,128)(2,1)S(1)} %collective-permute-done.12) | copy-start | bytes 921604 | tf_op jit(solution)/shard_map/cond
  48.8 0.8 %copy-start.12 = (bf16[3,2,240,128]{3,2,1,0:T(8,128)(2,1)}, bf16[3,2,240,128]{3,2,1,0:T(8,128)(2,1)S(1)}, u32[]{:S(2)}) copy-start(bf16[3,2,240,128]{3,2,1,0:T(8,128)(2,1)S(1)} %collective-permute-done.17.kv_right2) | copy-start | bytes 1105924 | tf_op jit(solution)/shard_map/cond
  49.6 0.7 copy-start.13
  61.1 8.8 %collective-permute-start.34 = (bf16[2,240,128]{2,1,0:T(8,128)(2,1)S(1)}, bf16[2,240,128]{2,1,0:T(8,128)(2,1)S(1)}, u32[]{:S(2)}, u32[]{:S(2)}) collective-permute-start(bf16[2,240,128]{2,1,0:T(8,128)(2,1)S(1)} %slice_bitcast_fusion.1), channel_id=1, source_target_pairs={{8,0},{10,2},{12,4},{14,6},{0,8},{2,10},{4,12},{6,14},{9,1},{11,3}... | collective-permute-start | bytes 368648 | tf_op jit(solution)/shard_map/cond/branch_1_fun/ppermute | solution.py:304
  61.2 8.7 %collective-permute-start.35 = (f32[8,256]{1,0:T(8,128)S(1)}, f32[8,256]{1,0:T(8,128)S(1)}, u32[]{:S(2)}, u32[]{:S(2)}) collective-permute-start(f32[8,256]{1,0:T(8,128)S(1)} %bitcast.64), channel_id=1, source_target_pairs={{8,0},{10,2},{12,4},{14,6},{0,8},{2,10},{4,12},{6,14},{9,1},{11,3}... | collective-permute-start | bytes 24584 | tf_op jit(solution)/shard_map/cond/branch_1_fun/ppermute | solution.py:305
  69.9 0.6 copy-start.34
  69.9 0.7 copy-start.29

commit v3 on v2

v3 whole, which is shorter than its diff:
```python
import functools

import jax
import jax.numpy as jnp
from jax import lax
from jax.experimental import pallas as pl
from jax.experimental.pallas import tpu as pltpu
from jax.sharding import PartitionSpec as P


HEAD_DIM = 128
NEG = -1e30
LOG2E = 1.4426950408889634
N_H, N_V, N_BOTH, SLOT_H, SLOT_V, ORDER_H, ORDER_V = 0, 1, 2, 8, 16, 24, 32
META = 40

VMEM = pl.BlockSpec(memory_space=pltpu.VMEM)
SMEM = pl.BlockSpec(memory_space=pltpu.SMEM)
HBM = pl.BlockSpec(memory_space=pltpu.HBM)


def params(mebibytes):
    return pltpu.CompilerParams(vmem_limit_bytes=mebibytes << 20)


def rank_heads(windows, meta, heads):
    wide = [jnp.where(windows[1, h] >= 3, 1, 0) for h in range(heads)]
    tall = [jnp.where(windows[0, h] >= 3, 1, 0) for h in range(heads)]
    both = [w * t for w, t in zip(wide, tall)]
    meta[N_H], meta[N_V], meta[N_BOTH] = sum(wide), sum(tall), sum(both)
    for classes, slot_at, order_at in (
        ([1 - w for w in wide], SLOT_H, ORDER_H),
        ([2 - t - b for t, b in zip(tall, both)], SLOT_V, ORDER_V),
    ):
        for h in range(heads):
            slot = sum(
                jnp.where((classes[o] < classes[h]) | ((classes[o] == classes[h]) & (o < h)), 1, 0)
                for o in range(heads) if o != h
            )
            meta[slot_at + h] = slot
            meta[order_at + slot] = h


def project_kernel(
    heads, windows_at, tokens_at, shift_at, scale_at, w_qkv, q_gain_at, k_gain_at,
    meta, q_here, q_send, kv_here,
    windows, tokens, shift, scale, q_gain, k_gain, modulated, w_buf, small_sems, sems,
):
    tile_tokens, frames, _ = tokens.shape
    inner = heads * HEAD_DIM
    queries, keys, values = 0, 1, 2
    small = [
        pltpu.make_async_copy(there, ref, small_sems.at[i])
        for i, (there, ref) in enumerate((
            (tokens_at, tokens), (shift_at, shift), (scale_at, scale),
            (windows_at, windows), (k_gain_at, k_gain), (q_gain_at, q_gain),
        ))
    ]
    blocks = {
        j: pltpu.make_async_copy(w_qkv.at[:, pl.ds(j * inner, inner)], w_buf.at[j], sems.at[j])
        for j in (keys, values, queries)
    }
    for copy in (*small, *blocks.values()):
        copy.start()
    for copy in small:
        copy.wait()
    rank_heads(windows, meta, heads)
    gain_row = 1.0 + scale[...][None, :]
    shift_row = shift[...][None, :]
    step = 4
    for t in range(0, tile_tokens, step):
        floated = tokens[t : t + step].astype(jnp.float32).reshape(step * frames, -1)
        average = jnp.mean(floated, axis=-1, keepdims=True)
        centered = floated - average
        variance = jnp.mean(centered * centered, axis=-1, keepdims=True)
        normed = centered * lax.rsqrt(variance + 1e-06)
        modulated[t * frames : (t + step) * frames] = (normed * gain_row + shift_row).astype(jnp.bfloat16)

    def block(j):
        blocks[j].wait()
        return jnp.dot(modulated[...], w_buf[j], preferred_element_type=jnp.float32)

    def normed_heads(columns, gains):
        squares = jnp.sum(columns * columns, axis=-1, keepdims=True)
        factor = lax.rsqrt(squares * (1.0 / inner) + 1e-06)
        gains_row = gains[...][None, :]
        for h in range(heads):
            at = slice(h * HEAD_DIM, (h + 1) * HEAD_DIM)
            yield h, (columns[:, at] * factor * gains_row[:, at]).astype(jnp.bfloat16)

    for h, part in normed_heads(block(keys), k_gain):
        kv_here[h, 0] = part
    columns = block(values)
    for h in range(heads):
        kv_here[h, 1] = columns[:, h * HEAD_DIM : (h + 1) * HEAD_DIM].astype(jnp.bfloat16)
    for h, part in normed_heads(block(queries), q_gain):
        q_here[h] = part
    for i in range(q_send.shape[0]):
        q_send[i] = q_here[meta[ORDER_V + i]]


def pack_kernel(meta, kv_here, k_send, v_send):
    for i in range(k_send.shape[0]):
        k_send[i] = kv_here[meta[ORDER_H + i], 0]
        v_send[i] = kv_here[meta[ORDER_H + i], 1]


def softmax_over(query, parts):
    factor = HEAD_DIM**-0.5 * LOG2E
    scores = []
    for pieces, bias in parts:
        keys = jnp.concatenate([key() for key, _ in pieces], axis=0)
        part = lax.dot_general(query, keys, (((1,), (1,)), ((), ())), preferred_element_type=jnp.float32)
        scores.append(part + bias[...])
    peak = functools.reduce(jnp.maximum, [jnp.max(part, axis=1, keepdims=True) for part in scores])
    total, summed = 0.0, 0.0
    for part, (pieces, _) in zip(scores, parts):
        values = jnp.concatenate([value() for _, value in pieces], axis=0)
        weights = jnp.exp2((part - peak) * factor)
        total = total + jnp.sum(weights, axis=1, keepdims=True)
        summed = summed + jnp.dot(weights.astype(jnp.bfloat16), values, preferred_element_type=jnp.float32)
    return summed / total, peak * factor + jnp.log2(total)


def own_pieces(kv_refs, head):
    return [(lambda ref=ref: ref[head, 0], lambda ref=ref: ref[head, 1]) for ref in kv_refs]


def near_pieces(refs, slot):
    return [(lambda k=k: k[slot], lambda v=v: v[slot]) for k, v in refs]


def own_tile_kernel(
    heads, place, lists, valid, q_here, kv_own, kv_own2, o_own, lse_own, bias_own, bias_near
):
    rows = q_here.shape[1]
    frame_total, listed = lists.shape
    frames = frame_total // 2
    here = place[0]
    key_at = lax.broadcasted_iota(jnp.int32, (1, 4 * rows), 1)
    query_at = lax.broadcasted_iota(jnp.int32, (rows, 1), 0)
    part = sum(jnp.where(key_at >= j * rows, 1, 0) for j in range(1, 4))
    frame_slot = (part & 1) * frames + lax.rem(key_at, frames)
    absent = jnp.where((part >= 2) & (place[1] == 0), NEG, 0.0)
    seen_rows = []
    for f in range(frames):
        row = jnp.full((1, 4 * rows), NEG, jnp.float32)
        for s in range(frame_total):
            frame = (here * frames + s) % frame_total
            query_frame = here * frames + f
            seen = jnp.where(lists[query_frame, 0] == frame, 1, 0)
            for k in range(1, listed):
                seen = seen | jnp.where(lists[query_frame, k] == frame, 1, 0)
            seen = seen & jnp.where(valid[frame] == 1, 1, 0)
            row = jnp.where((frame_slot == s) & (seen == 1), 0.0, row)
        seen_rows.append(row)
    query_frame = lax.rem(query_at, frames)

    def spread(picked):
        full = jnp.broadcast_to(picked[0], (rows, picked[0].shape[1]))
        for f in range(1, frames):
            full = jnp.where(query_frame == f, picked[f], full)
        return full

    bias_own[...] = spread([row[:, : 2 * rows] for row in seen_rows])
    bias_near[...] = spread([jnp.minimum(row, absent) for row in seen_rows])
    lane = lax.broadcasted_iota(jnp.int32, lse_own.shape, 1)
    lse_own[...] = jnp.zeros_like(lse_own)

    @pl.loop(0, heads)
    def _(h):
        out, lse = softmax_over(q_here[h], [(own_pieces((kv_own, kv_own2), h), bias_own)])
        o_own[h] = out
        lse_own[...] = jnp.where(lane == h, lse, lse_own[...])


def attend_kernel(
    meta, q_here, q_visit, kv_own, kv_own2, k_pair, v_pair, k_pair2, v_pair2, k_far, v_far, k_far2, v_far2,
    bias_own, bias_near, o_near, lse_near, o_visit, lse_visit, stats,
):
    directions, _, rows, _ = q_visit.shape
    lane = lax.broadcasted_iota(jnp.int32, (rows, stats.shape[1]), 1)
    stats[...] = jnp.zeros_like(stats)
    sent = k_pair.shape[0]

    def near(slot):
        refs = ((k_pair, v_pair), (k_pair2, v_pair2), (k_far, v_far), (k_far2, v_far2))
        return near_pieces(refs, slot), bias_near

    def own(head):
        return own_pieces((kv_own, kv_own2), head), bias_own

    def keep(lane_at, lse):
        stats[0:rows] = jnp.where(lane == lane_at, lse, stats[0:rows])

    for i in range(sent):
        out, lse = softmax_over(q_here[meta[ORDER_H + i]], [near(i)])
        o_near[i] = out
        keep(i, lse)

    for d in range(directions):
        @pl.loop(0, meta[N_BOTH])
        def _(i, d=d):
            head = meta[ORDER_V + i]
            out, lse = softmax_over(q_visit[d, i], [near(meta[SLOT_H + head]), own(head)])
            o_visit[d, i] = out.astype(o_visit.dtype)
            keep(16 + d * 8 + i, lse)

        @pl.loop(meta[N_BOTH], meta[N_V])
        def _(i, d=d):
            out, lse = softmax_over(q_visit[d, i], [own(meta[ORDER_V + i])])
            o_visit[d, i] = out.astype(o_visit.dtype)
            keep(16 + d * 8 + i, lse)

    lse_near[...] = stats[0:rows]
    turned = jnp.transpose(stats[...])
    for d in range(directions):
        lse_visit[d] = turned[16 + d * 8 : 24 + d * 8]


def merge(parts):
    peak = functools.reduce(jnp.maximum, [lse for lse, _ in parts])
    weights = [jnp.exp2(lse - peak) for lse, _ in parts]
    total = sum(weights[1:], weights[0])
    mixed = sum((w * o for w, (_, o) in zip(weights[1:], parts[1:])), weights[0] * parts[0][1])
    return mixed / total, peak + jnp.log2(total)


def pick_lane(table, at):
    lane = lax.broadcasted_iota(jnp.int32, table.shape, 1)
    return jnp.sum(jnp.where(lane == at, table, 0.0), axis=1, keepdims=True)


def row_kernel(heads, meta, o_own, lse_own, o_near, lse_near, o_row, lse_row):
    lane = lax.broadcasted_iota(jnp.int32, lse_row.shape, 1)
    own, near = lse_own[...], lse_near[...]
    merged = own
    for h in range(heads):
        slot = meta[SLOT_H + h]
        use = slot < meta[N_H]
        at = jnp.minimum(slot, o_near.shape[0] - 1)
        there = jnp.where(use, pick_lane(near, at), NEG)
        result, lse = merge([(own[:, h : h + 1], o_own[h]), (there, jnp.where(use, o_near[at], 0.0))])
        o_row[h] = result
        merged = jnp.where(lane == h, lse, merged)
    lse_row[...] = merged


def output_kernel(
    heads, meta, place, tokens, gate, w_out, o_row, lse_row, o_back, lse_back,
    out, attended, back, staged, sems,
):
    directions, slots, rows, _ = o_back.shape
    tile_tokens, frames, _ = tokens.shape
    back[...] = jnp.zeros_like(back)
    for d in range(directions):
        back[d * 8 : (d + 1) * 8] = lse_back[d]
    turned = jnp.transpose(back[...])[:rows]
    for h in range(heads):
        parts = [(lse_row[:, h : h + 1], o_row[h])]
        at = jnp.minimum(meta[SLOT_V + h], slots - 1)
        for d in range(directions):
            use = jnp.logical_and(meta[SLOT_V + h] < meta[N_V], place[2 + d] == 1)
            there = jnp.where(use, pick_lane(turned, d * 8 + at), NEG)
            parts.append((there, jnp.where(use, o_back[d, at].astype(jnp.float32), 0.0)))
        attended[:, h * HEAD_DIM : (h + 1) * HEAD_DIM] = merge(parts)[0].astype(jnp.bfloat16)
    width = out.shape[2] // sems.shape[0]
    copies = []
    for j in range(sems.shape[0]):
        at = slice(j * width, (j + 1) * width)
        branch = jnp.dot(attended[...], w_out[:, at], preferred_element_type=jnp.float32)
        branch = (branch * gate[at][None, :]).reshape(tile_tokens, frames, width)
        staged[:, :, at] = (tokens[:, :, at].astype(jnp.float32) + branch).astype(jnp.bfloat16)
        copies.append(pltpu.make_async_copy(staged.at[:, :, at], out.at[:, :, at], sems.at[j]))
        copies[-1].start()
    for copy in copies:
        copy.wait()


def per_device(
    tokens_in, mod_shift, mod_scale, mod_gate, w_qkv, q_gain, k_gain, w_out, windows, frame_lists, frame_valid
):
    frames, _, tile_tokens, feature_dim = tokens_in.shape
    inner = w_out.shape[0]
    heads = windows.shape[0]
    rows = frames * tile_tokens
    slots = heads - 1
    space_size = lax.axis_size("space")
    assert lax.axis_size("tm") == 2
    tile_cols = min(8, space_size // 2)
    tile_rows = space_size // tile_cols
    bf16, f32 = jnp.bfloat16, jnp.float32
    tokens = jnp.transpose(tokens_in[:, 0], (1, 0, 2))

    assert tile_cols % 2 == 0
    spots = range(space_size)
    col = lambda i: i % tile_cols
    pair = [(i, i ^ 1) for i in spots]
    inner_odd = [i for i in spots if col(i) % 2 and col(i) + 1 < tile_cols]
    far = [p for i in inner_odd for p in ((i, i + 1), (i + 1, i))]
    relay = [p for i in inner_odd for p in ((i - 1, i + 1), (i + 2, i))]
    down = [(i, i + tile_cols) for i in spots if i + tile_cols < space_size]
    up = [(j, i) for i, j in down]
    vertical = [down + up] if tile_rows == 2 else [down, up]
    directions = len(vertical)
    swap = [(0, 1), (1, 0)]

    position = lax.axis_index("space")
    tile_row = position // tile_cols
    tile_col = position % tile_cols
    has_partner = (
        [position >= 0] if tile_rows == 2 else [tile_row < tile_rows - 1, tile_row > 0]
    )
    place = jnp.stack(
        [lax.axis_index("tm"), (tile_col > 0) & (tile_col < tile_cols - 1), *has_partner]
    ).astype(jnp.int32)

    meta, q_here, q_send, kv_here = pl.pallas_call(
        functools.partial(project_kernel, heads),
        in_specs=[HBM] * 7,
        out_specs=[SMEM, VMEM, VMEM, VMEM],
        out_shape=[
            jax.ShapeDtypeStruct((META,), jnp.int32),
            jax.ShapeDtypeStruct((heads, rows, HEAD_DIM), bf16),
            jax.ShapeDtypeStruct((slots, rows, HEAD_DIM), bf16),
            jax.ShapeDtypeStruct((heads, 2, rows, HEAD_DIM), bf16),
        ],
        scratch_shapes=[
            pltpu.SMEM((2, heads), jnp.int32),
            pltpu.VMEM(tokens.shape, bf16),
            pltpu.VMEM(mod_shift.shape, f32),
            pltpu.VMEM(mod_scale.shape, f32),
            pltpu.VMEM(q_gain.shape, f32),
            pltpu.VMEM(k_gain.shape, f32),
            pltpu.VMEM((rows, feature_dim), bf16),
            pltpu.VMEM((3, feature_dim, inner), bf16),
            pltpu.SemaphoreType.DMA((6,)),
            pltpu.SemaphoreType.DMA((3,)),
        ],
        compiler_params=params(24),
        name="project",
    )(*[
        pltpu.with_memory_space_constraint(x, pltpu.HBM)
        for x in (windows.T, tokens, mod_shift, mod_scale, w_qkv, q_gain, k_gain)
    ])

    back = [[(j, i) for i, j in pairs] for pairs in vertical]
    lanes = 128
    stat_rows = 256

    def along_row(sent, *operands):
        return row_step(sent, *operands)

    def row_step(sent, kv_here, q_send, q_here, meta):
        k_send, v_send = pl.pallas_call(
            pack_kernel,
            in_specs=[SMEM, VMEM],
            out_specs=[VMEM, VMEM],
            out_shape=[jax.ShapeDtypeStruct((sent, rows, HEAD_DIM), bf16)] * 2,
            compiler_params=params(4),
            name="pack",
        )(meta, kv_here)
        kv_other = lax.ppermute(kv_here, "tm", swap)
        k_pair = lax.ppermute(k_send, "space", pair)
        q_visit = jnp.stack([lax.ppermute(q_send, "space", pairs) for pairs in vertical])
        v_far = lax.ppermute(v_send, "space", far)
        v_pair = lax.ppermute(v_send, "space", pair)
        k_far = lax.ppermute(k_pair, "space", relay)
        k_pair2, v_pair2, k_far2, v_far2 = [
            lax.ppermute(x, "tm", swap) for x in (k_pair, v_pair, k_far, v_far)
        ]
        o_own, lse_own, bias_own, bias_near = pl.pallas_call(
            functools.partial(own_tile_kernel, heads),
            in_specs=[SMEM] * 3 + [VMEM] * 3,
            out_specs=[VMEM] * 4,
            out_shape=[
                jax.ShapeDtypeStruct((heads, rows, HEAD_DIM), f32),
                jax.ShapeDtypeStruct((rows, lanes), f32),
                jax.ShapeDtypeStruct((rows, 2 * rows), f32),
                jax.ShapeDtypeStruct((rows, 4 * rows), f32),
            ],
            compiler_params=params(12),
            cost_estimate=pl.CostEstimate(
                flops=8 * heads * rows * rows * HEAD_DIM, bytes_accessed=6 << 20, transcendentals=2 * heads * rows * rows
            ),
            name="own_tile",
        )(place, frame_lists, frame_valid, q_here, kv_here, kv_other)
        o_near, lse_near, o_visit, lse_visit = pl.pallas_call(
            attend_kernel,
            in_specs=[SMEM] + [VMEM] * 14,
            out_specs=[VMEM] * 4,
            out_shape=[
                jax.ShapeDtypeStruct((sent, rows, HEAD_DIM), f32),
                jax.ShapeDtypeStruct((rows, lanes), f32),
                jax.ShapeDtypeStruct((directions, slots, rows, HEAD_DIM), bf16),
                jax.ShapeDtypeStruct((directions, 8, stat_rows), f32),
            ],
            scratch_shapes=[pltpu.VMEM((stat_rows, lanes), f32)],
            compiler_params=params(24),
            name="attend",
        )(meta, q_here, q_visit, kv_here, kv_other, k_pair, v_pair, k_pair2, v_pair2, k_far, v_far, k_far2, v_far2,
          bias_own, bias_near)
        o_near = jnp.pad(o_near, ((0, slots - sent), (0, 0), (0, 0)))
        return o_own, lse_own, o_near, lse_near, o_visit, lse_visit

    counts = jnp.sum(windows >= 3, axis=0)
    least = min(2, slots)

    def pick(count, branch, *operands):
        return lax.switch(
            count - least, [functools.partial(branch, n) for n in range(least, slots + 1)], *operands
        )

    o_own, lse_own, o_near, lse_near, o_visit, lse_visit = pick(
        counts[1], along_row, kv_here, q_send, q_here, meta
    )

    def between_rows(sent, *operands):
        return return_step(sent, *operands)

    def return_step(sent, o_own, lse_own, o_near, lse_near, o_visit, lse_visit, meta):
        o_back = jnp.stack([lax.ppermute(o_visit[d, :sent], "space", back[d]) for d in range(directions)])
        lse_back = jnp.stack([lax.ppermute(lse_visit[d], "space", back[d]) for d in range(directions)])
        o_row, lse_row = pl.pallas_call(
            functools.partial(row_kernel, heads),
            in_specs=[SMEM] + [VMEM] * 4,
            out_specs=[VMEM] * 2,
            out_shape=[
                jax.ShapeDtypeStruct((heads, rows, HEAD_DIM), f32),
                jax.ShapeDtypeStruct((rows, lanes), f32),
            ],
            compiler_params=params(8),
            cost_estimate=pl.CostEstimate(flops=1 << 22, bytes_accessed=2 << 20, transcendentals=1 << 14),
            name="row_merge",
        )(meta, o_own, lse_own, o_near, lse_near)
        return pl.pallas_call(
            functools.partial(output_kernel, heads),
            in_specs=[SMEM, SMEM] + [VMEM] * 7,
            out_specs=HBM,
            out_shape=pltpu.HBM(tokens.shape, bf16),
            scratch_shapes=[
                pltpu.VMEM((rows, inner), bf16),
                pltpu.VMEM((lanes, stat_rows), f32),
                pltpu.VMEM(tokens.shape, bf16),
                pltpu.SemaphoreType.DMA((3,)),
            ],
            compiler_params=params(16),
            name="output",
        )(meta, place, tokens, mod_gate, w_out, o_row, lse_row, o_back, lse_back)

    mixed = pick(counts[0], between_rows, o_own, lse_own, o_near, lse_near, o_visit, lse_visit, meta)
    return jnp.transpose(mixed, (1, 0, 2))[:, None]


def solution(mesh):
    in_specs = (
        P(("clips", "tm"), "space", None, None),
        P("clips"),
        P("clips"),
        P("clips"),
        P(),
        P(),
        P(),
        P(),
        P(),
        P("clips", None),
        P("clips"),
    )
    out_specs = P(("clips", "tm"), "space", None, None)
    return jax.shard_map(
        per_device, mesh=mesh, in_specs=in_specs, out_specs=out_specs, check_vma=False
    )
```

time: 74.9 us -> 55.4 us (0.74)
  waiting for transfers between devices: 34.2 us -> 11.8 us
  starting transfers between devices: 12.7 us -> 18.5 us
  local copies, waits for them, and re-layouts: 5.62 us -> 0.77 us
  Pallas kernels: 20.2 us -> 21.3 us
  other arithmetic: 0.08 us -> 0.9 us
    ppermute x6 -> x10, waiting for transfers between devices: 19.5 us -> 8.12 us  [the longest x1 4.74 us: row_step(): k_pair = lax.ppermute(k_send, 'space', pair)]
    ppermute x1, waiting for transfers between devices: 14.8 us -> 3.67 us  [row_step(): lax.ppermute(q_send, 'space', pairs)]
    ppermute x6 -> x10, starting transfers between devices: 10.1 us -> 15.3 us  [the longest x1 7.94 us: row_step(): k_far = lax.ppermute(k_pair, 'space', relay)]
    cond x14 -> x0, local copies, waits for them, and re-layouts: 2.91 us -> none
    slice x2 -> x1, local copies, waits for them, and re-layouts: 1.77 us -> 0.67 us  [per_device(): counts[1]]
    pallas_call x3 -> x6, Pallas kernels: 20.2 us -> 21.3 us  [the longest x1 6.58 us: per_device(): pl.pallas_call(functools.partial(project_kernel, heads), in_specs=[HBM] *...]
    squeeze x1, local copies, waits for them, and re-layouts: 0.91 us -> 0.01 us  [return_step(): o_visit[d, :sent]]
    reduce_sum x0 -> x1, other arithmetic: none -> 0.82 us  [per_device(): counts = jnp.sum(windows >= 3, axis=0)]
  transfers between devices with their start and end apart: 8 -> 12, of which waited for: 4 -> 4; matrix products, arithmetic and copies ran while one was open for 0% -> 0% of each run, Pallas kernels for 0% -> 12%
where the time goes in v3:
time: 55.4 us; the launch traced here: 55.2 us
  Pallas kernels  21.3 us (38%)
  starting transfers between devices  18.5 us (33%)
  waiting for transfers between devices  11.8 us (21%)
  between operations  1.59 us (3%)
  other arithmetic  0.9 us (2%)
  local copies, waits for them, and re-layouts  0.77 us (1%)
    ppermute x1, starting transfers between devices, row_step(): k_far = lax.ppermute(k_pair, 'space', relay)  7.94 us
    pallas_call x1, Pallas kernels, per_device(): pl.pallas_call(functools.partial(project_kernel, heads), in_specs=[HBM] *...  6.58 us
    ppermute x1, waiting for transfers between devices, row_step(): k_pair = lax.ppermute(k_send, 'space', pair)  4.74 us
    pallas_call x1, Pallas kernels, row_step(): pl.pallas_call(attend_kernel, in_specs=[SMEM] + [VMEM] * 14, out_specs=[V...  4.03 us
    pallas_call x1, Pallas kernels, row_step(): pl.pallas_call(functools.partial(own_tile_kernel, heads), in_specs=[SMEM]...  3.99 us
    pallas_call x1, Pallas kernels, return_step(): pl.pallas_call(functools.partial(output_kernel, heads), in_specs=[SMEM, S...  3.91 us
    ppermute x1, waiting for transfers between devices, row_step(): lax.ppermute(q_send, 'space', pairs)  3.67 us
    ppermute x1, waiting for transfers between devices, return_step(): lax.ppermute(lse_visit[d], 'space', back[d])  3.31 us
  transfers between devices with their start and end apart: 12, of which 4 were waited for; matrix products, arithmetic and copies ran while one was open for 0% of the time, Pallas kernels for 12%

profile of v3, /device:TPU:0, one launch (start us, length us, event | category | flops | bytes accessed | tf_op | source)
XLA Modules:
  0.0 55.2 jit_solution(6275392633426565225)
XLA Ops:
  0.0 0.0 copy-start.2
  0.0 0.0 copy-start.3
  0.0 0.8 %fusion = s32[2]{0:T(128)S(1)} fusion(s32[6,2]{0,1:T(2,128)} %param.27), kind=kLoop, calls=%fused_computation.4 | loop fusion | flops 34 | bytes 56 | tf_op jit(solution)/shard_map/reduce_sum | solution.py:406
  0.8 0.7 %fusion.1 = (s32[1]{0:T(128)}, s32[1]{0:T(128)}) fusion(s32[2]{0:T(128)S(1)} %fusion), kind=kLoop, calls=%fused_computation.6 | loop fusion | bytes 16 | tf_op jit(solution)/shard_map/slice | solution.py:415
  2.1 6.6 %project.1 = (s32[40]{0:T(128)S(1)}, bf16[6,240,128]{2,1,0:T(8,128)(2,1)S(1)}, bf16[5,240,128]{2,1,0:T(8,128)(2,1)}, bf16[6,2,240,128]{3,2,1,0:T(8,128)(2,1)S(1)}) custom-call(s32[2,6]{1,0:T(2,128)} %bitcast.53, bf16[60,4,1536]{2,1,0:T(4,128)(2,1)} %bitcast.47, f32[1536]{0:T(1024)} %shift_at.1, f32[1536]{0:T(1024)} %scale_at.1, bf16[1536,2304]{1,0:T(8,128)(2,1)} %w_qkv.1, ...), custom_call_target="tpu_custom_call" | custom-call | tf_op jit(solution)/shard_map/project/pallas_call | solution.py:318
  9.5 0.1 pad_add_fusion
  9.5 0.0 copy-done.2
  9.5 0.0 copy-done.3
  9.5 0.0 copy-start
  9.5 0.0 copy-start.1
  9.6 33.0 %conditional.2 = (f32[6,240,128]{2,1,0:T(8,128)S(1)}, f32[240,128]{1,0:T(8,128)S(1)}, f32[5,240,128]{2,1,0:T(8,128)S(1)}, f32[240,128]{1,0:T(8,128)S(1)}, bf16[1...) conditional(s32[]{:T(128)} %bitcast.24, ...), branch_computations={%region_1.2_spmd, %region_2.3_spmd, %region_3.4_spmd, %region_4.5_... | conditional | flops 353894400 | bytes 20300224 | solution.py:410
  9.6 0.6 %collective-permute-start.10 = (bf16[6,2,240,128]{3,2,1,0:T(8,128)(2,1)S(1)}, bf16[6,2,240,128]{3,2,1,0:T(8,128)(2,1)S(1)}, u32[]{:S(2)}, u32[]{:S(2)}) collective-permute-start(bf16[6,2,240,128]{3,2,1,0:T(8,128)(2,1)S(1)} %get-tuple-element.175.kv_own.kv_here), channel_id=1, source_target_pairs={{0,1},{1,0},{2,3},{3,2},{4,5},{5,4},{6,7},{7,6},{8,9},{9,8},{10,11... | collective-permute-start | bytes 2211848 | tf_op jit(solution)/shard_map/cond/branch_1_fun/ppermute | solution.py:363
  10.1 0.6 %pack.5 = (bf16[3,240,128]{2,1,0:T(8,128)(2,1)S(1)}, bf16[3,240,128]{2,1,0:T(8,128)(2,1)S(1)}) custom-call(s32[40]{0:T(128)S(1)} %get-tuple-element.178.meta, bf16[6,2,240,128]{3,2,1,0:T(8,128)(2,1)S(1)} %get-tuple-element.175.kv_own.kv_here), custom_call_target="tpu_custom_call" | custom-call | tf_op jit(solution)/shard_map/cond/branch_1_fun/pack/pallas_call | solution.py:355
  10.7 2.6 %collective-permute-start.12 = (bf16[3,240,128]{2,1,0:T(8,128)(2,1)S(1)}, bf16[3,240,128]{2,1,0:T(8,128)(2,1)S(1)}, u32[]{:S(2)}, u32[]{:S(2)}) collective-permute-start(bf16[3,240,128]{2,1,0:T(8,128)(2,1)S(1)} %get-tuple-element.180), channel_id=1, source_target_pairs={{0,2},{2,0},{4,6},{6,4},{8,10},{10,8},{12,14},{14,12},{1,3},{3,1},... | collective-permute-start | bytes 552968 | tf_op jit(solution)/shard_map/cond/branch_1_fun/ppermute | solution.py:364
  13.3 0.1 collective-permute-start.13
  13.4 0.7 %collective-permute-start.17 = (bf16[3,240,128]{2,1,0:T(8,128)(2,1)S(1)}, bf16[3,240,128]{2,1,0:T(8,128)(2,1)S(1)}, u32[]{:S(2)}, u32[]{:S(2)}) collective-permute-start(bf16[3,240,128]{2,1,0:T(8,128)(2,1)S(1)} %get-tuple-element.181), channel_id=1, source_target_pairs={{2,4},{4,2},{10,12},{12,10},{3,5},{5,3},{11,13},{13,11},{18,20},{2... | collective-permute-start | bytes 552968 | tf_op jit(solution)/shard_map/cond/branch_1_fun/ppermute | solution.py:366
  14.0 4.7 %collective-permute-done.12.k_pair = bf16[3,240,128]{2,1,0:T(8,128)(2,1)S(1)} collective-permute-done((bf16[3,240,128]{2,1,0:T(8,128)(2,1)S(1)}, bf16[3,240,128]{2,1,0:T(8,128)(2,1)S(1)}, u32[]{:S(2)}, u32[]{:S(2)}) %collective-permute-start.12) | collective-permute-done | bytes 184352 | tf_op jit(solution)/shard_map/cond/branch_1_fun/ppermute | solution.py:364
  18.8 7.9 %collective-permute-start.16 = (bf16[3,240,128]{2,1,0:T(8,128)(2,1)S(1)}, bf16[3,240,128]{2,1,0:T(8,128)(2,1)S(1)}, u32[]{:S(2)}, u32[]{:S(2)}) collective-permute-start(bf16[3,240,128]{2,1,0:T(8,128)(2,1)S(1)} %collective-permute-done.12.k_pair), channel_id=1, source_target_pairs={{0,4},{6,2},{8,12},{14,10},{1,5},{7,3},{9,13},{15,11},{16,20},{22,... | collective-permute-start | bytes 552968 | tf_op jit(solution)/shard_map/cond/branch_1_fun/ppermute | solution.py:368
  26.7 2.7 %collective-permute-start.11 = (bf16[5,240,128]{2,1,0:T(8,128)(2,1)}, bf16[5,240,128]{2,1,0:T(8,128)(2,1)S(1)}, u32[]{:S(2)}, u32[]{:S(2)}) collective-permute-start(bf16[5,240,128]{2,1,0:T(8,128)(2,1)} %get-tuple-element.179), channel_id=1, source_target_pairs={{0,8},{2,10},{4,12},{6,14},{8,0},{10,2},{12,4},{14,6},{1,9},{3,11}... | collective-permute-start | bytes 921608 | tf_op jit(solution)/shard_map/cond/branch_1_fun/ppermute | solution.py:365
  29.4 0.0 collective-permute-done.13.v_pair
  29.4 0.0 collective-permute-start.14
  29.4 0.0 collective-permute-done.17.v_far
  29.4 0.5 collective-permute-start.15
  29.9 0.1 collective-permute-done.16.k_far
  30.0 0.0 collective-permute-start.19
  30.0 0.0 collective-permute-done.10.kv_own2
  30.0 0.5 collective-permute-start.18
  30.5 4.0 %own_tile.5 = (f32[6,240,128]{2,1,0:T(8,128)S(1)}, f32[240,128]{1,0:T(8,128)S(1)}, f32[240,480]{1,0:T(8,128)S(1)}, f32[240,960]{1,0:T(8,128)S(1)}) custom-call(s32[3]{0:T(128)S(1)} %get-tuple-element.171.place, s32[8,6]{1,0:T(8,128)S(1)} %get-tuple-element.172.lists, s32[8]{0:T(128)S(1)} %get-tuple-element.173.valid, ...), custom_call_target="tpu_custom_call" | custom-call | flops 353894400 | bytes 6291456 | tf_op jit(solution)/shard_map/cond/branch_1_fun/own_tile/pallas_call | solution.py:372
  34.5 3.7 %collective-permute-done.11 = bf16[5,240,128]{2,1,0:T(8,128)(2,1)S(1)} collective-permute-done((bf16[5,240,128]{2,1,0:T(8,128)(2,1)}, bf16[5,240,128]{2,1,0:T(8,128)(2,1)S(1)}, u32[]{:S(2)}, u32[]{:S(2)}) %collective-permute-start.11) | collective-permute-done | bytes 307232 | tf_op jit(solution)/shard_map/cond/branch_1_fun/ppermute | solution.py:365
  38.1 0.0 collective-permute-done.14.k_pair2
  38.1 0.0 collective-permute-done.15.v_pair2
  38.1 0.0 collective-permute-done.19.v_far2
  38.2 0.0 collective-permute-done.18.k_far2
  38.2 4.0 %attend.5 = (f32[3,240,128]{2,1,0:T(8,128)S(1)}, f32[240,128]{1,0:T(8,128)S(1)}, bf16[1,5,240,128]{3,2,1,0:T(8,128)(2,1)S(1)}, f32[1,8,256]{2,1,0:T(8,128)S(1)}) custom-call(s32[40]{0:T(128)S(1)} %get-tuple-element.178.meta, bf16[6,240,128]{2,1,0:T(8,128)(2,1)S(1)} %get-tuple-element.174.q_here, bf16[1,5,240,128]{3,2,1,0:T(8,128)(2,1)S(1)} %bitcast.37, ...), custom_call_target="tpu_custom_call" | custom-call | tf_op jit(solution)/shard_map/cond/branch_1_fun/attend/pallas_call | solution.py:388
  42.2 0.1 pad.10
  42.5 0.0 copy-done
  42.5 0.0 copy-done.1
  42.5 12.5 %conditional.3 = (bf16[60,4,1536]{2,1,0:T(4,128)(2,1)}) conditional(s32[]{:T(128)} %bitcast.20, (s32[40]{0:T(128)S(1)}, f32[6,240,128]{2,1,0:T(8,128)S(1)}, f32[240,128]{1,0:T(8,128)S(1)}, f32[5,240,128]{2,1,0:T(8,128)S(1)}, f32[240,128]{1,0:T(8,128)S(1)}, /*index=5*/bf16[1,5,240,128]{3,2,1,0:T(8,128)(2,1)S(1)}, ...), branch_computations={%region_5.6_spmd, %region_6.7_spmd, %region_7.8_spmd, %region_8.9_... | conditional | flops 4194304 | bytes 3604568 | solution.py:410
  42.6 1.5 %collective-permute-start.42 = (bf16[2,240,128]{2,1,0:T(8,128)(2,1)S(1)}, bf16[2,240,128]{2,1,0:T(8,128)(2,1)S(1)}, u32[]{:S(2)}, u32[]{:S(2)}) collective-permute-start(bf16[2,240,128]{2,1,0:T(8,128)(2,1)S(1)} %slice_bitcast_fusion), channel_id=1, source_target_pairs={{8,0},{10,2},{12,4},{14,6},{0,8},{2,10},{4,12},{6,14},{9,1},{11,3}... | collective-permute-start | bytes 368648 | tf_op jit(solution)/shard_map/cond/branch_0_fun/ppermute | solution.py:422
  44.0 1.5 %collective-permute-start.43 = (f32[8,256]{1,0:T(8,128)S(1)}, f32[8,256]{1,0:T(8,128)S(1)}, u32[]{:S(2)}, u32[]{:S(2)}) collective-permute-start(f32[8,256]{1,0:T(8,128)S(1)} %bitcast.54), channel_id=1, source_target_pairs={{8,0},{10,2},{12,4},{14,6},{0,8},{2,10},{4,12},{6,14},{9,1},{11,3}... | collective-permute-start | bytes 24584 | tf_op jit(solution)/shard_map/cond/branch_0_fun/ppermute | solution.py:423
  45.6 2.2 %row_merge.4 = (f32[6,240,128]{2,1,0:T(8,128)S(1)}, f32[240,128]{1,0:T(8,128)S(1)}) custom-call(s32[40]{0:T(128)S(1)} %get-tuple-element.222.meta, f32[6,240,128]{2,1,0:T(8,128)S(1)} %get-tuple-element.227.o_own, f32[240,128]{1,0:T(8,128)S(1)} %get-tuple-element.228.lse_own, f32[5,240,128]{2,1,0:T(8,128)S(1)} %get-tuple-element.229.o_near, ...), custom_call_target="tpu_custom_call" | custom-call | flops 4194304 | bytes 2097152 | tf_op jit(solution)/shard_map/cond/branch_0_fun/row_merge/pallas_call | solution.py:424
  47.8 3.3 %collective-permute-done.43 = f32[8,256]{1,0:T(8,128)S(1)} collective-permute-done((f32[8,256]{1,0:T(8,128)S(1)}, f32[8,256]{1,0:T(8,128)S(1)}, u32[]{:S(2)}, u32[]{:S(2)}) %collective-permute-start.43) | collective-permute-done | bytes 8224 | tf_op jit(solution)/shard_map/cond/branch_0_fun/ppermute | solution.py:423
  51.1 0.0 collective-permute-done.42
  51.1 3.9 %output.4 = bf16[60,4,1536]{2,1,0:T(4,128)(2,1)} custom-call(s32[40]{0:T(128)S(1)} %get-tuple-element.222.meta, s32[3]{0:T(128)S(1)} %get-tuple-element.223.place, bf16[60,4,1536]{2,1,0:T(4,128)(2,1)} %get-tuple-element.224.tokens, f32[1536]{0:T(1024)S(1)} %get-tuple-element.225.gate, bf16[768,1536]{1,0:T(8,128)(2,1)S(1)} %get-tuple-element.226.w_out, ...), custom_call_target="tpu_custom_call" | custom-call | tf_op jit(solution)/shard_map/cond/branch_0_fun/output/pallas_call | solution.py:436
  (1 shorter events, 0.0 us)
Async XLA Ops:
  0.0 9.5 %copy-start.2 = (s32[8,6]{1,0:T(8,128)S(1)}, s32[8,6]{1,0:T(8,128)}, u32[]{:S(2)}) copy-start(s32[8,6]{1,0:T(8,128)} %param.28) | copy-start | bytes 580
  0.0 9.5 %copy-start.3 = (s32[8]{0:T(128)S(1)}, s32[8]{0:T(128)}, u32[]{:S(2)}) copy-start(s32[8]{0:T(128)} %param.29) | copy-start | bytes 100
  9.5 33.0 %copy-start = (bf16[768,1536]{1,0:T(8,128)(2,1)S(1)}, bf16[768,1536]{1,0:T(8,128)(2,1)}, u32[]{:S(2)}) copy-start(bf16[768,1536]{1,0:T(8,128)(2,1)} %param.26) | copy-start | bytes 7077892
  9.5 33.0 %copy-start.1 = (f32[1536]{0:T(1024)S(1)}, f32[1536]{0:T(1024)}, u32[]{:S(2)}) copy-start(f32[1536]{0:T(1024)} %param.22) | copy-start | bytes 18436
  9.6 20.4 %collective-permute-start.10 = (bf16[6,2,240,128]{3,2,1,0:T(8,128)(2,1)S(1)}, bf16[6,2,240,128]{3,2,1,0:T(8,128)(2,1)S(1)}, u32[]{:S(2)}, u32[]{:S(2)}) collective-permute-start(bf16[6,2,240,128]{3,2,1,0:T(8,128)(2,1)S(1)} %get-tuple-element.175.kv_own.kv_here), channel_id=1, source_target_pairs={{0,1},{1,0},{2,3},{3,2},{4,5},{5,4},{6,7},{7,6},{8,9},{9,8},{10,11... | collective-permute-start | bytes 2211848 | tf_op jit(solution)/shard_map/cond/branch_1_fun/ppermute | solution.py:363
  10.7 8.1 %collective-permute-start.12 = (bf16[3,240,128]{2,1,0:T(8,128)(2,1)S(1)}, bf16[3,240,128]{2,1,0:T(8,128)(2,1)S(1)}, u32[]{:S(2)}, u32[]{:S(2)}) collective-permute-start(bf16[3,240,128]{2,1,0:T(8,128)(2,1)S(1)} %get-tuple-element.180), channel_id=1, source_target_pairs={{0,2},{2,0},{4,6},{6,4},{8,10},{10,8},{12,14},{14,12},{1,3},{3,1},... | collective-permute-start | bytes 552968 | tf_op jit(solution)/shard_map/cond/branch_1_fun/ppermute | solution.py:364
  13.3 16.1 %collective-permute-start.13 = (bf16[3,240,128]{2,1,0:T(8,128)(2,1)S(1)}, bf16[3,240,128]{2,1,0:T(8,128)(2,1)S(1)}, u32[]{:S(2)}, u32[]{:S(2)}) collective-permute-start(bf16[3,240,128]{2,1,0:T(8,128)(2,1)S(1)} %get-tuple-element.181), channel_id=1, source_target_pairs={{0,2},{2,0},{4,6},{6,4},{8,10},{10,8},{12,14},{14,12},{1,3},{3,1},... | collective-permute-start | bytes 552968 | tf_op jit(solution)/shard_map/cond/branch_1_fun/ppermute | solution.py:367
  13.4 16.0 %collective-permute-start.17 = (bf16[3,240,128]{2,1,0:T(8,128)(2,1)S(1)}, bf16[3,240,128]{2,1,0:T(8,128)(2,1)S(1)}, u32[]{:S(2)}, u32[]{:S(2)}) collective-permute-start(bf16[3,240,128]{2,1,0:T(8,128)(2,1)S(1)} %get-tuple-element.181), channel_id=1, source_target_pairs={{2,4},{4,2},{10,12},{12,10},{3,5},{5,3},{11,13},{13,11},{18,20},{2... | collective-permute-start | bytes 552968 | tf_op jit(solution)/shard_map/cond/branch_1_fun/ppermute | solution.py:366
  18.8 11.2 %collective-permute-start.16 = (bf16[3,240,128]{2,1,0:T(8,128)(2,1)S(1)}, bf16[3,240,128]{2,1,0:T(8,128)(2,1)S(1)}, u32[]{:S(2)}, u32[]{:S(2)}) collective-permute-start(bf16[3,240,128]{2,1,0:T(8,128)(2,1)S(1)} %collective-permute-done.12.k_pair), channel_id=1, source_target_pairs={{0,4},{6,2},{8,12},{14,10},{1,5},{7,3},{9,13},{15,11},{16,20},{22,... | collective-permute-start | bytes 552968 | tf_op jit(solution)/shard_map/cond/branch_1_fun/ppermute | solution.py:368
  26.7 11.4 %collective-permute-start.11 = (bf16[5,240,128]{2,1,0:T(8,128)(2,1)}, bf16[5,240,128]{2,1,0:T(8,128)(2,1)S(1)}, u32[]{:S(2)}, u32[]{:S(2)}) collective-permute-start(bf16[5,240,128]{2,1,0:T(8,128)(2,1)} %get-tuple-element.179), channel_id=1, source_target_pairs={{0,8},{2,10},{4,12},{6,14},{8,0},{10,2},{12,4},{14,6},{1,9},{3,11}... | collective-permute-start | bytes 921608 | tf_op jit(solution)/shard_map/cond/branch_1_fun/ppermute | solution.py:365
  29.4 8.8 %collective-permute-start.14 = (bf16[3,240,128]{2,1,0:T(8,128)(2,1)S(1)}, bf16[3,240,128]{2,1,0:T(8,128)(2,1)S(1)}, u32[]{:S(2)}, u32[]{:S(2)}) collective-permute-start(bf16[3,240,128]{2,1,0:T(8,128)(2,1)S(1)} %collective-permute-done.12.k_pair), channel_id=1, source_target_pairs={{0,1},{1,0},{2,3},{3,2},{4,5},{5,4},{6,7},{7,6},{8,9},{9,8},{10,11... | collective-permute-start | bytes 552968 | tf_op jit(solution)/shard_map/cond/branch_1_fun/ppermute | solution.py:370
  29.4 8.7 %collective-permute-start.15 = (bf16[3,240,128]{2,1,0:T(8,128)(2,1)S(1)}, bf16[3,240,128]{2,1,0:T(8,128)(2,1)S(1)}, u32[]{:S(2)}, u32[]{:S(2)}) collective-permute-start(bf16[3,240,128]{2,1,0:T(8,128)(2,1)S(1)} %collective-permute-done.13.v_pair), channel_id=1, source_target_pairs={{0,1},{1,0},{2,3},{3,2},{4,5},{5,4},{6,7},{7,6},{8,9},{9,8},{10,11... | collective-permute-start | bytes 552968 | tf_op jit(solution)/shard_map/cond/branch_1_fun/ppermute | solution.py:370
  30.0 8.2 %collective-permute-start.19 = (bf16[3,240,128]{2,1,0:T(8,128)(2,1)S(1)}, bf16[3,240,128]{2,1,0:T(8,128)(2,1)S(1)}, u32[]{:S(2)}, u32[]{:S(2)}) collective-permute-start(bf16[3,240,128]{2,1,0:T(8,128)(2,1)S(1)} %collective-permute-done.17.v_far), channel_id=1, source_target_pairs={{0,1},{1,0},{2,3},{3,2},{4,5},{5,4},{6,7},{7,6},{8,9},{9,8},{10,11... | collective-permute-start | bytes 552968 | tf_op jit(solution)/shard_map/cond/branch_1_fun/ppermute | solution.py:370
  30.0 8.2 %collective-permute-start.18 = (bf16[3,240,128]{2,1,0:T(8,128)(2,1)S(1)}, bf16[3,240,128]{2,1,0:T(8,128)(2,1)S(1)}, u32[]{:S(2)}, u32[]{:S(2)}) collective-permute-start(bf16[3,240,128]{2,1,0:T(8,128)(2,1)S(1)} %collective-permute-done.16.k_far), channel_id=1, source_target_pairs={{0,1},{1,0},{2,3},{3,2},{4,5},{5,4},{6,7},{7,6},{8,9},{9,8},{10,11... | collective-permute-start | bytes 552968 | tf_op jit(solution)/shard_map/cond/branch_1_fun/ppermute | solution.py:370
  42.6 8.5 %collective-permute-start.42 = (bf16[2,240,128]{2,1,0:T(8,128)(2,1)S(1)}, bf16[2,240,128]{2,1,0:T(8,128)(2,1)S(1)}, u32[]{:S(2)}, u32[]{:S(2)}) collective-permute-start(bf16[2,240,128]{2,1,0:T(8,128)(2,1)S(1)} %slice_bitcast_fusion), channel_id=1, source_target_pairs={{8,0},{10,2},{12,4},{14,6},{0,8},{2,10},{4,12},{6,14},{9,1},{11,3}... | collective-permute-start | bytes 368648 | tf_op jit(solution)/shard_map/cond/branch_0_fun/ppermute | solution.py:422
  44.0 7.1 %collective-permute-start.43 = (f32[8,256]{1,0:T(8,128)S(1)}, f32[8,256]{1,0:T(8,128)S(1)}, u32[]{:S(2)}, u32[]{:S(2)}) collective-permute-start(f32[8,256]{1,0:T(8,128)S(1)} %bitcast.54), channel_id=1, source_target_pairs={{8,0},{10,2},{12,4},{14,6},{0,8},{2,10},{4,12},{6,14},{9,1},{11,3}... | collective-permute-start | bytes 24584 | tf_op jit(solution)/shard_map/cond/branch_0_fun/ppermute | solution.py:423

commit v4 on v3

--- a/solution.py
+++ b/solution.py
@@ -42,8 +42,8 @@
 
 
 def project_kernel(
-    heads, windows_at, tokens_at, shift_at, scale_at, w_qkv, q_gain_at, k_gain_at,
-    meta, q_here, q_send, kv_here,
+    heads, least, windows_at, tokens_at, shift_at, scale_at, w_qkv, q_gain_at, k_gain_at,
+    meta, wide_branch, tall_branch, q_here, q_send, kv_here,
     windows, tokens, shift, scale, q_gain, k_gain, modulated, w_buf, small_sems, sems,
 ):
     tile_tokens, frames, _ = tokens.shape
@@ -60,15 +60,19 @@
         j: pltpu.make_async_copy(w_qkv.at[:, pl.ds(j * inner, inner)], w_buf.at[j], sems.at[j])
         for j in (keys, values, queries)
     }
-    for copy in (*small, *blocks.values()):
+    for copy in (*small, blocks[keys]):
         copy.start()
     for copy in small:
         copy.wait()
     rank_heads(windows, meta, heads)
+    wide_branch[0] = jnp.clip(meta[N_H] - least, 0, heads - 1 - least)
+    tall_branch[0] = jnp.clip(meta[N_V] - least, 0, heads - 1 - least)
     gain_row = 1.0 + scale[...][None, :]
     shift_row = shift[...][None, :]
     step = 4
     for t in range(0, tile_tokens, step):
+        if t == tile_tokens // 2 // step * step:
+            blocks[values].start()
         floated = tokens[t : t + step].astype(jnp.float32).reshape(step * frames, -1)
         average = jnp.mean(floated, axis=-1, keepdims=True)
         centered = floated - average
@@ -88,7 +92,9 @@
             at = slice(h * HEAD_DIM, (h + 1) * HEAD_DIM)
             yield h, (columns[:, at] * factor * gains_row[:, at]).astype(jnp.bfloat16)
 
-    for h, part in normed_heads(block(keys), k_gain):
+    columns = block(keys)
+    blocks[queries].start()
+    for h, part in normed_heads(columns, k_gain):
         kv_here[h, 0] = part
     columns = block(values)
     for h in range(heads):
@@ -131,17 +137,19 @@
 
 
 def own_tile_kernel(
-    heads, place, lists, valid, q_here, kv_own, kv_own2, o_own, lse_own, bias_own, bias_near
+    heads, tile_cols, lists, valid, q_here, kv_own, kv_own2, o_own, lse_own, bias_own, bias_near
 ):
     rows = q_here.shape[1]
     frame_total, listed = lists.shape
     frames = frame_total // 2
-    here = place[0]
+    here = lax.axis_index("tm")
+    tile_col = lax.rem(lax.axis_index("space"), tile_cols)
+    has_far = (tile_col > 0) & (tile_col < tile_cols - 1)
     key_at = lax.broadcasted_iota(jnp.int32, (1, 4 * rows), 1)
     query_at = lax.broadcasted_iota(jnp.int32, (rows, 1), 0)
     part = sum(jnp.where(key_at >= j * rows, 1, 0) for j in range(1, 4))
     frame_slot = (part & 1) * frames + lax.rem(key_at, frames)
-    absent = jnp.where((part >= 2) & (place[1] == 0), NEG, 0.0)
+    absent = jnp.where((part >= 2) & jnp.logical_not(has_far), NEG, 0.0)
     seen_rows = []
     for f in range(frames):
         row = jnp.full((1, 4 * rows), NEG, jnp.float32)
@@ -247,7 +255,7 @@
 
 
 def output_kernel(
-    heads, meta, place, tokens, gate, w_out, o_row, lse_row, o_back, lse_back,
+    heads, tile_cols, tile_rows, meta, tokens, gate, w_out, o_row, lse_row, o_back, lse_back,
     out, attended, back, staged, sems,
 ):
     directions, slots, rows, _ = o_back.shape
@@ -256,11 +264,13 @@
     for d in range(directions):
         back[d * 8 : (d + 1) * 8] = lse_back[d]
     turned = jnp.transpose(back[...])[:rows]
+    tile_row = lax.axis_index("space") // tile_cols
+    exists = [True] if tile_rows == 2 else [tile_row < tile_rows - 1, tile_row > 0]
     for h in range(heads):
         parts = [(lse_row[:, h : h + 1], o_row[h])]
         at = jnp.minimum(meta[SLOT_V + h], slots - 1)
         for d in range(directions):
-            use = jnp.logical_and(meta[SLOT_V + h] < meta[N_V], place[2 + d] == 1)
+            use = jnp.logical_and(meta[SLOT_V + h] < meta[N_V], exists[d])
             there = jnp.where(use, pick_lane(turned, d * 8 + at), NEG)
             parts.append((there, jnp.where(use, o_back[d, at].astype(jnp.float32), 0.0)))
         attended[:, h * HEAD_DIM : (h + 1) * HEAD_DIM] = merge(parts)[0].astype(jnp.bfloat16)
@@ -277,6 +287,17 @@
         copy.wait()
 
 
+def branch_on(number, branches, *operands):
+    traced = jax.make_jaxpr(lambda *args: lax.switch(args[0], branches, *args[1:]))(number, *operands)
+    values = dict(zip(traced.jaxpr.constvars, traced.consts))
+    values.update(zip(traced.jaxpr.invars, (number, *operands)))
+    (choice,) = [eqn for eqn in traced.jaxpr.eqns if eqn.primitive.name == "cond"]
+    outs = choice.primitive.bind(number, *[values[v] for v in choice.invars[1:]], **choice.params)
+    values.update(zip(choice.outvars, outs))
+    outs = [values[v] for v in traced.jaxpr.outvars]
+    return outs[0] if len(outs) == 1 else outs
+
+
 def per_device(
     tokens_in, mod_shift, mod_scale, mod_gate, w_qkv, q_gain, k_gain, w_out, windows, frame_lists, frame_valid
 ):
@@ -305,22 +326,15 @@
     directions = len(vertical)
     swap = [(0, 1), (1, 0)]
 
-    position = lax.axis_index("space")
-    tile_row = position // tile_cols
-    tile_col = position % tile_cols
-    has_partner = (
-        [position >= 0] if tile_rows == 2 else [tile_row < tile_rows - 1, tile_row > 0]
-    )
-    place = jnp.stack(
-        [lax.axis_index("tm"), (tile_col > 0) & (tile_col < tile_cols - 1), *has_partner]
-    ).astype(jnp.int32)
-
-    meta, q_here, q_send, kv_here = pl.pallas_call(
-        functools.partial(project_kernel, heads),
+    least = min(2, slots)
+    meta, wide_branch, tall_branch, q_here, q_send, kv_here = pl.pallas_call(
+        functools.partial(project_kernel, heads, least),
         in_specs=[HBM] * 7,
-        out_specs=[SMEM, VMEM, VMEM, VMEM],
+        out_specs=[SMEM, SMEM, SMEM, VMEM, VMEM, VMEM],
         out_shape=[
             jax.ShapeDtypeStruct((META,), jnp.int32),
+            jax.ShapeDtypeStruct((1,), jnp.int32),
+            jax.ShapeDtypeStruct((1,), jnp.int32),
             jax.ShapeDtypeStruct((heads, rows, HEAD_DIM), bf16),
             jax.ShapeDtypeStruct((slots, rows, HEAD_DIM), bf16),
             jax.ShapeDtypeStruct((heads, 2, rows, HEAD_DIM), bf16),
@@ -370,8 +384,8 @@
             lax.ppermute(x, "tm", swap) for x in (k_pair, v_pair, k_far, v_far)
         ]
         o_own, lse_own, bias_own, bias_near = pl.pallas_call(
-            functools.partial(own_tile_kernel, heads),
-            in_specs=[SMEM] * 3 + [VMEM] * 3,
+            functools.partial(own_tile_kernel, heads, tile_cols),
+            in_specs=[SMEM] * 2 + [VMEM] * 3,
             out_specs=[VMEM] * 4,
             out_shape=[
                 jax.ShapeDtypeStruct((heads, rows, HEAD_DIM), f32),
@@ -384,7 +398,7 @@
                 flops=8 * heads * rows * rows * HEAD_DIM, bytes_accessed=6 << 20, transcendentals=2 * heads * rows * rows
             ),
             name="own_tile",
-        )(place, frame_lists, frame_valid, q_here, kv_here, kv_other)
+        )(frame_lists, frame_valid, q_here, kv_here, kv_other)
         o_near, lse_near, o_visit, lse_visit = pl.pallas_call(
             attend_kernel,
             in_specs=[SMEM] + [VMEM] * 14,
@@ -403,16 +417,13 @@
         o_near = jnp.pad(o_near, ((0, slots - sent), (0, 0), (0, 0)))
         return o_own, lse_own, o_near, lse_near, o_visit, lse_visit
 
-    counts = jnp.sum(windows >= 3, axis=0)
-    least = min(2, slots)
-
-    def pick(count, branch, *operands):
-        return lax.switch(
-            count - least, [functools.partial(branch, n) for n in range(least, slots + 1)], *operands
+    def pick(number, branch, *operands):
+        return branch_on(
+            number.reshape(()), [functools.partial(branch, n) for n in range(least, slots + 1)], *operands
         )
 
     o_own, lse_own, o_near, lse_near, o_visit, lse_visit = pick(
-        counts[1], along_row, kv_here, q_send, q_here, meta
+        wide_branch, along_row, kv_here, q_send, q_here, meta
     )
 
     def between_rows(sent, *operands):
@@ -434,8 +445,8 @@
             name="row_merge",
         )(meta, o_own, lse_own, o_near, lse_near)
         return pl.pallas_call(
-            functools.partial(output_kernel, heads),
-            in_specs=[SMEM, SMEM] + [VMEM] * 7,
+            functools.partial(output_kernel, heads, tile_cols, tile_rows),
+            in_specs=[SMEM] + [VMEM] * 7,
             out_specs=HBM,
             out_shape=pltpu.HBM(tokens.shape, bf16),
             scratch_shapes=[
@@ -446,9 +457,9 @@
             ],
             compiler_params=params(16),
             name="output",
-        )(meta, place, tokens, mod_gate, w_out, o_row, lse_row, o_back, lse_back)
-
-    mixed = pick(counts[0], between_rows, o_own, lse_own, o_near, lse_near, o_visit, lse_visit, meta)
+        )(meta, tokens, mod_gate, w_out, o_row, lse_row, o_back, lse_back)
+
+    mixed = pick(tall_branch, between_rows, o_own, lse_own, o_near, lse_near, o_visit, lse_visit, meta)
     return jnp.transpose(mixed, (1, 0, 2))[:, None]
 
 

time: 55.4 us -> 52.2 us (0.942)
  Pallas kernels: 21.3 us -> 19.7 us
  loops' own time: 0.37 us -> 1.79 us
  between operations: 1.59 us -> 0.26 us
  other arithmetic: 0.9 us -> 0 us
  local copies, waits for them, and re-layouts: 0.77 us -> 0.11 us
    pallas_call x3, Pallas kernels: 14.5 us -> 12.8 us  [the longest x1 5.47 us: per_device(): pl.pallas_call(functools.partial(project_kernel, heads, least), in_specs=...]
    another operation x2, loops' own time: 0.37 us -> 1.79 us  [branch_on(): choice.primitive.bind(number, *[values[v] for v in choice.invars[1:]], **...]
    reduce_sum x1 -> x0, other arithmetic: 0.82 us -> none  [per_device(): counts = jnp.sum(windows >= 3, axis=0)]
    slice x1 -> x0, local copies, waits for them, and re-layouts: 0.67 us -> none  [per_device(): counts[1]]
  transfers between devices with their start and end apart: 12 -> 12, of which waited for: 4 -> 3; matrix products, arithmetic and copies ran while one was open for 0% -> 0% of each run, Pallas kernels for 12% -> 13%
where the time goes in v4:
time: 52.2 us; the launch traced here: 52 us
  Pallas kernels  19.7 us (38%)
  starting transfers between devices  18.5 us (35%)
  waiting for transfers between devices  11.6 us (22%)
  loops' own time  1.79 us (3%)
    ppermute x1, starting transfers between devices, row_step(): k_far = lax.ppermute(k_pair, 'space', relay)  7.96 us
    pallas_call x1, Pallas kernels, per_device(): pl.pallas_call(functools.partial(project_kernel, heads, least), in_specs=...  5.47 us
    ppermute x1, waiting for transfers between devices, row_step(): k_pair = lax.ppermute(k_send, 'space', pair)  4.74 us
    pallas_call x1, Pallas kernels, row_step(): pl.pallas_call(attend_kernel, in_specs=[SMEM] + [VMEM] * 14, out_specs=[V...  4.07 us
    pallas_call x1, Pallas kernels, row_step(): pl.pallas_call(functools.partial(own_tile_kernel, heads, tile_cols), in_s...  4.03 us
    ppermute x1, waiting for transfers between devices, row_step(): lax.ppermute(q_send, 'space', pairs)  3.48 us
    ppermute x1, waiting for transfers between devices, return_step(): lax.ppermute(lse_visit[d], 'space', back[d])  3.39 us
    pallas_call x1, Pallas kernels, return_step(): pl.pallas_call(functools.partial(output_kernel, heads, tile_cols, tile_ro...  3.33 us
  transfers between devices with their start and end apart: 12, of which 3 were waited for; matrix products, arithmetic and copies ran while one was open for 0% of the time, Pallas kernels for 13%

profile of v4, /device:TPU:0, one launch (start us, length us, event | category | flops | bytes accessed | tf_op | source)
XLA Modules:
  0.0 52.0 jit_solution(15539779290026299005)
XLA Ops:
  0.0 0.0 copy-start.3
  0.0 0.0 copy-start.4
  0.0 5.5 %project.1 = (s32[40]{0:T(128)S(1)}, s32[1]{0:T(128)}, s32[1]{0:T(128)}, bf16[6,240,128]{2,1,0:T(8,128)(2,1)S(1)}, bf16[5,240,128]{2,1,0:T(8,128)(2,1)S(1)}, /*index=5*/bf16[6,2,240,128]{3,2,1,0:T(8,128)(2,1)S(1)}) custom-call(s32[2,6]{1,0:T(2,128)} %bitcast.50, bf16[60,4,1536]{2,1,0:T(4,128)(2,1)} %bitcast.44, f32[1536]{0:T(1024)} %shift_at.1, ...), custom_call_target="tpu_custom_call" | custom-call | tf_op jit(solution)/shard_map/project/pallas_call | solution.py:330
  5.5 0.0 copy-done.3
  5.5 0.0 copy-done.4
  5.5 0.0 copy-start
  5.5 0.0 copy-start.1
  5.5 0.0 copy-start.2
  5.5 33.6 %conditional.2 = (f32[6,240,128]{2,1,0:T(8,128)S(1)}, f32[240,128]{1,0:T(8,128)S(1)}, f32[5,240,128]{2,1,0:T(8,128)S(1)}, f32[240,128]{1,0:T(8,128)S(1)}, bf16[1...) conditional(s32[]{:T(128)} %bitcast.24, ...), branch_computations={%region_0.1_spmd, %region_1.2_spmd, %region_2.3_spmd, %region_3.4_... | conditional | flops 353894400 | bytes 20300224 | solution.py:295
  6.4 0.6 %collective-permute-start.10 = (bf16[6,2,240,128]{3,2,1,0:T(8,128)(2,1)S(1)}, bf16[6,2,240,128]{3,2,1,0:T(8,128)(2,1)S(1)}, u32[]{:S(2)}, u32[]{:S(2)}) collective-permute-start(bf16[6,2,240,128]{3,2,1,0:T(8,128)(2,1)S(1)} %get-tuple-element.157.kv_own.kv_here), channel_id=1, source_target_pairs={{0,1},{1,0},{2,3},{3,2},{4,5},{5,4},{6,7},{7,6},{8,9},{9,8},{10,11... | collective-permute-start | bytes 2211848 | tf_op jit(solution)/shard_map/cond/branch_1_fun/ppermute | solution.py:377
  6.9 0.6 %pack.5 = (bf16[3,240,128]{2,1,0:T(8,128)(2,1)S(1)}, bf16[3,240,128]{2,1,0:T(8,128)(2,1)S(1)}) custom-call(s32[40]{0:T(128)S(1)} %get-tuple-element.160.meta, bf16[6,2,240,128]{3,2,1,0:T(8,128)(2,1)S(1)} %get-tuple-element.157.kv_own.kv_here), custom_call_target="tpu_custom_call" | custom-call | tf_op jit(solution)/shard_map/cond/branch_1_fun/pack/pallas_call | solution.py:369
  7.5 2.6 %collective-permute-start.12 = (bf16[3,240,128]{2,1,0:T(8,128)(2,1)S(1)}, bf16[3,240,128]{2,1,0:T(8,128)(2,1)S(1)}, u32[]{:S(2)}, u32[]{:S(2)}) collective-permute-start(bf16[3,240,128]{2,1,0:T(8,128)(2,1)S(1)} %get-tuple-element.162), channel_id=1, source_target_pairs={{0,2},{2,0},{4,6},{6,4},{8,10},{10,8},{12,14},{14,12},{1,3},{3,1},... | collective-permute-start | bytes 552968 | tf_op jit(solution)/shard_map/cond/branch_1_fun/ppermute | solution.py:378
  10.1 0.1 collective-permute-start.13
  10.1 0.7 %collective-permute-start.17 = (bf16[3,240,128]{2,1,0:T(8,128)(2,1)S(1)}, bf16[3,240,128]{2,1,0:T(8,128)(2,1)S(1)}, u32[]{:S(2)}, u32[]{:S(2)}) collective-permute-start(bf16[3,240,128]{2,1,0:T(8,128)(2,1)S(1)} %get-tuple-element.163), channel_id=1, source_target_pairs={{2,4},{4,2},{10,12},{12,10},{3,5},{5,3},{11,13},{13,11},{18,20},{2... | collective-permute-start | bytes 552968 | tf_op jit(solution)/shard_map/cond/branch_1_fun/ppermute | solution.py:380
  10.8 4.7 %collective-permute-done.12.k_pair = bf16[3,240,128]{2,1,0:T(8,128)(2,1)S(1)} collective-permute-done((bf16[3,240,128]{2,1,0:T(8,128)(2,1)S(1)}, bf16[3,240,128]{2,1,0:T(8,128)(2,1)S(1)}, u32[]{:S(2)}, u32[]{:S(2)}) %collective-permute-start.12) | collective-permute-done | bytes 184352 | tf_op jit(solution)/shard_map/cond/branch_1_fun/ppermute | solution.py:378
  15.5 8.0 %collective-permute-start.16 = (bf16[3,240,128]{2,1,0:T(8,128)(2,1)S(1)}, bf16[3,240,128]{2,1,0:T(8,128)(2,1)S(1)}, u32[]{:S(2)}, u32[]{:S(2)}) collective-permute-start(bf16[3,240,128]{2,1,0:T(8,128)(2,1)S(1)} %collective-permute-done.12.k_pair), channel_id=1, source_target_pairs={{0,4},{6,2},{8,12},{14,10},{1,5},{7,3},{9,13},{15,11},{16,20},{22,... | collective-permute-start | bytes 552968 | tf_op jit(solution)/shard_map/cond/branch_1_fun/ppermute | solution.py:382
  23.5 2.7 %collective-permute-start.11 = (bf16[5,240,128]{2,1,0:T(8,128)(2,1)S(1)}, bf16[5,240,128]{2,1,0:T(8,128)(2,1)S(1)}, u32[]{:S(2)}, u32[]{:S(2)}) collective-permute-start(bf16[5,240,128]{2,1,0:T(8,128)(2,1)S(1)} %get-tuple-element.161), channel_id=1, source_target_pairs={{0,8},{2,10},{4,12},{6,14},{8,0},{10,2},{12,4},{14,6},{1,9},{3,11}... | collective-permute-start | bytes 921608 | tf_op jit(solution)/shard_map/cond/branch_1_fun/ppermute | solution.py:379
  26.2 0.0 collective-permute-done.13.v_pair
  26.2 0.0 collective-permute-start.14
  26.2 0.0 collective-permute-done.17.v_far
  26.2 0.5 collective-permute-start.15
  26.7 0.0 collective-permute-done.16.k_far
  26.7 0.1 collective-permute-start.19
  26.8 0.0 collective-permute-done.10.kv_own2
  26.8 0.4 collective-permute-start.18
  27.2 4.0 %own_tile.5 = (f32[6,240,128]{2,1,0:T(8,128)S(1)}, f32[240,128]{1,0:T(8,128)S(1)}, f32[240,480]{1,0:T(8,128)S(1)}, f32[240,960]{1,0:T(8,128)S(1)}) custom-call(s32[8,6]{1,0:T(8,128)S(1)} %get-tuple-element.154.lists, s32[8]{0:T(128)S(1)} %get-tuple-element.155.valid, bf16[6,240,128]{2,1,0:T(8,128)(2,1)S(1)} %get-tuple-element.156.q_here, ...), custom_call_target="tpu_custom_call" | custom-call | flops 353894400 | bytes 6291456 | tf_op jit(solution)/shard_map/cond/branch_1_fun/own_tile/pallas_call | solution.py:386
  31.2 3.5 %collective-permute-done.11 = bf16[5,240,128]{2,1,0:T(8,128)(2,1)S(1)} collective-permute-done((bf16[5,240,128]{2,1,0:T(8,128)(2,1)S(1)}, bf16[5,240,128]{2,1,0:T(8,128)(2,1)S(1)}, u32[]{:S(2)}, u32[]{:S(2)}) %collective-permute-start.11) | collective-permute-done | bytes 307232 | tf_op jit(solution)/shard_map/cond/branch_1_fun/ppermute | solution.py:379
  34.7 0.0 collective-permute-done.14.k_pair2
  34.7 0.0 collective-permute-done.15.v_pair2
  34.7 0.0 collective-permute-done.19.v_far2
  34.7 0.0 collective-permute-done.18.k_far2
  34.7 4.1 %attend.5 = (f32[3,240,128]{2,1,0:T(8,128)S(1)}, f32[240,128]{1,0:T(8,128)S(1)}, bf16[1,5,240,128]{3,2,1,0:T(8,128)(2,1)S(1)}, f32[1,8,256]{2,1,0:T(8,128)S(1)}) custom-call(s32[40]{0:T(128)S(1)} %get-tuple-element.160.meta, bf16[6,240,128]{2,1,0:T(8,128)(2,1)S(1)} %get-tuple-element.156.q_here, bf16[1,5,240,128]{3,2,1,0:T(8,128)(2,1)S(1)} %bitcast.34, ...), custom_call_target="tpu_custom_call" | custom-call | tf_op jit(solution)/shard_map/cond/branch_1_fun/attend/pallas_call | solution.py:402
  38.8 0.1 pad.10
  39.1 0.0 copy-done
  39.1 0.0 copy-done.1
  39.2 0.0 copy-done.2
  39.2 12.6 %conditional.3 = (bf16[60,4,1536]{2,1,0:T(4,128)(2,1)}) conditional(s32[]{:T(128)} %bitcast.23, (s32[40]{0:T(128)S(1)}, f32[6,240,128]{2,1,0:T(8,128)S(1)}, f32[240,128]{1,0:T(8,128)S(1)}, f32[5,240,128]{2,1,0:T(8,128)S(1)}, f32[240,128]{1,0:T(8,128)S(1)}, /*index=5*/bf16[1,5,240,128]{3,2,1,0:T(8,128)(2,1)S(1)}, ...), branch_computations={%region_4.5_spmd, %region_5.6_spmd, %region_6.7_spmd, %region_7.8_... | conditional | flops 4194304 | bytes 3604568 | solution.py:295
  39.8 1.6 %collective-permute-start.42 = (bf16[2,240,128]{2,1,0:T(8,128)(2,1)S(1)}, bf16[2,240,128]{2,1,0:T(8,128)(2,1)S(1)}, u32[]{:S(2)}, u32[]{:S(2)}) collective-permute-start(bf16[2,240,128]{2,1,0:T(8,128)(2,1)S(1)} %slice_bitcast_fusion), channel_id=1, source_target_pairs={{8,0},{10,2},{12,4},{14,6},{0,8},{2,10},{4,12},{6,14},{9,1},{11,3}... | collective-permute-start | bytes 368648 | tf_op jit(solution)/shard_map/cond/branch_0_fun/ppermute | solution.py:433
  41.4 1.4 %collective-permute-start.43 = (f32[8,256]{1,0:T(8,128)S(1)}, f32[8,256]{1,0:T(8,128)S(1)}, u32[]{:S(2)}, u32[]{:S(2)}) collective-permute-start(f32[8,256]{1,0:T(8,128)S(1)} %bitcast.51), channel_id=1, source_target_pairs={{8,0},{10,2},{12,4},{14,6},{0,8},{2,10},{4,12},{6,14},{9,1},{11,3}... | collective-permute-start | bytes 24584 | tf_op jit(solution)/shard_map/cond/branch_0_fun/ppermute | solution.py:434
  42.8 2.2 %row_merge.4 = (f32[6,240,128]{2,1,0:T(8,128)S(1)}, f32[240,128]{1,0:T(8,128)S(1)}) custom-call(s32[40]{0:T(128)S(1)} %get-tuple-element.202.meta, f32[6,240,128]{2,1,0:T(8,128)S(1)} %get-tuple-element.206.o_own, f32[240,128]{1,0:T(8,128)S(1)} %get-tuple-element.207.lse_own, f32[5,240,128]{2,1,0:T(8,128)S(1)} %get-tuple-element.208.o_near, ...), custom_call_target="tpu_custom_call" | custom-call | flops 4194304 | bytes 2097152 | tf_op jit(solution)/shard_map/cond/branch_0_fun/row_merge/pallas_call | solution.py:435
  45.0 3.4 %collective-permute-done.43 = f32[8,256]{1,0:T(8,128)S(1)} collective-permute-done((f32[8,256]{1,0:T(8,128)S(1)}, f32[8,256]{1,0:T(8,128)S(1)}, u32[]{:S(2)}, u32[]{:S(2)}) %collective-permute-start.43) | collective-permute-done | bytes 8224 | tf_op jit(solution)/shard_map/cond/branch_0_fun/ppermute | solution.py:434
  48.4 0.0 collective-permute-done.42
  48.4 3.3 %output.4 = bf16[60,4,1536]{2,1,0:T(4,128)(2,1)} custom-call(s32[40]{0:T(128)S(1)} %get-tuple-element.202.meta, bf16[60,4,1536]{2,1,0:T(4,128)(2,1)S(1)} %get-tuple-element.203.tokens, f32[1536]{0:T(1024)S(1)} %get-tuple-element.204.gate, bf16[768,1536]{1,0:T(8,128)(2,1)S(1)} %get-tuple-element.205.w_out, f32[6,240,128]{2,1,0:T(8,128)S(1)} %get-tuple-element.210.o_row, ...), custom_call_target="tpu_custom_call" | custom-call | tf_op jit(solution)/shard_map/cond/branch_0_fun/output/pallas_call | solution.py:447
  (1 shorter events, 0.0 us)
Async XLA Ops:
  0.0 5.5 %copy-start.3 = (s32[8,6]{1,0:T(8,128)S(1)}, s32[8,6]{1,0:T(8,128)}, u32[]{:S(2)}) copy-start(s32[8,6]{1,0:T(8,128)} %param.28) | copy-start | bytes 580
  0.0 5.5 %copy-start.4 = (s32[8]{0:T(128)S(1)}, s32[8]{0:T(128)}, u32[]{:S(2)}) copy-start(s32[8]{0:T(128)} %param.29) | copy-start | bytes 100
  5.5 33.6 %copy-start = (bf16[768,1536]{1,0:T(8,128)(2,1)S(1)}, bf16[768,1536]{1,0:T(8,128)(2,1)}, u32[]{:S(2)}) copy-start(bf16[768,1536]{1,0:T(8,128)(2,1)} %param.26) | copy-start | bytes 7077892
  5.5 33.6 %copy-start.1 = (bf16[4,1,60,1536]{3,0,2,1:T(4,128)(2,1)S(1)}, bf16[4,1,60,1536]{3,0,2,1:T(4,128)(2,1)}, u32[]{:S(2)}) copy-start(bf16[4,1,60,1536]{3,0,2,1:T(4,128)(2,1)} %param.19) | copy-start | bytes 2211844
  5.5 33.6 %copy-start.2 = (f32[1536]{0:T(1024)S(1)}, f32[1536]{0:T(1024)}, u32[]{:S(2)}) copy-start(f32[1536]{0:T(1024)} %param.22) | copy-start | bytes 18436
  6.4 20.4 %collective-permute-start.10 = (bf16[6,2,240,128]{3,2,1,0:T(8,128)(2,1)S(1)}, bf16[6,2,240,128]{3,2,1,0:T(8,128)(2,1)S(1)}, u32[]{:S(2)}, u32[]{:S(2)}) collective-permute-start(bf16[6,2,240,128]{3,2,1,0:T(8,128)(2,1)S(1)} %get-tuple-element.157.kv_own.kv_here), channel_id=1, source_target_pairs={{0,1},{1,0},{2,3},{3,2},{4,5},{5,4},{6,7},{7,6},{8,9},{9,8},{10,11... | collective-permute-start | bytes 2211848 | tf_op jit(solution)/shard_map/cond/branch_1_fun/ppermute | solution.py:377
  7.5 8.0 %collective-permute-start.12 = (bf16[3,240,128]{2,1,0:T(8,128)(2,1)S(1)}, bf16[3,240,128]{2,1,0:T(8,128)(2,1)S(1)}, u32[]{:S(2)}, u32[]{:S(2)}) collective-permute-start(bf16[3,240,128]{2,1,0:T(8,128)(2,1)S(1)} %get-tuple-element.162), channel_id=1, source_target_pairs={{0,2},{2,0},{4,6},{6,4},{8,10},{10,8},{12,14},{14,12},{1,3},{3,1},... | collective-permute-start | bytes 552968 | tf_op jit(solution)/shard_map/cond/branch_1_fun/ppermute | solution.py:378
  10.1 16.1 %collective-permute-start.13 = (bf16[3,240,128]{2,1,0:T(8,128)(2,1)S(1)}, bf16[3,240,128]{2,1,0:T(8,128)(2,1)S(1)}, u32[]{:S(2)}, u32[]{:S(2)}) collective-permute-start(bf16[3,240,128]{2,1,0:T(8,128)(2,1)S(1)} %get-tuple-element.163), channel_id=1, source_target_pairs={{0,2},{2,0},{4,6},{6,4},{8,10},{10,8},{12,14},{14,12},{1,3},{3,1},... | collective-permute-start | bytes 552968 | tf_op jit(solution)/shard_map/cond/branch_1_fun/ppermute | solution.py:381
  10.1 16.0 %collective-permute-start.17 = (bf16[3,240,128]{2,1,0:T(8,128)(2,1)S(1)}, bf16[3,240,128]{2,1,0:T(8,128)(2,1)S(1)}, u32[]{:S(2)}, u32[]{:S(2)}) collective-permute-start(bf16[3,240,128]{2,1,0:T(8,128)(2,1)S(1)} %get-tuple-element.163), channel_id=1, source_target_pairs={{2,4},{4,2},{10,12},{12,10},{3,5},{5,3},{11,13},{13,11},{18,20},{2... | collective-permute-start | bytes 552968 | tf_op jit(solution)/shard_map/cond/branch_1_fun/ppermute | solution.py:380
  15.5 11.1 %collective-permute-start.16 = (bf16[3,240,128]{2,1,0:T(8,128)(2,1)S(1)}, bf16[3,240,128]{2,1,0:T(8,128)(2,1)S(1)}, u32[]{:S(2)}, u32[]{:S(2)}) collective-permute-start(bf16[3,240,128]{2,1,0:T(8,128)(2,1)S(1)} %collective-permute-done.12.k_pair), channel_id=1, source_target_pairs={{0,4},{6,2},{8,12},{14,10},{1,5},{7,3},{9,13},{15,11},{16,20},{22,... | collective-permute-start | bytes 552968 | tf_op jit(solution)/shard_map/cond/branch_1_fun/ppermute | solution.py:382
  23.5 11.2 %collective-permute-start.11 = (bf16[5,240,128]{2,1,0:T(8,128)(2,1)S(1)}, bf16[5,240,128]{2,1,0:T(8,128)(2,1)S(1)}, u32[]{:S(2)}, u32[]{:S(2)}) collective-permute-start(bf16[5,240,128]{2,1,0:T(8,128)(2,1)S(1)} %get-tuple-element.161), channel_id=1, source_target_pairs={{0,8},{2,10},{4,12},{6,14},{8,0},{10,2},{12,4},{14,6},{1,9},{3,11}... | collective-permute-start | bytes 921608 | tf_op jit(solution)/shard_map/cond/branch_1_fun/ppermute | solution.py:379
  26.2 8.6 %collective-permute-start.14 = (bf16[3,240,128]{2,1,0:T(8,128)(2,1)S(1)}, bf16[3,240,128]{2,1,0:T(8,128)(2,1)S(1)}, u32[]{:S(2)}, u32[]{:S(2)}) collective-permute-start(bf16[3,240,128]{2,1,0:T(8,128)(2,1)S(1)} %collective-permute-done.12.k_pair), channel_id=1, source_target_pairs={{0,1},{1,0},{2,3},{3,2},{4,5},{5,4},{6,7},{7,6},{8,9},{9,8},{10,11... | collective-permute-start | bytes 552968 | tf_op jit(solution)/shard_map/cond/branch_1_fun/ppermute | solution.py:384
  26.2 8.6 %collective-permute-start.15 = (bf16[3,240,128]{2,1,0:T(8,128)(2,1)S(1)}, bf16[3,240,128]{2,1,0:T(8,128)(2,1)S(1)}, u32[]{:S(2)}, u32[]{:S(2)}) collective-permute-start(bf16[3,240,128]{2,1,0:T(8,128)(2,1)S(1)} %collective-permute-done.13.v_pair), channel_id=1, source_target_pairs={{0,1},{1,0},{2,3},{3,2},{4,5},{5,4},{6,7},{7,6},{8,9},{9,8},{10,11... | collective-permute-start | bytes 552968 | tf_op jit(solution)/shard_map/cond/branch_1_fun/ppermute | solution.py:384
  26.7 8.0 %collective-permute-start.19 = (bf16[3,240,128]{2,1,0:T(8,128)(2,1)S(1)}, bf16[3,240,128]{2,1,0:T(8,128)(2,1)S(1)}, u32[]{:S(2)}, u32[]{:S(2)}) collective-permute-start(bf16[3,240,128]{2,1,0:T(8,128)(2,1)S(1)} %collective-permute-done.17.v_far), channel_id=1, source_target_pairs={{0,1},{1,0},{2,3},{3,2},{4,5},{5,4},{6,7},{7,6},{8,9},{9,8},{10,11... | collective-permute-start | bytes 552968 | tf_op jit(solution)/shard_map/cond/branch_1_fun/ppermute | solution.py:384
  26.8 8.0 %collective-permute-start.18 = (bf16[3,240,128]{2,1,0:T(8,128)(2,1)S(1)}, bf16[3,240,128]{2,1,0:T(8,128)(2,1)S(1)}, u32[]{:S(2)}, u32[]{:S(2)}) collective-permute-start(bf16[3,240,128]{2,1,0:T(8,128)(2,1)S(1)} %collective-permute-done.16.k_far), channel_id=1, source_target_pairs={{0,1},{1,0},{2,3},{3,2},{4,5},{5,4},{6,7},{7,6},{8,9},{9,8},{10,11... | collective-permute-start | bytes 552968 | tf_op jit(solution)/shard_map/cond/branch_1_fun/ppermute | solution.py:384
  39.8 8.6 %collective-permute-start.42 = (bf16[2,240,128]{2,1,0:T(8,128)(2,1)S(1)}, bf16[2,240,128]{2,1,0:T(8,128)(2,1)S(1)}, u32[]{:S(2)}, u32[]{:S(2)}) collective-permute-start(bf16[2,240,128]{2,1,0:T(8,128)(2,1)S(1)} %slice_bitcast_fusion), channel_id=1, source_target_pairs={{8,0},{10,2},{12,4},{14,6},{0,8},{2,10},{4,12},{6,14},{9,1},{11,3}... | collective-permute-start | bytes 368648 | tf_op jit(solution)/shard_map/cond/branch_0_fun/ppermute | solution.py:433
  41.4 7.0 %collective-permute-start.43 = (f32[8,256]{1,0:T(8,128)S(1)}, f32[8,256]{1,0:T(8,128)S(1)}, u32[]{:S(2)}, u32[]{:S(2)}) collective-permute-start(f32[8,256]{1,0:T(8,128)S(1)} %bitcast.51), channel_id=1, source_target_pairs={{8,0},{10,2},{12,4},{14,6},{0,8},{2,10},{4,12},{6,14},{9,1},{11,3}... | collective-permute-start | bytes 24584 | tf_op jit(solution)/shard_map/cond/branch_0_fun/ppermute | solution.py:434

commit v5 on v4

--- a/solution.py
+++ b/solution.py
@@ -105,10 +105,11 @@
         q_send[i] = q_here[meta[ORDER_V + i]]
 
 
-def pack_kernel(meta, kv_here, k_send, v_send):
-    for i in range(k_send.shape[0]):
-        k_send[i] = kv_here[meta[ORDER_H + i], 0]
-        v_send[i] = kv_here[meta[ORDER_H + i], 1]
+def pack_kernel(meta, kv_here, *sends):
+    each = sends[0].shape[1]
+    for j, send in enumerate(sends):
+        for i in range(send.shape[0]):
+            send[i] = kv_here[meta[ORDER_H + i], j * each : (j + 1) * each]
 
 
 def softmax_over(query, parts):
@@ -132,8 +133,14 @@
     return [(lambda ref=ref: ref[head, 0], lambda ref=ref: ref[head, 1]) for ref in kv_refs]
 
 
-def near_pieces(refs, slot):
-    return [(lambda k=k: k[slot], lambda v=v: v[slot]) for k, v in refs]
+def two_at_a_time(first, last, compute, store):
+    @pl.loop(0, lax.shift_right_logical(jnp.int32(last - first + 1), jnp.int32(1)))
+    def _(j):
+        one = first + 2 * j
+        other = jnp.minimum(one + 1, last - 1)
+        results = [(i, compute(i)) for i in (one, other)]
+        for i, result in results:
+            store(i, *result)
 
 
 def own_tile_kernel(
@@ -175,25 +182,30 @@
     lane = lax.broadcasted_iota(jnp.int32, lse_own.shape, 1)
     lse_own[...] = jnp.zeros_like(lse_own)
 
-    @pl.loop(0, heads)
-    def _(h):
-        out, lse = softmax_over(q_here[h], [(own_pieces((kv_own, kv_own2), h), bias_own)])
+    def compute(h):
+        return softmax_over(q_here[h], [(own_pieces((kv_own, kv_own2), h), bias_own)])
+
+    def store(h, out, lse):
         o_own[h] = out
         lse_own[...] = jnp.where(lane == h, lse, lse_own[...])
 
-
-def attend_kernel(
-    meta, q_here, q_visit, kv_own, kv_own2, k_pair, v_pair, k_pair2, v_pair2, k_far, v_far, k_far2, v_far2,
-    bias_own, bias_near, o_near, lse_near, o_visit, lse_visit, stats,
-):
+    two_at_a_time(0, heads, compute, store)
+
+
+def attend_kernel(parts, meta, q_here, q_visit, kv_own, kv_own2, *refs):
+    near_refs, (bias_own, bias_near, o_near, lse_near, o_visit, lse_visit, stats) = refs[:-7], refs[-7:]
     directions, _, rows, _ = q_visit.shape
     lane = lax.broadcasted_iota(jnp.int32, (rows, stats.shape[1]), 1)
     stats[...] = jnp.zeros_like(stats)
-    sent = k_pair.shape[0]
+    sent = near_refs[0].shape[0]
 
     def near(slot):
-        refs = ((k_pair, v_pair), (k_pair2, v_pair2), (k_far, v_far), (k_far2, v_far2))
-        return near_pieces(refs, slot), bias_near
+        last = 2 // parts - 1
+        pieces = [
+            (lambda k=k: k[slot, 0], lambda v=v: v[slot, last])
+            for k, v in zip(near_refs[::parts], near_refs[parts - 1 :: parts])
+        ]
+        return pieces, bias_near
 
     def own(head):
         return own_pieces((kv_own, kv_own2), head), bias_own
@@ -207,18 +219,21 @@
         keep(i, lse)
 
     for d in range(directions):
-        @pl.loop(0, meta[N_BOTH])
-        def _(i, d=d):
-            head = meta[ORDER_V + i]
-            out, lse = softmax_over(q_visit[d, i], [near(meta[SLOT_H + head]), own(head)])
+        def store(i, out, lse, d=d):
             o_visit[d, i] = out.astype(o_visit.dtype)
             keep(16 + d * 8 + i, lse)
 
+        def over_row(i, d=d):
+            head = meta[ORDER_V + i]
+            return softmax_over(q_visit[d, i], [near(meta[SLOT_H + head]), own(head)])
+
+        @pl.loop(0, meta[N_BOTH])
+        def _(i, store=store, over_row=over_row):
+            store(i, *over_row(i))
+
         @pl.loop(meta[N_BOTH], meta[N_V])
-        def _(i, d=d):
-            out, lse = softmax_over(q_visit[d, i], [own(meta[ORDER_V + i])])
-            o_visit[d, i] = out.astype(o_visit.dtype)
-            keep(16 + d * 8 + i, lse)
+        def _(i, d=d, store=store):
+            store(i, *softmax_over(q_visit[d, i], [own(meta[ORDER_V + i])]))
 
     lse_near[...] = stats[0:rows]
     turned = jnp.transpose(stats[...])
@@ -239,41 +254,50 @@
     return jnp.sum(jnp.where(lane == at, table, 0.0), axis=1, keepdims=True)
 
 
-def row_kernel(heads, meta, o_own, lse_own, o_near, lse_near, o_row, lse_row):
+def row_kernel(heads, meta, o_own, lse_own, o_near, lse_near, o_row, lse_row, attended):
     lane = lax.broadcasted_iota(jnp.int32, lse_row.shape, 1)
-    own, near = lse_own[...], lse_near[...]
-    merged = own
-    for h in range(heads):
+    lse_row[...] = lse_own[...]
+
+    @pl.loop(0, heads)
+    def _(h):
         slot = meta[SLOT_H + h]
         use = slot < meta[N_H]
         at = jnp.minimum(slot, o_near.shape[0] - 1)
-        there = jnp.where(use, pick_lane(near, at), NEG)
-        result, lse = merge([(own[:, h : h + 1], o_own[h]), (there, jnp.where(use, o_near[at], 0.0))])
+        there = jnp.where(use, pick_lane(lse_near[...], at), NEG)
+        result, lse = merge(
+            [(pick_lane(lse_own[...], h), o_own[h]), (there, jnp.where(use, o_near[at], 0.0))]
+        )
         o_row[h] = result
-        merged = jnp.where(lane == h, lse, merged)
-    lse_row[...] = merged
+        attended[:, pl.ds(pl.multiple_of(h * HEAD_DIM, HEAD_DIM), HEAD_DIM)] = result.astype(jnp.bfloat16)
+        lse_row[...] = jnp.where(lane == h, lse, lse_row[...])
 
 
 def output_kernel(
-    heads, tile_cols, tile_rows, meta, tokens, gate, w_out, o_row, lse_row, o_back, lse_back,
+    tile_cols, tile_rows, meta, tokens, gate, w_out, o_row, lse_row, row_attended, o_back, lse_back,
     out, attended, back, staged, sems,
 ):
-    directions, slots, rows, _ = o_back.shape
+    directions, _, rows, _ = o_back.shape
     tile_tokens, frames, _ = tokens.shape
-    back[...] = jnp.zeros_like(back)
     for d in range(directions):
         back[d * 8 : (d + 1) * 8] = lse_back[d]
     turned = jnp.transpose(back[...])[:rows]
     tile_row = lax.axis_index("space") // tile_cols
     exists = [True] if tile_rows == 2 else [tile_row < tile_rows - 1, tile_row > 0]
-    for h in range(heads):
-        parts = [(lse_row[:, h : h + 1], o_row[h])]
-        at = jnp.minimum(meta[SLOT_V + h], slots - 1)
+    attended[...] = row_attended[...]
+
+    def compute(i):
+        head = meta[ORDER_V + i]
+        parts = [(pick_lane(lse_row[...], head), o_row[head])]
         for d in range(directions):
-            use = jnp.logical_and(meta[SLOT_V + h] < meta[N_V], exists[d])
-            there = jnp.where(use, pick_lane(turned, d * 8 + at), NEG)
-            parts.append((there, jnp.where(use, o_back[d, at].astype(jnp.float32), 0.0)))
-        attended[:, h * HEAD_DIM : (h + 1) * HEAD_DIM] = merge(parts)[0].astype(jnp.bfloat16)
+            there = jnp.where(exists[d], pick_lane(turned, d * 8 + i), NEG)
+            parts.append((there, jnp.where(exists[d], o_back[d, i].astype(jnp.float32), 0.0)))
+        return (merge(parts)[0].astype(jnp.bfloat16),)
+
+    def store(i, mixed):
+        at = pl.multiple_of(meta[ORDER_V + i] * HEAD_DIM, HEAD_DIM)
+        attended[:, pl.ds(at, HEAD_DIM)] = mixed
+
+    two_at_a_time(0, meta[N_V], compute, store)
     width = out.shape[2] // sems.shape[0]
     copies = []
     for j in range(sems.shape[0]):
@@ -326,7 +350,7 @@
     directions = len(vertical)
     swap = [(0, 1), (1, 0)]
 
-    least = min(2, slots)
+    least, few = min(2, slots), min(3, slots)
     meta, wide_branch, tall_branch, q_here, q_send, kv_here = pl.pallas_call(
         functools.partial(project_kernel, heads, least),
         in_specs=[HBM] * 7,
@@ -366,23 +390,26 @@
         return row_step(sent, *operands)
 
     def row_step(sent, kv_here, q_send, q_here, meta):
-        k_send, v_send = pl.pallas_call(
+        parts = 2 if sent > few else 1
+        packed = pl.pallas_call(
             pack_kernel,
             in_specs=[SMEM, VMEM],
-            out_specs=[VMEM, VMEM],
-            out_shape=[jax.ShapeDtypeStruct((sent, rows, HEAD_DIM), bf16)] * 2,
+            out_specs=[VMEM] * parts,
+            out_shape=[jax.ShapeDtypeStruct((sent, 2 // parts, rows, HEAD_DIM), bf16)] * parts,
             compiler_params=params(4),
             name="pack",
         )(meta, kv_here)
         kv_other = lax.ppermute(kv_here, "tm", swap)
-        k_pair = lax.ppermute(k_send, "space", pair)
+        near = [lax.ppermute(packed[0], "space", pair)]
         q_visit = jnp.stack([lax.ppermute(q_send, "space", pairs) for pairs in vertical])
-        v_far = lax.ppermute(v_send, "space", far)
-        v_pair = lax.ppermute(v_send, "space", pair)
-        k_far = lax.ppermute(k_pair, "space", relay)
-        k_pair2, v_pair2, k_far2, v_far2 = [
-            lax.ppermute(x, "tm", swap) for x in (k_pair, v_pair, k_far, v_far)
-        ]
+        far_part = lax.ppermute(packed[-1], "space", far)
+        if parts == 2:
+            near.append(lax.ppermute(packed[1], "space", pair))
+            near.append(lax.ppermute(near[0], "space", relay))
+        near.append(far_part)
+        near = [x for part in near for x in (part, lax.ppermute(part, "tm", swap))]
+        if parts == 2:
+            near = [near[i] for i in (0, 2, 1, 3, 4, 6, 5, 7)]
         o_own, lse_own, bias_own, bias_near = pl.pallas_call(
             functools.partial(own_tile_kernel, heads, tile_cols),
             in_specs=[SMEM] * 2 + [VMEM] * 3,
@@ -400,11 +427,11 @@
             name="own_tile",
         )(frame_lists, frame_valid, q_here, kv_here, kv_other)
         o_near, lse_near, o_visit, lse_visit = pl.pallas_call(
-            attend_kernel,
-            in_specs=[SMEM] + [VMEM] * 14,
+            functools.partial(attend_kernel, parts),
+            in_specs=[SMEM] + [VMEM] * (6 + len(near)),
             out_specs=[VMEM] * 4,
             out_shape=[
-                jax.ShapeDtypeStruct((sent, rows, HEAD_DIM), f32),
+                jax.ShapeDtypeStruct((slots, rows, HEAD_DIM), f32),
                 jax.ShapeDtypeStruct((rows, lanes), f32),
                 jax.ShapeDtypeStruct((directions, slots, rows, HEAD_DIM), bf16),
                 jax.ShapeDtypeStruct((directions, 8, stat_rows), f32),
@@ -412,18 +439,13 @@
             scratch_shapes=[pltpu.VMEM((stat_rows, lanes), f32)],
             compiler_params=params(24),
             name="attend",
-        )(meta, q_here, q_visit, kv_here, kv_other, k_pair, v_pair, k_pair2, v_pair2, k_far, v_far, k_far2, v_far2,
-          bias_own, bias_near)
-        o_near = jnp.pad(o_near, ((0, slots - sent), (0, 0), (0, 0)))
+        )(meta, q_here, q_visit, kv_here, kv_other, *near, bias_own, bias_near)
         return o_own, lse_own, o_near, lse_near, o_visit, lse_visit
 
-    def pick(number, branch, *operands):
-        return branch_on(
-            number.reshape(()), [functools.partial(branch, n) for n in range(least, slots + 1)], *operands
-        )
-
-    o_own, lse_own, o_near, lse_near, o_visit, lse_visit = pick(
-        wide_branch, along_row, kv_here, q_send, q_here, meta
+    o_own, lse_own, o_near, lse_near, o_visit, lse_visit = branch_on(
+        wide_branch.reshape(()),
+        [functools.partial(along_row, n) for n in range(least, slots + 1)],
+        kv_here, q_send, q_here, meta,
     )
 
     def between_rows(sent, *operands):
@@ -432,21 +454,22 @@
     def return_step(sent, o_own, lse_own, o_near, lse_near, o_visit, lse_visit, meta):
         o_back = jnp.stack([lax.ppermute(o_visit[d, :sent], "space", back[d]) for d in range(directions)])
         lse_back = jnp.stack([lax.ppermute(lse_visit[d], "space", back[d]) for d in range(directions)])
-        o_row, lse_row = pl.pallas_call(
+        row = pl.pallas_call(
             functools.partial(row_kernel, heads),
             in_specs=[SMEM] + [VMEM] * 4,
-            out_specs=[VMEM] * 2,
+            out_specs=[VMEM] * 3,
             out_shape=[
                 jax.ShapeDtypeStruct((heads, rows, HEAD_DIM), f32),
                 jax.ShapeDtypeStruct((rows, lanes), f32),
+                jax.ShapeDtypeStruct((rows, inner), bf16),
             ],
             compiler_params=params(8),
             cost_estimate=pl.CostEstimate(flops=1 << 22, bytes_accessed=2 << 20, transcendentals=1 << 14),
             name="row_merge",
         )(meta, o_own, lse_own, o_near, lse_near)
         return pl.pallas_call(
-            functools.partial(output_kernel, heads, tile_cols, tile_rows),
-            in_specs=[SMEM] + [VMEM] * 7,
+            functools.partial(output_kernel, tile_cols, tile_rows),
+            in_specs=[SMEM] + [VMEM] * 8,
             out_specs=HBM,
             out_shape=pltpu.HBM(tokens.shape, bf16),
             scratch_shapes=[
@@ -457,9 +480,13 @@
             ],
             compiler_params=params(16),
             name="output",
-        )(meta, tokens, mod_gate, w_out, o_row, lse_row, o_back, lse_back)
-
-    mixed = pick(tall_branch, between_rows, o_own, lse_own, o_near, lse_near, o_visit, lse_visit, meta)
+        )(meta, tokens, mod_gate, w_out, *row, o_back, lse_back)
+
+    mixed = branch_on(
+        tall_branch.reshape(()),
+        [functools.partial(between_rows, n) for n in range(least, slots + 1)],
+        o_own, lse_own, o_near, lse_near, o_visit, lse_visit, meta,
+    )
     return jnp.transpose(mixed, (1, 0, 2))[:, None]
 
 

time: 52.2 us -> 60.1 us (1.15)
  waiting for transfers between devices: 11.6 us -> 30.3 us
  starting transfers between devices: 18.5 us -> 9.86 us
  Pallas kernels: 19.7 us -> 17.7 us
    ppermute x8 -> x4, waiting for transfers between devices: 4.76 us -> 15.7 us  [the longest x1 15.7 us: row_step(): near = [lax.ppermute(packed[0], 'space', pair)]]
    ppermute x8 -> x4, starting transfers between devices: 12.3 us -> 3.74 us  [the longest x1 2.56 us: row_step(): near = [lax.ppermute(packed[0], 'space', pair)]]
    ppermute x1, waiting for transfers between devices: 3.48 us -> 10.6 us  [row_step(): lax.ppermute(q_send, 'space', pairs)]
    ppermute x1, starting transfers between devices: 1.57 us -> 0.07 us  [return_step(): lax.ppermute(o_visit[d, :sent], 'space', back[d])]
    ppermute x1, starting transfers between devices: 1.42 us -> 2.91 us  [return_step(): lax.ppermute(lse_visit[d], 'space', back[d])]
    pallas_call x3, Pallas kernels: 7.97 us -> 7.01 us  [the longest x1 4.01 us: row_step(): pl.pallas_call(functools.partial(attend_kernel, parts), in_specs=[SMEM] +...]
  transfers between devices with their start and end apart: 12 -> 8, of which waited for: 3 -> 3; matrix products, arithmetic and copies ran while one was open for 0% -> 0% of each run, Pallas kernels for 13% -> 10%
where the time goes in v5:
time: 60.1 us; the launch traced here: 59.9 us
  waiting for transfers between devices  30.3 us (50%)
  Pallas kernels  17.7 us (29%)
  starting transfers between devices  9.86 us (16%)
  loops' own time  1.75 us (3%)
    ppermute x1, waiting for transfers between devices, row_step(): near = [lax.ppermute(packed[0], 'space', pair)]  15.7 us
    ppermute x1, waiting for transfers between devices, row_step(): lax.ppermute(q_send, 'space', pairs)  10.6 us
    pallas_call x1, Pallas kernels, per_device(): pl.pallas_call(functools.partial(project_kernel, heads, least), in_specs=...  5.47 us
    pallas_call x1, Pallas kernels, row_step(): pl.pallas_call(functools.partial(attend_kernel, parts), in_specs=[SMEM] +...  4.01 us
    ppermute x1, waiting for transfers between devices, return_step(): lax.ppermute(lse_visit[d], 'space', back[d])  3.93 us
    pallas_call x1, Pallas kernels, row_step(): pl.pallas_call(functools.partial(own_tile_kernel, heads, tile_cols), in_s...  3.46 us
    ppermute x1, starting transfers between devices, return_step(): lax.ppermute(lse_visit[d], 'space', back[d])  2.91 us
    ppermute x1, starting transfers between devices, row_step(): lax.ppermute(q_send, 'space', pairs)  2.58 us
  transfers between devices with their start and end apart: 8, of which 3 were waited for; matrix products, arithmetic and copies ran while one was open for 0% of the time, Pallas kernels for 10%

profile of v5, /device:TPU:0, one launch (start us, length us, event | category | flops | bytes accessed | tf_op | source)
XLA Modules:
  0.0 59.9 jit_solution(9553433111269257627)
XLA Ops:
  0.0 0.0 copy-start.3
  0.0 0.0 copy-start.4
  0.0 5.5 %project.1 = (s32[40]{0:T(128)S(1)}, s32[1]{0:T(128)}, s32[1]{0:T(128)}, bf16[6,240,128]{2,1,0:T(8,128)(2,1)S(1)}, bf16[5,240,128]{2,1,0:T(8,128)(2,1)S(1)}, /*index=5*/bf16[6,2,240,128]{3,2,1,0:T(8,128)(2,1)S(1)}) custom-call(s32[2,6]{1,0:T(2,128)} %bitcast.50, bf16[60,4,1536]{2,1,0:T(4,128)(2,1)} %bitcast.44, f32[1536]{0:T(1024)} %shift_at.1, ...), custom_call_target="tpu_custom_call" | custom-call | tf_op jit(solution)/shard_map/project/pallas_call | solution.py:354
  5.5 0.0 copy-done.3
  5.5 0.0 copy-done.4
  5.5 0.0 copy-start
  5.5 0.0 copy-start.1
  5.5 0.0 copy-start.2
  5.5 42.3 %conditional.2 = (f32[6,240,128]{2,1,0:T(8,128)S(1)}, f32[240,128]{1,0:T(8,128)S(1)}, f32[5,240,128]{2,1,0:T(8,128)S(1)}, f32[240,128]{1,0:T(8,128)S(1)}, bf16[1...) conditional(s32[]{:T(128)} %bitcast.24, ...), branch_computations={%region_0.0_spmd, %region_1.0_spmd, %region_2.0_spmd, %region_3.0_... | conditional | flops 353894400 | bytes 20300224 | solution.py:319
  6.4 0.6 collective-permute-start.6
  6.9 0.6 pack.5
  7.5 2.6 %collective-permute-start.8 = (bf16[3,2,240,128]{3,2,1,0:T(8,128)(2,1)S(1)}, bf16[3,2,240,128]{3,2,1,0:T(8,128)(2,1)S(1)}, u32[]{:S(2)}, u32[]{:S(2)}) collective-permute-start(bf16[3,2,240,128]{3,2,1,0:T(8,128)(2,1)S(1)} %pack.5), channel_id=1, source_target_pairs={{0,2},{2,0},{4,6},{6,4},{8,10},{10,8},{12,14},{14,12},{1,3},{3,1},... | collective-permute-start | bytes 1105928 | tf_op jit(solution)/shard_map/cond/branch_1_fun/ppermute | solution.py:403
  10.1 0.7 %collective-permute-start.10 = (bf16[3,2,240,128]{3,2,1,0:T(8,128)(2,1)S(1)}, bf16[3,2,240,128]{3,2,1,0:T(8,128)(2,1)S(1)}, u32[]{:S(2)}, u32[]{:S(2)}) collective-permute-start(bf16[3,2,240,128]{3,2,1,0:T(8,128)(2,1)S(1)} %pack.5), channel_id=1, source_target_pairs={{2,4},{4,2},{10,12},{12,10},{3,5},{5,3},{11,13},{13,11},{18,20},{2... | collective-permute-start | bytes 1105928 | tf_op jit(solution)/shard_map/cond/branch_1_fun/ppermute | solution.py:405
  10.7 15.7 %collective-permute-done.8.refs_0_ = bf16[3,2,240,128]{3,2,1,0:T(8,128)(2,1)S(1)} collective-permute-done((bf16[3,2,240,128]{3,2,1,0:T(8,128)(2,1)S(1)}, bf16[3,2,240,128]{3,2,1,0:T(8,128)(2,1)S(1)}, u32[]{:S(2)}, u32[]{:S(2)}) %collective-permute-start.8) | collective-permute-done | bytes 368672 | tf_op jit(solution)/shard_map/cond/branch_1_fun/ppermute | solution.py:403
  26.5 0.0 collective-permute-start.9
  26.5 0.0 collective-permute-done.10.refs_2_
  26.5 0.5 collective-permute-start.11
  27.0 2.6 %collective-permute-start.7 = (bf16[5,240,128]{2,1,0:T(8,128)(2,1)S(1)}, bf16[5,240,128]{2,1,0:T(8,128)(2,1)S(1)}, u32[]{:S(2)}, u32[]{:S(2)}) collective-permute-start(bf16[5,240,128]{2,1,0:T(8,128)(2,1)S(1)} %get-tuple-element.159), channel_id=1, source_target_pairs={{0,8},{2,10},{4,12},{6,14},{8,0},{10,2},{12,4},{14,6},{1,9},{3,11}... | collective-permute-start | bytes 921608 | tf_op jit(solution)/shard_map/cond/branch_1_fun/ppermute | solution.py:404
  29.6 0.0 collective-permute-done.6.kv_own2
  29.6 3.5 %own_tile.5 = (f32[6,240,128]{2,1,0:T(8,128)S(1)}, f32[240,128]{1,0:T(8,128)S(1)}, f32[240,480]{1,0:T(8,128)S(1)}, f32[240,960]{1,0:T(8,128)S(1)}) custom-call(s32[8,6]{1,0:T(8,128)S(1)} %get-tuple-element.152.lists, s32[8]{0:T(128)S(1)} %get-tuple-element.153.valid, bf16[6,240,128]{2,1,0:T(8,128)(2,1)S(1)} %get-tuple-element.154.q_here, ...), custom_call_target="tpu_custom_call" | custom-call | flops 353894400 | bytes 6291456 | tf_op jit(solution)/shard_map/cond/branch_1_fun/own_tile/pallas_call | solution.py:413
  33.0 10.6 %collective-permute-done.7 = bf16[5,240,128]{2,1,0:T(8,128)(2,1)S(1)} collective-permute-done((bf16[5,240,128]{2,1,0:T(8,128)(2,1)S(1)}, bf16[5,240,128]{2,1,0:T(8,128)(2,1)S(1)}, u32[]{:S(2)}, u32[]{:S(2)}) %collective-permute-start.7) | collective-permute-done | bytes 307232 | tf_op jit(solution)/shard_map/cond/branch_1_fun/ppermute | solution.py:404
  43.6 0.0 collective-permute-done.9.refs_1_
  43.6 0.0 collective-permute-done.11.refs_3_
  43.6 4.0 %attend.5 = (f32[5,240,128]{2,1,0:T(8,128)S(1)}, f32[240,128]{1,0:T(8,128)S(1)}, bf16[1,5,240,128]{3,2,1,0:T(8,128)(2,1)S(1)}, f32[1,8,256]{2,1,0:T(8,128)S(1)}) custom-call(s32[40]{0:T(128)S(1)} %get-tuple-element.158.meta, bf16[6,240,128]{2,1,0:T(8,128)(2,1)S(1)} %get-tuple-element.154.q_here, bf16[1,5,240,128]{3,2,1,0:T(8,128)(2,1)S(1)} %bitcast.36, ...), custom_call_target="tpu_custom_call" | custom-call | tf_op jit(solution)/shard_map/cond/branch_1_fun/attend/pallas_call | solution.py:429
  47.9 0.0 copy-done
  47.9 0.0 copy-done.1
  47.9 0.0 copy-done.2
  47.9 11.7 %conditional.3 = (bf16[60,4,1536]{2,1,0:T(4,128)(2,1)}) conditional(s32[]{:T(128)} %bitcast.23, (s32[40]{0:T(128)S(1)}, f32[6,240,128]{2,1,0:T(8,128)S(1)}, f32[240,128]{1,0:T(8,128)S(1)}, f32[5,240,128]{2,1,0:T(8,128)S(1)}, f32[240,128]{1,0:T(8,128)S(1)}, /*index=5*/bf16[1,5,240,128]{3,2,1,0:T(8,128)(2,1)S(1)}, ...), branch_computations={%region_4.0_spmd, %region_5.0_spmd, %region_6.0_spmd, %region_7.0_... | conditional | flops 4194304 | bytes 3604568 | solution.py:319
  48.6 0.1 collective-permute-start.34
  48.7 2.9 %collective-permute-start.35 = (f32[8,256]{1,0:T(8,128)S(1)}, f32[8,256]{1,0:T(8,128)S(1)}, u32[]{:S(2)}, u32[]{:S(2)}) collective-permute-start(f32[8,256]{1,0:T(8,128)S(1)} %bitcast.51), channel_id=1, source_target_pairs={{8,0},{10,2},{12,4},{14,6},{0,8},{2,10},{4,12},{6,14},{9,1},{11,3}... | collective-permute-start | bytes 24584 | tf_op jit(solution)/shard_map/cond/branch_0_fun/ppermute | solution.py:456
  51.6 1.7 %row_merge.4 = (f32[6,240,128]{2,1,0:T(8,128)S(1)}, f32[240,128]{1,0:T(8,128)S(1)}, bf16[240,768]{1,0:T(8,128)(2,1)S(1)}) custom-call(s32[40]{0:T(128)S(1)} %get-tuple-element.198.meta, f32[6,240,128]{2,1,0:T(8,128)S(1)} %get-tuple-element.202.o_own, f32[240,128]{1,0:T(8,128)S(1)} %get-tuple-element.203.lse_own, ...), custom_call_target="tpu_custom_call" | custom-call | flops 4194304 | bytes 2097152 | tf_op jit(solution)/shard_map/cond/branch_0_fun/row_merge/pallas_call | solution.py:457
  53.3 3.9 %collective-permute-done.35 = f32[8,256]{1,0:T(8,128)S(1)} collective-permute-done((f32[8,256]{1,0:T(8,128)S(1)}, f32[8,256]{1,0:T(8,128)S(1)}, u32[]{:S(2)}, u32[]{:S(2)}) %collective-permute-start.35) | collective-permute-done | bytes 8224 | tf_op jit(solution)/shard_map/cond/branch_0_fun/ppermute | solution.py:456
  57.2 0.0 collective-permute-done.34
  57.2 2.4 %output.4 = bf16[60,4,1536]{2,1,0:T(4,128)(2,1)} custom-call(s32[40]{0:T(128)S(1)} %get-tuple-element.198.meta, bf16[60,4,1536]{2,1,0:T(4,128)(2,1)S(1)} %get-tuple-element.199.tokens, f32[1536]{0:T(1024)S(1)} %get-tuple-element.200.gate, bf16[768,1536]{1,0:T(8,128)(2,1)S(1)} %get-tuple-element.201.w_out, f32[6,240,128]{2,1,0:T(8,128)S(1)} %get-tuple-element.206.o_row, ...), custom_call_target="tpu_custom_call" | custom-call | tf_op jit(solution)/shard_map/cond/branch_0_fun/output/pallas_call | solution.py:470
  (1 shorter events, 0.0 us)
Async XLA Ops:
  0.0 5.5 %copy-start.3 = (s32[8,6]{1,0:T(8,128)S(1)}, s32[8,6]{1,0:T(8,128)}, u32[]{:S(2)}) copy-start(s32[8,6]{1,0:T(8,128)} %param.28) | copy-start | bytes 580
  0.0 5.5 %copy-start.4 = (s32[8]{0:T(128)S(1)}, s32[8]{0:T(128)}, u32[]{:S(2)}) copy-start(s32[8]{0:T(128)} %param.29) | copy-start | bytes 100
  5.5 42.4 %copy-start = (bf16[768,1536]{1,0:T(8,128)(2,1)S(1)}, bf16[768,1536]{1,0:T(8,128)(2,1)}, u32[]{:S(2)}) copy-start(bf16[768,1536]{1,0:T(8,128)(2,1)} %param.26) | copy-start | bytes 7077892
  5.5 42.4 %copy-start.1 = (bf16[4,1,60,1536]{3,0,2,1:T(4,128)(2,1)S(1)}, bf16[4,1,60,1536]{3,0,2,1:T(4,128)(2,1)}, u32[]{:S(2)}) copy-start(bf16[4,1,60,1536]{3,0,2,1:T(4,128)(2,1)} %param.19) | copy-start | bytes 2211844
  5.5 42.4 %copy-start.2 = (f32[1536]{0:T(1024)S(1)}, f32[1536]{0:T(1024)}, u32[]{:S(2)}) copy-start(f32[1536]{0:T(1024)} %param.22) | copy-start | bytes 18436
  6.4 23.2 %collective-permute-start.6 = (bf16[6,2,240,128]{3,2,1,0:T(8,128)(2,1)S(1)}, bf16[6,2,240,128]{3,2,1,0:T(8,128)(2,1)S(1)}, u32[]{:S(2)}, u32[]{:S(2)}) collective-permute-start(bf16[6,2,240,128]{3,2,1,0:T(8,128)(2,1)S(1)} %get-tuple-element.155.kv_own.kv_here), channel_id=1, source_target_pairs={{0,1},{1,0},{2,3},{3,2},{4,5},{5,4},{6,7},{7,6},{8,9},{9,8},{10,11... | collective-permute-start | bytes 2211848 | tf_op jit(solution)/shard_map/cond/branch_1_fun/ppermute | solution.py:402
  7.5 19.0 %collective-permute-start.8 = (bf16[3,2,240,128]{3,2,1,0:T(8,128)(2,1)S(1)}, bf16[3,2,240,128]{3,2,1,0:T(8,128)(2,1)S(1)}, u32[]{:S(2)}, u32[]{:S(2)}) collective-permute-start(bf16[3,2,240,128]{3,2,1,0:T(8,128)(2,1)S(1)} %pack.5), channel_id=1, source_target_pairs={{0,2},{2,0},{4,6},{6,4},{8,10},{10,8},{12,14},{14,12},{1,3},{3,1},... | collective-permute-start | bytes 1105928 | tf_op jit(solution)/shard_map/cond/branch_1_fun/ppermute | solution.py:403
  10.1 16.4 %collective-permute-start.10 = (bf16[3,2,240,128]{3,2,1,0:T(8,128)(2,1)S(1)}, bf16[3,2,240,128]{3,2,1,0:T(8,128)(2,1)S(1)}, u32[]{:S(2)}, u32[]{:S(2)}) collective-permute-start(bf16[3,2,240,128]{3,2,1,0:T(8,128)(2,1)S(1)} %pack.5), channel_id=1, source_target_pairs={{2,4},{4,2},{10,12},{12,10},{3,5},{5,3},{11,13},{13,11},{18,20},{2... | collective-permute-start | bytes 1105928 | tf_op jit(solution)/shard_map/cond/branch_1_fun/ppermute | solution.py:405
  26.5 17.2 %collective-permute-start.9 = (bf16[3,2,240,128]{3,2,1,0:T(8,128)(2,1)S(1)}, bf16[3,2,240,128]{3,2,1,0:T(8,128)(2,1)S(1)}, u32[]{:S(2)}, u32[]{:S(2)}) collective-permute-start(bf16[3,2,240,128]{3,2,1,0:T(8,128)(2,1)S(1)} %collective-permute-done.8.refs_0_), channel_id=1, source_target_pairs={{0,1},{1,0},{2,3},{3,2},{4,5},{5,4},{6,7},{7,6},{8,9},{9,8},{10,11... | collective-permute-start | bytes 1105928 | tf_op jit(solution)/shard_map/cond/branch_1_fun/ppermute | solution.py:410
  26.5 17.2 %collective-permute-start.11 = (bf16[3,2,240,128]{3,2,1,0:T(8,128)(2,1)S(1)}, bf16[3,2,240,128]{3,2,1,0:T(8,128)(2,1)S(1)}, u32[]{:S(2)}, u32[]{:S(2)}) collective-permute-start(bf16[3,2,240,128]{3,2,1,0:T(8,128)(2,1)S(1)} %collective-permute-done.10.refs_2_), channel_id=1, source_target_pairs={{0,1},{1,0},{2,3},{3,2},{4,5},{5,4},{6,7},{7,6},{8,9},{9,8},{10,11... | collective-permute-start | bytes 1105928 | tf_op jit(solution)/shard_map/cond/branch_1_fun/ppermute | solution.py:410
  27.0 16.7 %collective-permute-start.7 = (bf16[5,240,128]{2,1,0:T(8,128)(2,1)S(1)}, bf16[5,240,128]{2,1,0:T(8,128)(2,1)S(1)}, u32[]{:S(2)}, u32[]{:S(2)}) collective-permute-start(bf16[5,240,128]{2,1,0:T(8,128)(2,1)S(1)} %get-tuple-element.159), channel_id=1, source_target_pairs={{0,8},{2,10},{4,12},{6,14},{8,0},{10,2},{12,4},{14,6},{1,9},{3,11}... | collective-permute-start | bytes 921608 | tf_op jit(solution)/shard_map/cond/branch_1_fun/ppermute | solution.py:404
  48.6 8.7 %collective-permute-start.34 = (bf16[2,240,128]{2,1,0:T(8,128)(2,1)S(1)}, bf16[2,240,128]{2,1,0:T(8,128)(2,1)S(1)}, u32[]{:S(2)}, u32[]{:S(2)}) collective-permute-start(bf16[2,240,128]{2,1,0:T(8,128)(2,1)S(1)} %slice_bitcast_fusion), channel_id=1, source_target_pairs={{8,0},{10,2},{12,4},{14,6},{0,8},{2,10},{4,12},{6,14},{9,1},{11,3}... | collective-permute-start | bytes 368648 | tf_op jit(solution)/shard_map/cond/branch_0_fun/ppermute | solution.py:455
  48.7 8.6 %collective-permute-start.35 = (f32[8,256]{1,0:T(8,128)S(1)}, f32[8,256]{1,0:T(8,128)S(1)}, u32[]{:S(2)}, u32[]{:S(2)}) collective-permute-start(f32[8,256]{1,0:T(8,128)S(1)} %bitcast.51), channel_id=1, source_target_pairs={{8,0},{10,2},{12,4},{14,6},{0,8},{2,10},{4,12},{6,14},{9,1},{11,3}... | collective-permute-start | bytes 24584 | tf_op jit(solution)/shard_map/cond/branch_0_fun/ppermute | solution.py:456

commit v6 on v5

--- a/solution.py
+++ b/solution.py
@@ -42,7 +42,7 @@
 
 
 def project_kernel(
-    heads, least, windows_at, tokens_at, shift_at, scale_at, w_qkv, q_gain_at, k_gain_at,
+    heads, least, few, windows_at, tokens_at, shift_at, scale_at, w_qkv, q_gain_at, k_gain_at,
     meta, wide_branch, tall_branch, q_here, q_send, kv_here,
     windows, tokens, shift, scale, q_gain, k_gain, modulated, w_buf, small_sems, sems,
 ):
@@ -65,7 +65,8 @@
     for copy in small:
         copy.wait()
     rank_heads(windows, meta, heads)
-    wide_branch[0] = jnp.clip(meta[N_H] - least, 0, heads - 1 - least)
+    wide = jnp.clip(meta[N_H] - least, 0, heads - 1 - least)
+    wide_branch[0] = jnp.where((wide == 0) & (meta[N_V] <= few), 0, wide + 1)
     tall_branch[0] = jnp.clip(meta[N_V] - least, 0, heads - 1 - least)
     gain_row = 1.0 + scale[...][None, :]
     shift_row = shift[...][None, :]
@@ -352,7 +353,7 @@
 
     least, few = min(2, slots), min(3, slots)
     meta, wide_branch, tall_branch, q_here, q_send, kv_here = pl.pallas_call(
-        functools.partial(project_kernel, heads, least),
+        functools.partial(project_kernel, heads, least, few),
         in_specs=[HBM] * 7,
         out_specs=[SMEM, SMEM, SMEM, VMEM, VMEM, VMEM],
         out_shape=[
@@ -386,10 +387,10 @@
     lanes = 128
     stat_rows = 256
 
-    def along_row(sent, *operands):
-        return row_step(sent, *operands)
-
-    def row_step(sent, kv_here, q_send, q_here, meta):
+    def along_row(sent, asked, *operands):
+        return row_step(sent, asked, *operands)
+
+    def row_step(sent, asked, kv_here, q_send, q_here, meta):
         parts = 2 if sent > few else 1
         packed = pl.pallas_call(
             pack_kernel,
@@ -401,7 +402,7 @@
         )(meta, kv_here)
         kv_other = lax.ppermute(kv_here, "tm", swap)
         near = [lax.ppermute(packed[0], "space", pair)]
-        q_visit = jnp.stack([lax.ppermute(q_send, "space", pairs) for pairs in vertical])
+        q_visit = jnp.stack([lax.ppermute(q_send[:asked], "space", pairs) for pairs in vertical])
         far_part = lax.ppermute(packed[-1], "space", far)
         if parts == 2:
             near.append(lax.ppermute(packed[1], "space", pair))
@@ -442,9 +443,10 @@
         )(meta, q_here, q_visit, kv_here, kv_other, *near, bias_own, bias_near)
         return o_own, lse_own, o_near, lse_near, o_visit, lse_visit
 
+    ways = [(n, asked) for n in range(least, slots + 1) for asked in ((few, slots) if n == least else (slots,))]
     o_own, lse_own, o_near, lse_near, o_visit, lse_visit = branch_on(
         wide_branch.reshape(()),
-        [functools.partial(along_row, n) for n in range(least, slots + 1)],
+        [functools.partial(along_row, *way) for way in ways],
         kv_here, q_send, q_here, meta,
     )
 

time: 60.1 us -> 60.9 us (1.013)
  transfers between devices with their start and end apart: 8 -> 8, of which waited for: 3 -> 3; matrix products, arithmetic and copies ran while one was open for 0% -> 0% of each run, Pallas kernels for 10% -> 9%
where the time goes in v6:
time: 60.9 us; the launch traced here: 60.6 us
  waiting for transfers between devices  30 us (49%)
  Pallas kernels  18.2 us (30%)
  starting transfers between devices  10.1 us (17%)
  loops' own time  1.98 us (3%)
    ppermute x1, waiting for transfers between devices, row_step(): near = [lax.ppermute(packed[0], 'space', pair)]  15.5 us
    ppermute x1, waiting for transfers between devices, row_step(): lax.ppermute(q_send[:asked], 'space', pairs)  10.6 us
    pallas_call x1, Pallas kernels, per_device(): pl.pallas_call(functools.partial(project_kernel, heads, least, few), in_s...  5.47 us
    pallas_call x1, Pallas kernels, row_step(): pl.pallas_call(functools.partial(attend_kernel, parts), in_specs=[SMEM] +...  4 us
    ppermute x1, waiting for transfers between devices, return_step(): lax.ppermute(lse_visit[d], 'space', back[d])  3.93 us
    pallas_call x1, Pallas kernels, row_step(): pl.pallas_call(functools.partial(own_tile_kernel, heads, tile_cols), in_s...  3.45 us
    pallas_call x1, Pallas kernels, return_step(): pl.pallas_call(functools.partial(output_kernel, tile_cols, tile_rows), in...  3.01 us
    ppermute x1, starting transfers between devices, return_step(): lax.ppermute(lse_visit[d], 'space', back[d])  2.91 us
  transfers between devices with their start and end apart: 8, of which 3 were waited for; matrix products, arithmetic and copies ran while one was open for 0% of the time, Pallas kernels for 9%

profile of v6, /device:TPU:0, one launch (start us, length us, event | category | flops | bytes accessed | tf_op | source)
XLA Modules:
  0.0 60.6 jit_solution(13675622136955053863)
XLA Ops:
  0.0 0.0 copy-start.2
  0.0 0.0 copy-start.3
  0.0 5.5 %project.1 = (s32[40]{0:T(128)S(1)}, s32[1]{0:T(128)}, s32[1]{0:T(128)}, bf16[6,240,128]{2,1,0:T(8,128)(2,1)S(1)}, bf16[5,240,128]{2,1,0:T(8,128)(2,1)S(1)}, /*index=5*/bf16[6,2,240,128]{3,2,1,0:T(8,128)(2,1)S(1)}) custom-call(s32[2,6]{1,0:T(2,128)} %bitcast.52, bf16[60,4,1536]{2,1,0:T(4,128)(2,1)} %bitcast.46, f32[1536]{0:T(1024)} %shift_at.1, ...), custom_call_target="tpu_custom_call" | custom-call | tf_op jit(solution)/shard_map/project/pallas_call | solution.py:355
  5.5 0.0 copy-done.2
  5.5 0.0 copy-done.3
  5.5 0.0 copy-start
  5.5 0.0 copy-start.1
  5.5 42.6 %conditional.2 = (f32[6,240,128]{2,1,0:T(8,128)S(1)}, f32[240,128]{1,0:T(8,128)S(1)}, f32[5,240,128]{2,1,0:T(8,128)S(1)}, f32[240,128]{1,0:T(8,128)S(1)}, bf16[1...) conditional(s32[]{:T(128)} %bitcast.25, ...), branch_computations={%region_0.0_spmd, %region_1.0_spmd, %region_2.0_spmd, %region_3.0_... | conditional | flops 353894400 | bytes 20300224 | solution.py:320
  6.4 0.6 collective-permute-start.12
  6.9 0.6 pack.7
  7.5 2.6 %collective-permute-start.14 = (bf16[3,2,240,128]{3,2,1,0:T(8,128)(2,1)S(1)}, bf16[3,2,240,128]{3,2,1,0:T(8,128)(2,1)S(1)}, u32[]{:S(2)}, u32[]{:S(2)}) collective-permute-start(bf16[3,2,240,128]{3,2,1,0:T(8,128)(2,1)S(1)} %pack.7), channel_id=1, source_target_pairs={{0,2},{2,0},{4,6},{6,4},{8,10},{10,8},{12,14},{14,12},{1,3},{3,1},... | collective-permute-start | bytes 1105928 | tf_op jit(solution)/shard_map/cond/branch_2_fun/ppermute | solution.py:404
  10.0 0.9 %collective-permute-start.16 = (bf16[3,2,240,128]{3,2,1,0:T(8,128)(2,1)S(1)}, bf16[3,2,240,128]{3,2,1,0:T(8,128)(2,1)S(1)}, u32[]{:S(2)}, u32[]{:S(2)}) collective-permute-start(bf16[3,2,240,128]{3,2,1,0:T(8,128)(2,1)S(1)} %pack.7), channel_id=1, source_target_pairs={{2,4},{4,2},{10,12},{12,10},{3,5},{5,3},{11,13},{13,11},{18,20},{2... | collective-permute-start | bytes 1105928 | tf_op jit(solution)/shard_map/cond/branch_2_fun/ppermute | solution.py:406
  11.0 15.5 %collective-permute-done.14.refs_0_ = bf16[3,2,240,128]{3,2,1,0:T(8,128)(2,1)S(1)} collective-permute-done((bf16[3,2,240,128]{3,2,1,0:T(8,128)(2,1)S(1)}, bf16[3,2,240,128]{3,2,1,0:T(8,128)(2,1)S(1)}, u32[]{:S(2)}, u32[]{:S(2)}) %collective-permute-start.14) | collective-permute-done | bytes 368672 | tf_op jit(solution)/shard_map/cond/branch_2_fun/ppermute | solution.py:404
  26.5 0.0 collective-permute-start.15
  26.5 0.0 collective-permute-done.16.refs_2_
  26.5 0.5 collective-permute-start.17
  27.0 2.6 %collective-permute-start.13 = (bf16[5,240,128]{2,1,0:T(8,128)(2,1)S(1)}, bf16[5,240,128]{2,1,0:T(8,128)(2,1)S(1)}, u32[]{:S(2)}, u32[]{:S(2)}) collective-permute-start(bf16[5,240,128]{2,1,0:T(8,128)(2,1)S(1)} %get-tuple-element.185), channel_id=1, source_target_pairs={{0,8},{2,10},{4,12},{6,14},{8,0},{10,2},{12,4},{14,6},{1,9},{3,11}... | collective-permute-start | bytes 921608 | tf_op jit(solution)/shard_map/cond/branch_2_fun/ppermute | solution.py:405
  29.5 0.0 collective-permute-done.12.kv_own2
  29.6 3.5 %own_tile.7 = (f32[6,240,128]{2,1,0:T(8,128)S(1)}, f32[240,128]{1,0:T(8,128)S(1)}, f32[240,480]{1,0:T(8,128)S(1)}, f32[240,960]{1,0:T(8,128)S(1)}) custom-call(s32[8,6]{1,0:T(8,128)S(1)} %get-tuple-element.178.lists, s32[8]{0:T(128)S(1)} %get-tuple-element.179.valid, bf16[6,240,128]{2,1,0:T(8,128)(2,1)S(1)} %get-tuple-element.180.q_here, ...), custom_call_target="tpu_custom_call" | custom-call | flops 353894400 | bytes 6291456 | tf_op jit(solution)/shard_map/cond/branch_2_fun/own_tile/pallas_call | solution.py:414
  33.0 10.6 %collective-permute-done.13 = bf16[5,240,128]{2,1,0:T(8,128)(2,1)S(1)} collective-permute-done((bf16[5,240,128]{2,1,0:T(8,128)(2,1)S(1)}, bf16[5,240,128]{2,1,0:T(8,128)(2,1)S(1)}, u32[]{:S(2)}, u32[]{:S(2)}) %collective-permute-start.13) | collective-permute-done | bytes 307232 | tf_op jit(solution)/shard_map/cond/branch_2_fun/ppermute | solution.py:405
  43.6 0.0 collective-permute-done.15.refs_1_
  43.6 0.0 collective-permute-done.17.refs_3_
  43.6 4.0 %attend.7 = (f32[5,240,128]{2,1,0:T(8,128)S(1)}, f32[240,128]{1,0:T(8,128)S(1)}, bf16[1,5,240,128]{3,2,1,0:T(8,128)(2,1)S(1)}, f32[1,8,256]{2,1,0:T(8,128)S(1)}) custom-call(s32[40]{0:T(128)S(1)} %get-tuple-element.184.meta, bf16[6,240,128]{2,1,0:T(8,128)(2,1)S(1)} %get-tuple-element.180.q_here, bf16[1,5,240,128]{3,2,1,0:T(8,128)(2,1)S(1)} %bitcast.37, ...), custom_call_target="tpu_custom_call" | custom-call | tf_op jit(solution)/shard_map/cond/branch_2_fun/attend/pallas_call | solution.py:430
  48.1 0.0 copy-done
  48.2 0.0 copy-done.1
  48.2 12.3 %conditional.3 = (bf16[60,4,1536]{2,1,0:T(4,128)(2,1)}) conditional(s32[]{:T(128)} %bitcast.24, (s32[40]{0:T(128)S(1)}, f32[6,240,128]{2,1,0:T(8,128)S(1)}, f32[240,128]{1,0:T(8,128)S(1)}, f32[5,240,128]{2,1,0:T(8,128)S(1)}, f32[240,128]{1,0:T(8,128)S(1)}, /*index=5*/bf16[1,5,240,128]{3,2,1,0:T(8,128)(2,1)S(1)}, ...), branch_computations={%region_5.0_spmd, %region_6.0_spmd, %region_7.0_spmd, %region_8.0_... | conditional | flops 4194304 | bytes 3604568 | solution.py:320
  48.8 0.1 collective-permute-start.40
  48.8 2.9 %collective-permute-start.41 = (f32[8,256]{1,0:T(8,128)S(1)}, f32[8,256]{1,0:T(8,128)S(1)}, u32[]{:S(2)}, u32[]{:S(2)}) collective-permute-start(f32[8,256]{1,0:T(8,128)S(1)} %bitcast.53), channel_id=1, source_target_pairs={{8,0},{10,2},{12,4},{14,6},{0,8},{2,10},{4,12},{6,14},{9,1},{11,3}... | collective-permute-start | bytes 24584 | tf_op jit(solution)/shard_map/cond/branch_0_fun/ppermute | solution.py:458
  51.8 1.7 %row_merge.4 = (f32[6,240,128]{2,1,0:T(8,128)S(1)}, f32[240,128]{1,0:T(8,128)S(1)}, bf16[240,768]{1,0:T(8,128)(2,1)S(1)}) custom-call(s32[40]{0:T(128)S(1)} %get-tuple-element.224.meta, f32[6,240,128]{2,1,0:T(8,128)S(1)} %get-tuple-element.228.o_own, f32[240,128]{1,0:T(8,128)S(1)} %get-tuple-element.229.lse_own, ...), custom_call_target="tpu_custom_call" | custom-call | flops 4194304 | bytes 2097152 | tf_op jit(solution)/shard_map/cond/branch_0_fun/row_merge/pallas_call | solution.py:459
  53.5 3.9 %collective-permute-done.41 = f32[8,256]{1,0:T(8,128)S(1)} collective-permute-done((f32[8,256]{1,0:T(8,128)S(1)}, f32[8,256]{1,0:T(8,128)S(1)}, u32[]{:S(2)}, u32[]{:S(2)}) %collective-permute-start.41) | collective-permute-done | bytes 8224 | tf_op jit(solution)/shard_map/cond/branch_0_fun/ppermute | solution.py:458
  57.4 0.0 collective-permute-done.40
  57.4 3.0 %output.4 = bf16[60,4,1536]{2,1,0:T(4,128)(2,1)} custom-call(s32[40]{0:T(128)S(1)} %get-tuple-element.224.meta, bf16[60,4,1536]{2,1,0:T(4,128)(2,1)} %get-tuple-element.225.tokens, f32[1536]{0:T(1024)S(1)} %get-tuple-element.226.gate, bf16[768,1536]{1,0:T(8,128)(2,1)S(1)} %get-tuple-element.227.w_out, f32[6,240,128]{2,1,0:T(8,128)S(1)} %get-tuple-element.232.o_row, ...), custom_call_target="tpu_custom_call" | custom-call | tf_op jit(solution)/shard_map/cond/branch_0_fun/output/pallas_call | solution.py:472
  (1 shorter events, 0.0 us)
Async XLA Ops:
  0.0 5.5 %copy-start.2 = (s32[8,6]{1,0:T(8,128)S(1)}, s32[8,6]{1,0:T(8,128)}, u32[]{:S(2)}) copy-start(s32[8,6]{1,0:T(8,128)} %param.29) | copy-start | bytes 580
  0.0 5.5 %copy-start.3 = (s32[8]{0:T(128)S(1)}, s32[8]{0:T(128)}, u32[]{:S(2)}) copy-start(s32[8]{0:T(128)} %param.30) | copy-start | bytes 100
  5.5 42.6 %copy-start = (bf16[768,1536]{1,0:T(8,128)(2,1)S(1)}, bf16[768,1536]{1,0:T(8,128)(2,1)}, u32[]{:S(2)}) copy-start(bf16[768,1536]{1,0:T(8,128)(2,1)} %param.27) | copy-start | bytes 7077892
  5.5 42.6 %copy-start.1 = (f32[1536]{0:T(1024)S(1)}, f32[1536]{0:T(1024)}, u32[]{:S(2)}) copy-start(f32[1536]{0:T(1024)} %param.23) | copy-start | bytes 18436
  6.4 23.2 %collective-permute-start.12 = (bf16[6,2,240,128]{3,2,1,0:T(8,128)(2,1)S(1)}, bf16[6,2,240,128]{3,2,1,0:T(8,128)(2,1)S(1)}, u32[]{:S(2)}, u32[]{:S(2)}) collective-permute-start(bf16[6,2,240,128]{3,2,1,0:T(8,128)(2,1)S(1)} %get-tuple-element.181.kv_own.kv_here), channel_id=1, source_target_pairs={{0,1},{1,0},{2,3},{3,2},{4,5},{5,4},{6,7},{7,6},{8,9},{9,8},{10,11... | collective-permute-start | bytes 2211848 | tf_op jit(solution)/shard_map/cond/branch_2_fun/ppermute | solution.py:403
  7.5 19.0 %collective-permute-start.14 = (bf16[3,2,240,128]{3,2,1,0:T(8,128)(2,1)S(1)}, bf16[3,2,240,128]{3,2,1,0:T(8,128)(2,1)S(1)}, u32[]{:S(2)}, u32[]{:S(2)}) collective-permute-start(bf16[3,2,240,128]{3,2,1,0:T(8,128)(2,1)S(1)} %pack.7), channel_id=1, source_target_pairs={{0,2},{2,0},{4,6},{6,4},{8,10},{10,8},{12,14},{14,12},{1,3},{3,1},... | collective-permute-start | bytes 1105928 | tf_op jit(solution)/shard_map/cond/branch_2_fun/ppermute | solution.py:404
  10.0 16.4 %collective-permute-start.16 = (bf16[3,2,240,128]{3,2,1,0:T(8,128)(2,1)S(1)}, bf16[3,2,240,128]{3,2,1,0:T(8,128)(2,1)S(1)}, u32[]{:S(2)}, u32[]{:S(2)}) collective-permute-start(bf16[3,2,240,128]{3,2,1,0:T(8,128)(2,1)S(1)} %pack.7), channel_id=1, source_target_pairs={{2,4},{4,2},{10,12},{12,10},{3,5},{5,3},{11,13},{13,11},{18,20},{2... | collective-permute-start | bytes 1105928 | tf_op jit(solution)/shard_map/cond/branch_2_fun/ppermute | solution.py:406
  26.5 17.2 %collective-permute-start.15 = (bf16[3,2,240,128]{3,2,1,0:T(8,128)(2,1)S(1)}, bf16[3,2,240,128]{3,2,1,0:T(8,128)(2,1)S(1)}, u32[]{:S(2)}, u32[]{:S(2)}) collective-permute-start(bf16[3,2,240,128]{3,2,1,0:T(8,128)(2,1)S(1)} %collective-permute-done.14.refs_0_), channel_id=1, source_target_pairs={{0,1},{1,0},{2,3},{3,2},{4,5},{5,4},{6,7},{7,6},{8,9},{9,8},{10,11... | collective-permute-start | bytes 1105928 | tf_op jit(solution)/shard_map/cond/branch_2_fun/ppermute | solution.py:411
  26.5 17.2 %collective-permute-start.17 = (bf16[3,2,240,128]{3,2,1,0:T(8,128)(2,1)S(1)}, bf16[3,2,240,128]{3,2,1,0:T(8,128)(2,1)S(1)}, u32[]{:S(2)}, u32[]{:S(2)}) collective-permute-start(bf16[3,2,240,128]{3,2,1,0:T(8,128)(2,1)S(1)} %collective-permute-done.16.refs_2_), channel_id=1, source_target_pairs={{0,1},{1,0},{2,3},{3,2},{4,5},{5,4},{6,7},{7,6},{8,9},{9,8},{10,11... | collective-permute-start | bytes 1105928 | tf_op jit(solution)/shard_map/cond/branch_2_fun/ppermute | solution.py:411
  27.0 16.7 %collective-permute-start.13 = (bf16[5,240,128]{2,1,0:T(8,128)(2,1)S(1)}, bf16[5,240,128]{2,1,0:T(8,128)(2,1)S(1)}, u32[]{:S(2)}, u32[]{:S(2)}) collective-permute-start(bf16[5,240,128]{2,1,0:T(8,128)(2,1)S(1)} %get-tuple-element.185), channel_id=1, source_target_pairs={{0,8},{2,10},{4,12},{6,14},{8,0},{10,2},{12,4},{14,6},{1,9},{3,11}... | collective-permute-start | bytes 921608 | tf_op jit(solution)/shard_map/cond/branch_2_fun/ppermute | solution.py:405
  48.8 8.6 %collective-permute-start.40 = (bf16[2,240,128]{2,1,0:T(8,128)(2,1)S(1)}, bf16[2,240,128]{2,1,0:T(8,128)(2,1)S(1)}, u32[]{:S(2)}, u32[]{:S(2)}) collective-permute-start(bf16[2,240,128]{2,1,0:T(8,128)(2,1)S(1)} %slice_bitcast_fusion), channel_id=1, source_target_pairs={{8,0},{10,2},{12,4},{14,6},{0,8},{2,10},{4,12},{6,14},{9,1},{11,3}... | collective-permute-start | bytes 368648 | tf_op jit(solution)/shard_map/cond/branch_0_fun/ppermute | solution.py:457
  48.8 8.6 %collective-permute-start.41 = (f32[8,256]{1,0:T(8,128)S(1)}, f32[8,256]{1,0:T(8,128)S(1)}, u32[]{:S(2)}, u32[]{:S(2)}) collective-permute-start(f32[8,256]{1,0:T(8,128)S(1)} %bitcast.53), channel_id=1, source_target_pairs={{8,0},{10,2},{12,4},{14,6},{0,8},{2,10},{4,12},{6,14},{9,1},{11,3}... | collective-permute-start | bytes 24584 | tf_op jit(solution)/shard_map/cond/branch_0_fun/ppermute | solution.py:458

commit v7 on v6

--- a/solution.py
+++ b/solution.py
@@ -43,7 +43,7 @@
 
 def project_kernel(
     heads, least, few, windows_at, tokens_at, shift_at, scale_at, w_qkv, q_gain_at, k_gain_at,
-    meta, wide_branch, tall_branch, q_here, q_send, kv_here,
+    meta, wide_branch, tall_branch, q_here, q_send, kv_here, kv_send,
     windows, tokens, shift, scale, q_gain, k_gain, modulated, w_buf, small_sems, sems,
 ):
     tile_tokens, frames, _ = tokens.shape
@@ -102,15 +102,10 @@
         kv_here[h, 1] = columns[:, h * HEAD_DIM : (h + 1) * HEAD_DIM].astype(jnp.bfloat16)
     for h, part in normed_heads(block(queries), q_gain):
         q_here[h] = part
+    for i in range(kv_send.shape[0]):
+        kv_send[i] = kv_here[meta[ORDER_H + i]]
     for i in range(q_send.shape[0]):
         q_send[i] = q_here[meta[ORDER_V + i]]
-
-
-def pack_kernel(meta, kv_here, *sends):
-    each = sends[0].shape[1]
-    for j, send in enumerate(sends):
-        for i in range(send.shape[0]):
-            send[i] = kv_here[meta[ORDER_H + i], j * each : (j + 1) * each]
 
 
 def softmax_over(query, parts):
@@ -352,10 +347,10 @@
     swap = [(0, 1), (1, 0)]
 
     least, few = min(2, slots), min(3, slots)
-    meta, wide_branch, tall_branch, q_here, q_send, kv_here = pl.pallas_call(
+    meta, wide_branch, tall_branch, q_here, q_send, kv_here, kv_send = pl.pallas_call(
         functools.partial(project_kernel, heads, least, few),
         in_specs=[HBM] * 7,
-        out_specs=[SMEM, SMEM, SMEM, VMEM, VMEM, VMEM],
+        out_specs=[SMEM] * 3 + [VMEM] * 4,
         out_shape=[
             jax.ShapeDtypeStruct((META,), jnp.int32),
             jax.ShapeDtypeStruct((1,), jnp.int32),
@@ -363,6 +358,7 @@
             jax.ShapeDtypeStruct((heads, rows, HEAD_DIM), bf16),
             jax.ShapeDtypeStruct((slots, rows, HEAD_DIM), bf16),
             jax.ShapeDtypeStruct((heads, 2, rows, HEAD_DIM), bf16),
+            jax.ShapeDtypeStruct((slots, 2, rows, HEAD_DIM), bf16),
         ],
         scratch_shapes=[
             pltpu.SMEM((2, heads), jnp.int32),
@@ -390,16 +386,10 @@
     def along_row(sent, asked, *operands):
         return row_step(sent, asked, *operands)
 
-    def row_step(sent, asked, kv_here, q_send, q_here, meta):
+    def row_step(sent, asked, kv_send, kv_here, q_send, q_here, meta):
         parts = 2 if sent > few else 1
-        packed = pl.pallas_call(
-            pack_kernel,
-            in_specs=[SMEM, VMEM],
-            out_specs=[VMEM] * parts,
-            out_shape=[jax.ShapeDtypeStruct((sent, 2 // parts, rows, HEAD_DIM), bf16)] * parts,
-            compiler_params=params(4),
-            name="pack",
-        )(meta, kv_here)
+        each = 2 // parts
+        packed = [kv_send[:sent, j * each : (j + 1) * each] for j in range(parts)]
         kv_other = lax.ppermute(kv_here, "tm", swap)
         near = [lax.ppermute(packed[0], "space", pair)]
         q_visit = jnp.stack([lax.ppermute(q_send[:asked], "space", pairs) for pairs in vertical])
@@ -447,7 +437,7 @@
     o_own, lse_own, o_near, lse_near, o_visit, lse_visit = branch_on(
         wide_branch.reshape(()),
         [functools.partial(along_row, *way) for way in ways],
-        kv_here, q_send, q_here, meta,
+        kv_send, kv_here, q_send, q_here, meta,
     )
 
     def between_rows(sent, *operands):

time: 60.9 us -> 60.4 us (level)
  no operation moved by 1% of the time
where the time goes in v7:
time: 60.4 us; the launch traced here: 60.1 us
  waiting for transfers between devices  30 us (50%)
  Pallas kernels  17.7 us (29%)
  starting transfers between devices  10.1 us (17%)
  loops' own time  1.97 us (3%)
    ppermute x1, waiting for transfers between devices, row_step(): near = [lax.ppermute(packed[0], 'space', pair)]  15.5 us
    ppermute x1, waiting for transfers between devices, row_step(): lax.ppermute(q_send[:asked], 'space', pairs)  10.6 us
    pallas_call x1, Pallas kernels, per_device(): pl.pallas_call(functools.partial(project_kernel, heads, least, few), in_s...  5.51 us
    pallas_call x1, Pallas kernels, row_step(): pl.pallas_call(functools.partial(attend_kernel, parts), in_specs=[SMEM] +...  4 us
    ppermute x1, waiting for transfers between devices, return_step(): lax.ppermute(lse_visit[d], 'space', back[d])  3.92 us
    pallas_call x1, Pallas kernels, row_step(): pl.pallas_call(functools.partial(own_tile_kernel, heads, tile_cols), in_s...  3.45 us
    pallas_call x1, Pallas kernels, return_step(): pl.pallas_call(functools.partial(output_kernel, tile_cols, tile_rows), in...  3.01 us
    ppermute x1, starting transfers between devices, return_step(): lax.ppermute(lse_visit[d], 'space', back[d])  2.91 us
  transfers between devices with their start and end apart: 8, of which 3 were waited for; matrix products, arithmetic and copies ran while one was open for 0% of the time, Pallas kernels for 9%

profile of v7, /device:TPU:0, one launch (start us, length us, event | category | flops | bytes accessed | tf_op | source)
XLA Modules:
  0.0 60.1 jit_solution(8421820946304293255)
XLA Ops:
  0.0 0.0 copy-start.2
  0.0 0.0 copy-start.3
  0.0 5.5 %project.1 = (s32[40]{0:T(128)S(1)}, s32[1]{0:T(128)}, s32[1]{0:T(128)}, bf16[6,240,128]{2,1,0:T(8,128)(2,1)S(1)}, bf16[5,240,128]{2,1,0:T(8,128)(2,1)S(1)}, /*i...) custom-call(s32[2,6]{1,0:T(2,128)} %bitcast.52, bf16[60,4,1536]{2,1,0:T(4,128)(2,1)} %bitcast.46, ...), custom_call_target="tpu_custom_call" | custom-call | tf_op jit(solution)/shard_map/project/pallas_call | solution.py:350
  5.5 0.0 copy-done.2
  5.5 0.0 copy-done.3
  5.5 0.0 copy-start
  5.6 0.0 copy-start.1
  5.6 42.1 %conditional.2 = (f32[6,240,128]{2,1,0:T(8,128)S(1)}, f32[240,128]{1,0:T(8,128)S(1)}, f32[5,240,128]{2,1,0:T(8,128)S(1)}, f32[240,128]{1,0:T(8,128)S(1)}, bf16[1...) conditional(s32[]{:T(128)} %bitcast.25, ...), branch_computations={%region_0.0_spmd, %region_1.0_spmd, %region_2.0_spmd, %region_3.0_... | conditional | flops 353894400 | bytes 21529024 | solution.py:315
  6.4 0.6 collective-permute-start.12
  7.0 2.6 %collective-permute-start.14 = (bf16[3,2,240,128]{3,2,1,0:T(8,128)(2,1)S(1)}, bf16[3,2,240,128]{3,2,1,0:T(8,128)(2,1)S(1)}, u32[]{:S(2)}, u32[]{:S(2)}) collective-permute-start(bf16[3,2,240,128]{3,2,1,0:T(8,128)(2,1)S(1)} %slice.25), channel_id=1, source_target_pairs={{0,2},{2,0},{4,6},{6,4},{8,10},{10,8},{12,14},{14,12},{1,3},{3,1},... | collective-permute-start | bytes 1105928 | tf_op jit(solution)/shard_map/cond/branch_2_fun/ppermute | solution.py:394
  9.5 0.9 %collective-permute-start.16 = (bf16[3,2,240,128]{3,2,1,0:T(8,128)(2,1)S(1)}, bf16[3,2,240,128]{3,2,1,0:T(8,128)(2,1)S(1)}, u32[]{:S(2)}, u32[]{:S(2)}) collective-permute-start(bf16[3,2,240,128]{3,2,1,0:T(8,128)(2,1)S(1)} %slice.25), channel_id=1, source_target_pairs={{2,4},{4,2},{10,12},{12,10},{3,5},{5,3},{11,13},{13,11},{18,20},{2... | collective-permute-start | bytes 1105928 | tf_op jit(solution)/shard_map/cond/branch_2_fun/ppermute | solution.py:396
  10.5 15.5 %collective-permute-done.14.refs_0_ = bf16[3,2,240,128]{3,2,1,0:T(8,128)(2,1)S(1)} collective-permute-done((bf16[3,2,240,128]{3,2,1,0:T(8,128)(2,1)S(1)}, bf16[3,2,240,128]{3,2,1,0:T(8,128)(2,1)S(1)}, u32[]{:S(2)}, u32[]{:S(2)}) %collective-permute-start.14) | collective-permute-done | bytes 368672 | tf_op jit(solution)/shard_map/cond/branch_2_fun/ppermute | solution.py:394
  25.9 0.0 collective-permute-start.15
  25.9 0.0 collective-permute-done.16.refs_2_
  25.9 0.5 collective-permute-start.17
  26.5 2.6 %collective-permute-start.13 = (bf16[5,240,128]{2,1,0:T(8,128)(2,1)S(1)}, bf16[5,240,128]{2,1,0:T(8,128)(2,1)S(1)}, u32[]{:S(2)}, u32[]{:S(2)}) collective-permute-start(bf16[5,240,128]{2,1,0:T(8,128)(2,1)S(1)} %get-tuple-element.197), channel_id=1, source_target_pairs={{0,8},{2,10},{4,12},{6,14},{8,0},{10,2},{12,4},{14,6},{1,9},{3,11}... | collective-permute-start | bytes 921608 | tf_op jit(solution)/shard_map/cond/branch_2_fun/ppermute | solution.py:395
  29.0 0.0 collective-permute-done.12.kv_own2
  29.0 3.4 %own_tile.7 = (f32[6,240,128]{2,1,0:T(8,128)S(1)}, f32[240,128]{1,0:T(8,128)S(1)}, f32[240,480]{1,0:T(8,128)S(1)}, f32[240,960]{1,0:T(8,128)S(1)}) custom-call(s32[8,6]{1,0:T(8,128)S(1)} %get-tuple-element.190.lists, s32[8]{0:T(128)S(1)} %get-tuple-element.191.valid, bf16[6,240,128]{2,1,0:T(8,128)(2,1)S(1)} %get-tuple-element.192.q_here, ...), custom_call_target="tpu_custom_call" | custom-call | flops 353894400 | bytes 6291456 | tf_op jit(solution)/shard_map/cond/branch_2_fun/own_tile/pallas_call | solution.py:404
  32.5 10.6 %collective-permute-done.13 = bf16[5,240,128]{2,1,0:T(8,128)(2,1)S(1)} collective-permute-done((bf16[5,240,128]{2,1,0:T(8,128)(2,1)S(1)}, bf16[5,240,128]{2,1,0:T(8,128)(2,1)S(1)}, u32[]{:S(2)}, u32[]{:S(2)}) %collective-permute-start.13) | collective-permute-done | bytes 307232 | tf_op jit(solution)/shard_map/cond/branch_2_fun/ppermute | solution.py:395
  43.1 0.0 collective-permute-done.15.refs_1_
  43.1 0.0 collective-permute-done.17.refs_3_
  43.1 4.0 %attend.7 = (f32[5,240,128]{2,1,0:T(8,128)S(1)}, f32[240,128]{1,0:T(8,128)S(1)}, bf16[1,5,240,128]{3,2,1,0:T(8,128)(2,1)S(1)}, f32[1,8,256]{2,1,0:T(8,128)S(1)}) custom-call(s32[40]{0:T(128)S(1)} %get-tuple-element.196.meta, bf16[6,240,128]{2,1,0:T(8,128)(2,1)S(1)} %get-tuple-element.192.q_here, bf16[1,5,240,128]{3,2,1,0:T(8,128)(2,1)S(1)} %bitcast.37, ...), custom_call_target="tpu_custom_call" | custom-call | tf_op jit(solution)/shard_map/cond/branch_2_fun/attend/pallas_call | solution.py:420
  47.6 0.0 copy-done
  47.6 0.0 copy-done.1
  47.7 12.3 %conditional.3 = (bf16[60,4,1536]{2,1,0:T(4,128)(2,1)}) conditional(s32[]{:T(128)} %bitcast.24, (s32[40]{0:T(128)S(1)}, f32[6,240,128]{2,1,0:T(8,128)S(1)}, f32[240,128]{1,0:T(8,128)S(1)}, f32[5,240,128]{2,1,0:T(8,128)S(1)}, f32[240,128]{1,0:T(8,128)S(1)}, /*index=5*/bf16[1,5,240,128]{3,2,1,0:T(8,128)(2,1)S(1)}, ...), branch_computations={%region_5.0_spmd, %region_6.0_spmd, %region_7.0_spmd, %region_8.0_... | conditional | flops 4194304 | bytes 3604568 | solution.py:315
  48.3 0.1 collective-permute-start.20
  48.3 2.9 %collective-permute-start.21 = (f32[8,256]{1,0:T(8,128)S(1)}, f32[8,256]{1,0:T(8,128)S(1)}, u32[]{:S(2)}, u32[]{:S(2)}) collective-permute-start(f32[8,256]{1,0:T(8,128)S(1)} %bitcast.53), channel_id=1, source_target_pairs={{8,0},{10,2},{12,4},{14,6},{0,8},{2,10},{4,12},{6,14},{9,1},{11,3}... | collective-permute-start | bytes 24584 | tf_op jit(solution)/shard_map/cond/branch_0_fun/ppermute | solution.py:448
  51.2 1.7 %row_merge.4 = (f32[6,240,128]{2,1,0:T(8,128)S(1)}, f32[240,128]{1,0:T(8,128)S(1)}, bf16[240,768]{1,0:T(8,128)(2,1)S(1)}) custom-call(s32[40]{0:T(128)S(1)} %get-tuple-element.235.meta, f32[6,240,128]{2,1,0:T(8,128)S(1)} %get-tuple-element.239.o_own, f32[240,128]{1,0:T(8,128)S(1)} %get-tuple-element.240.lse_own, ...), custom_call_target="tpu_custom_call" | custom-call | flops 4194304 | bytes 2097152 | tf_op jit(solution)/shard_map/cond/branch_0_fun/row_merge/pallas_call | solution.py:449
  53.0 3.9 %collective-permute-done.21 = f32[8,256]{1,0:T(8,128)S(1)} collective-permute-done((f32[8,256]{1,0:T(8,128)S(1)}, f32[8,256]{1,0:T(8,128)S(1)}, u32[]{:S(2)}, u32[]{:S(2)}) %collective-permute-start.21) | collective-permute-done | bytes 8224 | tf_op jit(solution)/shard_map/cond/branch_0_fun/ppermute | solution.py:448
  56.9 0.0 collective-permute-done.20
  56.9 3.0 %output.4 = bf16[60,4,1536]{2,1,0:T(4,128)(2,1)} custom-call(s32[40]{0:T(128)S(1)} %get-tuple-element.235.meta, bf16[60,4,1536]{2,1,0:T(4,128)(2,1)} %get-tuple-element.236.tokens, f32[1536]{0:T(1024)S(1)} %get-tuple-element.237.gate, bf16[768,1536]{1,0:T(8,128)(2,1)S(1)} %get-tuple-element.238.w_out, f32[6,240,128]{2,1,0:T(8,128)S(1)} %get-tuple-element.243.o_row, ...), custom_call_target="tpu_custom_call" | custom-call | tf_op jit(solution)/shard_map/cond/branch_0_fun/output/pallas_call | solution.py:462
  (2 shorter events, 0.0 us)
Async XLA Ops:
  0.0 5.5 %copy-start.2 = (s32[8,6]{1,0:T(8,128)S(1)}, s32[8,6]{1,0:T(8,128)}, u32[]{:S(2)}) copy-start(s32[8,6]{1,0:T(8,128)} %param.29) | copy-start | bytes 580
  0.0 5.5 %copy-start.3 = (s32[8]{0:T(128)S(1)}, s32[8]{0:T(128)}, u32[]{:S(2)}) copy-start(s32[8]{0:T(128)} %param.30) | copy-start | bytes 100
  5.5 42.1 %copy-start = (bf16[768,1536]{1,0:T(8,128)(2,1)S(1)}, bf16[768,1536]{1,0:T(8,128)(2,1)}, u32[]{:S(2)}) copy-start(bf16[768,1536]{1,0:T(8,128)(2,1)} %param.27) | copy-start | bytes 7077892
  5.6 42.1 %copy-start.1 = (f32[1536]{0:T(1024)S(1)}, f32[1536]{0:T(1024)}, u32[]{:S(2)}) copy-start(f32[1536]{0:T(1024)} %param.23) | copy-start | bytes 18436
  6.4 22.7 %collective-permute-start.12 = (bf16[6,2,240,128]{3,2,1,0:T(8,128)(2,1)S(1)}, bf16[6,2,240,128]{3,2,1,0:T(8,128)(2,1)S(1)}, u32[]{:S(2)}, u32[]{:S(2)}) collective-permute-start(bf16[6,2,240,128]{3,2,1,0:T(8,128)(2,1)S(1)} %get-tuple-element.193.kv_own), channel_id=1, source_target_pairs={{0,1},{1,0},{2,3},{3,2},{4,5},{5,4},{6,7},{7,6},{8,9},{9,8},{10,11... | collective-permute-start | bytes 2211848 | tf_op jit(solution)/shard_map/cond/branch_2_fun/ppermute | solution.py:393
  7.0 19.0 %collective-permute-start.14 = (bf16[3,2,240,128]{3,2,1,0:T(8,128)(2,1)S(1)}, bf16[3,2,240,128]{3,2,1,0:T(8,128)(2,1)S(1)}, u32[]{:S(2)}, u32[]{:S(2)}) collective-permute-start(bf16[3,2,240,128]{3,2,1,0:T(8,128)(2,1)S(1)} %slice.25), channel_id=1, source_target_pairs={{0,2},{2,0},{4,6},{6,4},{8,10},{10,8},{12,14},{14,12},{1,3},{3,1},... | collective-permute-start | bytes 1105928 | tf_op jit(solution)/shard_map/cond/branch_2_fun/ppermute | solution.py:394
  9.5 16.4 %collective-permute-start.16 = (bf16[3,2,240,128]{3,2,1,0:T(8,128)(2,1)S(1)}, bf16[3,2,240,128]{3,2,1,0:T(8,128)(2,1)S(1)}, u32[]{:S(2)}, u32[]{:S(2)}) collective-permute-start(bf16[3,2,240,128]{3,2,1,0:T(8,128)(2,1)S(1)} %slice.25), channel_id=1, source_target_pairs={{2,4},{4,2},{10,12},{12,10},{3,5},{5,3},{11,13},{13,11},{18,20},{2... | collective-permute-start | bytes 1105928 | tf_op jit(solution)/shard_map/cond/branch_2_fun/ppermute | solution.py:396
  25.9 17.2 %collective-permute-start.15 = (bf16[3,2,240,128]{3,2,1,0:T(8,128)(2,1)S(1)}, bf16[3,2,240,128]{3,2,1,0:T(8,128)(2,1)S(1)}, u32[]{:S(2)}, u32[]{:S(2)}) collective-permute-start(bf16[3,2,240,128]{3,2,1,0:T(8,128)(2,1)S(1)} %collective-permute-done.14.refs_0_), channel_id=1, source_target_pairs={{0,1},{1,0},{2,3},{3,2},{4,5},{5,4},{6,7},{7,6},{8,9},{9,8},{10,11... | collective-permute-start | bytes 1105928 | tf_op jit(solution)/shard_map/cond/branch_2_fun/ppermute | solution.py:401
  25.9 17.2 %collective-permute-start.17 = (bf16[3,2,240,128]{3,2,1,0:T(8,128)(2,1)S(1)}, bf16[3,2,240,128]{3,2,1,0:T(8,128)(2,1)S(1)}, u32[]{:S(2)}, u32[]{:S(2)}) collective-permute-start(bf16[3,2,240,128]{3,2,1,0:T(8,128)(2,1)S(1)} %collective-permute-done.16.refs_2_), channel_id=1, source_target_pairs={{0,1},{1,0},{2,3},{3,2},{4,5},{5,4},{6,7},{7,6},{8,9},{9,8},{10,11... | collective-permute-start | bytes 1105928 | tf_op jit(solution)/shard_map/cond/branch_2_fun/ppermute | solution.py:401
  26.5 16.7 %collective-permute-start.13 = (bf16[5,240,128]{2,1,0:T(8,128)(2,1)S(1)}, bf16[5,240,128]{2,1,0:T(8,128)(2,1)S(1)}, u32[]{:S(2)}, u32[]{:S(2)}) collective-permute-start(bf16[5,240,128]{2,1,0:T(8,128)(2,1)S(1)} %get-tuple-element.197), channel_id=1, source_target_pairs={{0,8},{2,10},{4,12},{6,14},{8,0},{10,2},{12,4},{14,6},{1,9},{3,11}... | collective-permute-start | bytes 921608 | tf_op jit(solution)/shard_map/cond/branch_2_fun/ppermute | solution.py:395
  48.3 8.6 %collective-permute-start.20 = (bf16[2,240,128]{2,1,0:T(8,128)(2,1)S(1)}, bf16[2,240,128]{2,1,0:T(8,128)(2,1)S(1)}, u32[]{:S(2)}, u32[]{:S(2)}) collective-permute-start(bf16[2,240,128]{2,1,0:T(8,128)(2,1)S(1)} %slice_bitcast_fusion), channel_id=1, source_target_pairs={{8,0},{10,2},{12,4},{14,6},{0,8},{2,10},{4,12},{6,14},{9,1},{11,3}... | collective-permute-start | bytes 368648 | tf_op jit(solution)/shard_map/cond/branch_0_fun/ppermute | solution.py:447
  48.3 8.6 %collective-permute-start.21 = (f32[8,256]{1,0:T(8,128)S(1)}, f32[8,256]{1,0:T(8,128)S(1)}, u32[]{:S(2)}, u32[]{:S(2)}) collective-permute-start(f32[8,256]{1,0:T(8,128)S(1)} %bitcast.53), channel_id=1, source_target_pairs={{8,0},{10,2},{12,4},{14,6},{0,8},{2,10},{4,12},{6,14},{9,1},{11,3}... | collective-permute-start | bytes 24584 | tf_op jit(solution)/shard_map/cond/branch_0_fun/ppermute | solution.py:448
